TPU v7x, 32 devices: a whole 2x2x4 slice. The times are simulated.
32 devices in a mesh: replica: 4 (over y, x), fsdp: 8 (over z, core).
Axes of the slice: x: 2, y: 2, z: 4, core: 2. Of those that a mesh axis runs over, the one named last changes fastest.
Arguments:
- hidden_in: bfloat16 [8192, 1024], P(('replica', 'fsdp')), may hold values from -8 to 8
- seq_lengths: int32 [32, 4], P(('replica', 'fsdp')), may hold values from 0 to 256, as said below
- routes: int32 [8192, 8], P(('replica', 'fsdp')), may hold values from 0 to 15, all different within a row; in each aligned block of 256 rows (0 to 255, 256 to 511, ...) at most 144 rows name the same one
- norm1_gain: bfloat16 [1024], P('fsdp'), may hold values from 0.25 to 1.75
- w_query: bfloat16 [1024, 1024], P('fsdp'), may hold values from -1 to 1
- w_key: bfloat16 [1024, 512], P('fsdp'), may hold values from -1 to 1
- w_value: bfloat16 [1024, 512], P('fsdp'), may hold values from -0.1875 to 0.1875
- w_output: bfloat16 [1024, 1024], P('fsdp'), may hold values from -6 to 6
- norm2_gain: bfloat16 [1024], P('fsdp'), may hold values from 0.25 to 1.75
- w_router: bfloat16 [1024, 16], P('fsdp'), may hold values from -3 to 3
- expert_weights: bfloat16 [16, 1536, 1024], P('fsdp'), may hold values from -3 to 3
- out_cotangent: bfloat16 [8192, 1024], P(('replica', 'fsdp')), may hold values from -6 to 6
Outputs:
- layer_out: bfloat16 [8192, 1024], P(('replica', 'fsdp'))
- grad_in: float32 [8192, 1024], P(('replica', 'fsdp'))
- grad_norm1: float32 [1024], P('fsdp')
- grad_query: float32 [1024, 1024], P('fsdp')
- grad_key: float32 [1024, 512], P('fsdp')
- grad_value: float32 [1024, 512], P('fsdp')
- grad_output: float32 [1024, 1024], P('fsdp')
- grad_norm2: float32 [1024], P('fsdp')
- grad_router: float32 [1024, 16], P('fsdp')
- grad_experts: float32 [16, 1536, 1024], P('fsdp')
Inputs may be any that keep to these rules, and one draw needn't show every extreme that they name: `seq_lengths`: each row sums to 256; a length may be 0; some row holds one sequence of 256. `routes`: A token's experts differ; among the rows of one device no expert is named more than 144 times, a bound that some block reaches.
All inputs are finite; a program needn't handle non-finite values.
Results may differ from a plain program's by a relative error of at most 0.015.
The roundings to bfloat16 on the way count: a program that leaves them out, or rounds other values in their place, can miss the bound.
Values may be sent and summed in bfloat16 or wider, within the bound.
A program may use at most 384 MiB of HBM per device.

v0:
```python
import jax
import jax.numpy as jnp
from jax import lax
from jax.sharding import PartitionSpec as P

D = 1024
H = 16
KVH = 8
HD = 64
FF = 512
TOPK = 8
E = 16
CAP = 144


norm_eps = 1e-06
score_scale = 0.015625
residual_scale = 0.22
rope_base = 10000.0
masked_score = -1e30


def inverse_rms(vector):
    return lax.rsqrt(jnp.mean(vector * vector, axis=-1, keepdims=True) + norm_eps)


def rms_back(vector, factor, gain_full, incoming):
    scaled = incoming * gain_full
    grad_gain = jnp.sum(incoming * vector * factor, axis=0)
    grad_vector = factor * scaled - vector * factor**3 * jnp.mean(
        scaled * vector, axis=-1, keepdims=True
    )
    return (grad_vector, grad_gain)


def rotate(vector, cosines, sine_table):
    half_size = vector.shape[-1] // 2
    turned = jnp.concatenate([-vector[..., half_size:], vector[..., :half_size]], axis=-1)
    return vector * cosines[:, None, :] + turned * sine_table[:, None, :]


def expert_forward(slot_inputs, weight_rows):
    gate_pre = jnp.einsum(
        "ecd,efd->ecf", slot_inputs, weight_rows[:, :FF], preferred_element_type=jnp.float32
    )
    up_pre = jnp.einsum(
        "ecd,efd->ecf", slot_inputs, weight_rows[:, FF : 2 * FF], preferred_element_type=jnp.float32
    )
    hidden_act = (jax.nn.silu(gate_pre) * up_pre).astype(jnp.bfloat16)
    produced = jnp.einsum(
        "ecf,efd->ecd", hidden_act, weight_rows[:, 2 * FF :], preferred_element_type=jnp.float32
    )
    return (produced.astype(jnp.bfloat16), gate_pre, up_pre)


def expert_backward(slot_grads, gate_pre, up_pre, weight_rows):
    sigmoid_gate = jax.nn.sigmoid(gate_pre)
    grad_act = jnp.einsum(
        "ecd,efd->ecf", slot_grads, weight_rows[:, 2 * FF :], preferred_element_type=jnp.float32
    )
    grad_gate = (
        grad_act * up_pre * (sigmoid_gate * (1.0 + gate_pre * (1.0 - sigmoid_gate)))
    ).astype(jnp.bfloat16)
    grad_up = (grad_act * jax.nn.silu(gate_pre)).astype(jnp.bfloat16)
    grad_rows = jnp.einsum(
        "ecf,efd->ecd", grad_gate, weight_rows[:, :FF], preferred_element_type=jnp.float32
    )
    grad_rows = grad_rows + jnp.einsum(
        "ecf,efd->ecd", grad_up, weight_rows[:, FF : 2 * FF], preferred_element_type=jnp.float32
    )
    return (grad_gate, grad_up, grad_rows.astype(jnp.bfloat16))


def expert_grads(slot_inputs, slot_grads, gate_pre, up_pre, grad_gate, grad_up):
    hidden_act = (jax.nn.silu(gate_pre) * up_pre).astype(jnp.bfloat16)
    return jnp.concatenate(
        [
            jnp.einsum("ecf,ecd->efd", grad_gate, slot_inputs, preferred_element_type=jnp.float32),
            jnp.einsum("ecf,ecd->efd", grad_up, slot_inputs, preferred_element_type=jnp.float32),
            jnp.einsum("ecf,ecd->efd", hidden_act, slot_grads, preferred_element_type=jnp.float32),
        ],
        axis=1,
    )


def body(
    hidden_in,
    seq_lengths,
    routes,
    norm1_gain,
    w_query,
    w_key,
    w_value,
    w_output,
    norm2_gain,
    w_router,
    expert_weights,
    out_cotangent,
):
    gain_one, query_w, key_w, value_w, output_w, gain_two, router_w = (
        lax.all_gather(norm1_gain, "fsdp", axis=0, tiled=True),
        lax.all_gather(w_query, "fsdp", axis=0, tiled=True),
        lax.all_gather(w_key, "fsdp", axis=0, tiled=True),
        lax.all_gather(w_value, "fsdp", axis=0, tiled=True),
        lax.all_gather(w_output, "fsdp", axis=0, tiled=True),
        lax.all_gather(norm2_gain, "fsdp", axis=0, tiled=True),
        lax.all_gather(w_router, "fsdp", axis=0, tiled=True),
    )
    tokens = hidden_in.shape[0]
    group = H // KVH
    block_rows = min(512, tokens)
    token_index = jnp.arange(tokens, dtype=jnp.int32)
    seq_ends = jnp.cumsum(seq_lengths[0])
    passed = token_index[:, None] >= seq_ends[None, :]
    segment = jnp.sum(passed.astype(jnp.int32), axis=1)
    position = token_index - jnp.max(jnp.where(passed, seq_ends[None, :], 0), axis=1)
    frequency = rope_base ** (-jnp.arange(0, HD, 2, dtype=jnp.float32) / HD)
    angles = position.astype(jnp.float32)[:, None] * frequency[None, :]
    angles = jnp.concatenate([angles, angles], axis=1)
    cosines = jnp.cos(angles)
    sine_table = jnp.sin(angles)
    allowed = (segment[:, None] == segment[None, :]) & (
        token_index[None, :] <= token_index[:, None]
    )
    source = hidden_in.astype(jnp.float32)
    factor_one = inverse_rms(source)
    gain_first = gain_one.astype(jnp.float32)
    normed = (source * factor_one * gain_first).astype(jnp.bfloat16)
    query_rot = rotate(
        jnp.dot(normed, query_w, preferred_element_type=jnp.float32).reshape(tokens, H, HD),
        cosines,
        sine_table,
    )
    query_rot = query_rot.astype(jnp.bfloat16).reshape(tokens, KVH, group, HD)
    key_rot = rotate(
        jnp.dot(normed, key_w, preferred_element_type=jnp.float32).reshape(tokens, KVH, HD),
        cosines,
        sine_table,
    )
    key_rot = key_rot.astype(jnp.bfloat16)
    value_rows = (
        jnp.dot(normed, value_w, preferred_element_type=jnp.float32)
        .astype(jnp.bfloat16)
        .reshape(tokens, KVH, HD)
    )

    def block_scores():
        raw_scores = (
            jnp.einsum("qkgd,tkd->kgqt", query_rot, key_rot, preferred_element_type=jnp.float32)
            * score_scale
        )
        return jnp.where(allowed[None, None], raw_scores, masked_score)

    scores = block_scores()
    row_max = jnp.max(scores, axis=-1, keepdims=True)
    shifted = jnp.exp(scores - row_max)
    row_total = jnp.sum(shifted, axis=-1, keepdims=True)
    weights = (shifted / row_total).astype(jnp.bfloat16)
    mixed_parts = jnp.einsum(
        "kgqt,tkd->qkgd", weights, value_rows, preferred_element_type=jnp.float32
    )
    log_totals = [row_max + jnp.log(row_total)]
    mixed = mixed_parts.reshape(tokens, H * HD).astype(jnp.bfloat16)
    after = source + residual_scale * jnp.dot(mixed, output_w, preferred_element_type=jnp.float32)
    factor_two = inverse_rms(after)
    gain_second = gain_two.astype(jnp.float32)
    normed_two = (after * factor_two * gain_second).astype(jnp.bfloat16)
    logits = jnp.dot(normed_two, router_w, preferred_element_type=jnp.float32)
    route_hits = (routes[:, :, None] == jnp.arange(E, dtype=jnp.int32)[None, None, :]).astype(
        jnp.float32
    )
    chosen = jnp.sum(route_hits * logits[:, None, :], axis=2)
    gate_probs = jax.nn.softmax(chosen, axis=1)
    flat_routes = routes.reshape(-1)
    flat_hits = (flat_routes[:, None] == jnp.arange(E, dtype=jnp.int32)[None, :]).astype(jnp.int32)
    slot_rank = jnp.sum((jnp.cumsum(flat_hits, axis=0) - flat_hits) * flat_hits, axis=1)
    slot_ids = flat_routes * CAP + slot_rank
    numbered = jnp.arange(tokens * TOPK, dtype=jnp.int32) + 1
    slot_owner = jnp.zeros((E * CAP,), jnp.int32).at[slot_ids].set(numbered) - 1
    filled = slot_owner >= 0
    owner_rows = jnp.maximum(slot_owner, 0)
    zero_half = jnp.zeros((), jnp.bfloat16)
    slot_inputs = jnp.where(filled[:, None], normed_two[owner_rows // TOPK], zero_half).reshape(
        E, CAP, D
    )
    produced, gate_pre, up_pre = expert_forward(
        slot_inputs, lax.all_gather(expert_weights, "fsdp", axis=0, tiled=True)
    )
    picked = produced.reshape(E * CAP, D)[slot_ids].reshape(tokens, TOPK, D)
    mixture = jnp.einsum("tk,tkd->td", gate_probs, picked, preferred_element_type=jnp.float32)
    layer_out = (after + residual_scale * mixture).astype(jnp.bfloat16)
    grad_out = out_cotangent.astype(jnp.float32)
    grad_moe = residual_scale * grad_out
    grad_gates = jnp.einsum("td,tkd->tk", grad_moe, picked, preferred_element_type=jnp.float32)
    grad_chosen = gate_probs * (
        grad_gates - jnp.sum(gate_probs * grad_gates, axis=1, keepdims=True)
    )
    grad_logits = jnp.sum(route_hits * grad_chosen[:, :, None], axis=1).astype(jnp.bfloat16)
    grad_router = jnp.einsum(
        "td,te->de", normed_two, grad_logits, preferred_element_type=jnp.float32
    )
    grad_picked = (
        (gate_probs[:, :, None] * grad_moe[:, None, :])
        .astype(jnp.bfloat16)
        .reshape(tokens * TOPK, D)
    )
    slot_grads = jnp.where(filled[:, None], grad_picked[owner_rows], zero_half).reshape(E, CAP, D)
    grad_gate, grad_up, grad_rows = expert_backward(
        slot_grads, gate_pre, up_pre, lax.all_gather(expert_weights, "fsdp", axis=0, tiled=True)
    )
    grad_expert_shard = lax.psum_scatter(
        expert_grads(slot_inputs, slot_grads, gate_pre, up_pre, grad_gate, grad_up),
        "fsdp",
        scatter_dimension=0,
        tiled=True,
    )
    returned = grad_rows.reshape(E * CAP, D)[slot_ids].reshape(tokens, TOPK, D)
    grad_normed_two = jnp.einsum(
        "te,de->td", grad_logits, router_w, preferred_element_type=jnp.float32
    )
    grad_normed_two = grad_normed_two + jnp.sum(returned, axis=1, dtype=jnp.float32)
    grad_after_norm, grad_gain_two = rms_back(after, factor_two, gain_second, grad_normed_two)
    grad_after = grad_out + grad_after_norm
    grad_branch = (residual_scale * grad_after).astype(jnp.bfloat16)
    grad_output_w = jnp.einsum("tc,td->cd", mixed, grad_branch, preferred_element_type=jnp.float32)
    grad_mixed = jnp.einsum("td,cd->tc", grad_branch, output_w, preferred_element_type=jnp.float32)
    grad_mixed = grad_mixed.astype(jnp.bfloat16).reshape(tokens, KVH, group, HD)
    query_parts = []
    grad_key_rot = jnp.zeros((tokens, KVH, HD), jnp.float32)
    grad_value_rows = jnp.zeros((tokens, KVH, HD), jnp.float32)
    for number, offset in enumerate(range(0, tokens, block_rows)):
        scores = block_scores()
        weights_full = jnp.exp(scores - log_totals[number])
        grad_weights = jnp.einsum(
            "qkgd,tkd->kgqt", grad_mixed, value_rows, preferred_element_type=jnp.float32
        )
        grad_scores = weights_full * (
            grad_weights - jnp.sum(weights_full * grad_weights, axis=-1, keepdims=True)
        )
        grad_scores = grad_scores.astype(jnp.bfloat16)
        query_parts.append(
            jnp.einsum("kgqt,tkd->qkgd", grad_scores, key_rot, preferred_element_type=jnp.float32)
            * score_scale
        )
        grad_key_rot = (
            jnp.einsum("kgqt,qkgd->tkd", grad_scores, query_rot, preferred_element_type=jnp.float32)
            * score_scale
        )
        grad_value_rows = jnp.einsum(
            "kgqt,qkgd->tkd",
            weights_full.astype(jnp.bfloat16),
            grad_mixed,
            preferred_element_type=jnp.float32,
        )
    grad_query_rows = rotate(query_parts[0].reshape(tokens, H, HD), cosines, -sine_table)
    grad_query_rows = grad_query_rows.astype(jnp.bfloat16).reshape(tokens, H * HD)
    grad_key_rows = (
        rotate(grad_key_rot, cosines, -sine_table).astype(jnp.bfloat16).reshape(tokens, KVH * HD)
    )
    grad_value_flat = grad_value_rows.astype(jnp.bfloat16).reshape(tokens, KVH * HD)
    grad_query_w = jnp.einsum(
        "td,tc->dc", normed, grad_query_rows, preferred_element_type=jnp.float32
    )
    grad_key_w = jnp.einsum("td,tc->dc", normed, grad_key_rows, preferred_element_type=jnp.float32)
    grad_value_w = jnp.einsum(
        "td,tc->dc", normed, grad_value_flat, preferred_element_type=jnp.float32
    )
    grad_normed = jnp.einsum(
        "tc,dc->td", grad_query_rows, query_w, preferred_element_type=jnp.float32
    )
    grad_normed = grad_normed + jnp.einsum(
        "tc,dc->td", grad_key_rows, key_w, preferred_element_type=jnp.float32
    )
    grad_normed = grad_normed + jnp.einsum(
        "tc,dc->td", grad_value_flat, value_w, preferred_element_type=jnp.float32
    )
    grad_input_norm, grad_gain_one = rms_back(source, factor_one, gain_first, grad_normed)
    grad_in = grad_after + grad_input_norm
    (
        shard_gain_one,
        shard_query,
        shard_key,
        shard_value,
        shard_output,
        shard_gain_two,
        shard_router,
    ) = (
        lax.psum_scatter(grad_gain_one, "fsdp", scatter_dimension=0, tiled=True),
        lax.psum_scatter(grad_query_w, "fsdp", scatter_dimension=0, tiled=True),
        lax.psum_scatter(grad_key_w, "fsdp", scatter_dimension=0, tiled=True),
        lax.psum_scatter(grad_value_w, "fsdp", scatter_dimension=0, tiled=True),
        lax.psum_scatter(grad_output_w, "fsdp", scatter_dimension=0, tiled=True),
        lax.psum_scatter(grad_gain_two, "fsdp", scatter_dimension=0, tiled=True),
        lax.psum_scatter(grad_router, "fsdp", scatter_dimension=0, tiled=True),
    )
    summed = lax.psum(
        (
            shard_gain_one,
            shard_query,
            shard_key,
            shard_value,
            shard_output,
            shard_gain_two,
            shard_router,
            grad_expert_shard,
        ),
        "replica",
    )
    return (
        layer_out,
        grad_in,
        summed[0],
        summed[1],
        summed[2],
        summed[3],
        summed[4],
        summed[5],
        summed[6],
        summed[7],
    )


def solution(mesh):
    return jax.shard_map(
        body,
        mesh=mesh,
        in_specs=(
            P(("replica", "fsdp"), None),
            P(("replica", "fsdp"), None),
            P(("replica", "fsdp"), None),
            P("fsdp"),
            P("fsdp", None),
            P("fsdp", None),
            P("fsdp", None),
            P("fsdp", None),
            P("fsdp"),
            P("fsdp", None),
            P("fsdp", None, None),
            P(("replica", "fsdp"), None),
        ),
        out_specs=(
            P(("replica", "fsdp"), None),
            P(("replica", "fsdp"), None),
            P("fsdp"),
            P("fsdp", None),
            P("fsdp", None),
            P("fsdp", None),
            P("fsdp", None),
            P("fsdp"),
            P("fsdp", None),
            P("fsdp", None, None),
        ),
        check_vma=False,
    )
```

profile of v0, /device:TPU:10, one launch (start us, length us, event | category | flops | bytes accessed | tf_op | source)
XLA Modules:
  0.0 2148.2 jit_solution(16897767280440720643)
XLA Ops:
  11.1 9.0 all-gather
  20.1 11.8 all-gather.1
  32.4 4.5 reduce-window.19
  37.7 8.1 scatter_custom_fusion
  45.9 11.3 all_gather.31
  64.1 22.7 %all-gather.12.cloned.1.call-done = bf16[1024,1024]{1,0:T(8,128)(2,1)} async-done(((bf16[128,1024]{1,0:T(8,128)(2,1)}), bf16[1024,1024]{1,0:T(8,128)(2,1)}) %all-gather.12.cloned.1.call-update) | async-done | bytes 2097168 | tf_op jit(solution)/shard_map/all_gather | solution.py:102
  94.2 22.7 %all-gather.14.cloned.1.call-done = bf16[1024,1024]{1,0:T(8,128)(2,1)} async-done(((bf16[128,1024]{1,0:T(8,128)(2,1)}), bf16[1024,1024]{1,0:T(8,128)(2,1)}) %all-gather.14.cloned.1.call-update) | async-done | bytes 2097168 | tf_op jit(solution)/shard_map/all_gather | solution.py:105
  120.5 8.3 gather_fusion
  129.8 412.8 %all-gather.16.cloned.1.call-done = bf16[16,1536,1024]{2,1,0:T(8,128)(2,1)} async-done(((bf16[2,1536,1024]{2,1,0:T(8,128)(2,1)}), bf16[16,1536,1024]{2,1,0:T(8,128)(2,1)}) %all-gather.16.cloned.1.call-update) | async-done | bytes 50331664 | tf_op jit(solution)/shard_map/all_gather | solution.py:187
  542.6 11.5 fusion.10
  554.1 13.0 multiply_convert_fusion.2
  567.1 11.4 fusion.26
  578.5 14.4 gather_fusion.1
  592.9 4.5 fusion.17
  597.9 4.4 fusion.19
  604.8 13.7 gather_fusion.2
  618.5 14.3 multiply_convert_fusion.1
  632.8 12.3 fusion.4
  645.0 12.3 add_convert_fusion
  657.4 13.9 gather_fusion.3
  671.3 5.6 convert_reduce_fusion
  708.8 18.9 fusion.21
  728.0 19.2 fusion.25
  747.2 18.2 fusion.24
  765.4 66.6 %pad_maximum_fusion = f32[16,1536,1024]{2,1,0:T(8,128)} fusion(f32[16,512,1024]{2,1,0:T(8,128)} %fusion.21, f32[16,512,1024]{2,1,0:T(8,128)} %fusion.24, f32[16,512,1024]{2,1,0:T(8,128)} %fusion.25), kind=kLoop, calls=%fused_computation.5 | loop fusion | flops 50331648 | bytes 201326592 | tf_op jit(solution)/shard_map/concatenate | solution.py:76
  834.0 27.2 %reduce-scatter.7.cloned.1.call-done = f32[128,1024]{1,0:T(8,128)} async-done(((f32[1024,1024]{1,0:T(8,128)}), f32[128,1024]{1,0:T(8,128)}) %reduce-scatter.7.cloned.1.call-update) | async-done | bytes 524304 | tf_op jit(solution)/shard_map/reduce_scatter | solution.py:289
  861.2 956.0 %reduce-scatter.17.cloned.1.call-done = f32[2,1536,1024]{2,1,0:T(8,128)} async-done(((f32[16,1536,1024]{2,1,0:T(8,128)}), f32[2,1536,1024]{2,1,0:T(8,128)}) %reduce-scatter.17.cloned.1.call-update) | async-done | bytes 12582928 | tf_op jit(solution)/shard_map/reduce_scatter | solution.py:211
  1825.3 13.2 all-reduce.2
  1840.0 7.8 reduce-scatter.15.cloned.1.call-done
  1847.8 9.0 all-reduce.3
  1856.8 265.0 %all-reduce.7.cloned.1.call-done = (f32[128,1024]{1,0:T(8,128)}, f32[128,512]{1,0:T(8,128)}, f32[128,512]{1,0:T(8,128)}, f32[128,1024]{1,0:T(8,128)}, f32[2,1536,1024]{2,1,0:T(8,128)}) async-done(((f32[128,1024]{1,0:T(8,128)}, f32[128,512]{1,0:T(8,128)}, f32[128,512]{1,0:T(8,128)}, f32[128,1024]{1,0:T(8,128)}, f32[2,1536,1024]{2,1,0:T(8,128)}), (f32[128,1024]{1,0:T(8,128)}, f32[128,512]{1,0:T(8,128)}, ...) | async-done | bytes 14155792 | tf_op jit(solution)/shard_map/psum | solution.py:296
  2128.9 12.1 copy.107
  (237 shorter events, 76.3 us)
Async XLA Ops:
  7.2 12.9 copy-start.56
  7.2 24.9 %copy-start.57 = (s32[1,4]{1,0:T(1,128)S(1)}, s32[1,4]{1,0:T(1,128)}, u32[]{:S(2)}) copy-start(s32[1,4]{1,0:T(1,128)} %param.13) | copy-start | bytes 52
  7.2 38.7 %copy-start.54 = (bf16[128,16]{0,1:T(8,128)(2,1)S(1)}, bf16[128,16]{0,1:T(8,128)(2,1)}, u32[]{:S(2)}) copy-start(bf16[128,16]{0,1:T(8,128)(2,1)} %param.21) | copy-start | bytes 12292
  7.2 51.0 %copy-start.4 = (bf16[256,1024]{1,0:T(8,128)(2,1)S(1)}, bf16[256,1024]{1,0:T(8,128)(2,1)}, u32[]{:S(2)}) copy-start(bf16[256,1024]{1,0:T(8,128)(2,1)} %param.12) | copy-start | bytes 1572868
  7.2 52.9 %all-gather.8.cloned.1.call-start = ((), (), s32[]{:S(2)}) async-start(), calls=%async_computation.6 | async-start | bytes 1179648 | tf_op jit(solution)/shard_map/all_gather | solution.py:104
  8.0 54.1 %all-gather.10.cloned.1.call-start = ((), (), s32[]{:S(2)}) async-start(), calls=%async_computation.7 | async-start | bytes 1179648 | tf_op jit(solution)/shard_map/all_gather | solution.py:103
  8.7 78.1 %all-gather.12.cloned.1.call-start = ((), (), s32[]{:S(2)}) async-start(), calls=%async_computation.8 | async-start | bytes 2359296 | tf_op jit(solution)/shard_map/all_gather | solution.py:102
  9.5 49.6 %copy-start.15 = (bf16[256,1024]{1,0:T(8,128)(2,1)S(1)}, bf16[256,1024]{1,0:T(8,128)(2,1)}, u32[]{:S(2)}) copy-start(bf16[256,1024]{1,0:T(8,128)(2,1)} %param.23) | copy-start | bytes 1572868
  9.5 107.4 %all-gather.14.cloned.1.call-start = ((), (), s32[]{:S(2)}) async-start(), calls=%async_computation.9 | async-start | bytes 2359296 | tf_op jit(solution)/shard_map/all_gather | solution.py:105
  10.0 532.6 %all-gather.16.cloned.1.call-start = ((), (), s32[]{:S(2)}) async-start(), calls=%async_computation.10 | async-start | bytes 56623104 | tf_op jit(solution)/shard_map/all_gather | solution.py:187
  10.6 823.3 %reduce-scatter.11.cloned.1.call-start = ((), (), s32[]{:S(2)}) async-start(), calls=%async_computation.13 | async-start | bytes 2359296 | tf_op jit(solution)/shard_map/reduce_scatter | solution.py:291
  20.1 66.8 %copy-start.38 = (f32[8,1,128]{2,1,0:T(1,128)}, f32[8,1,128]{2,1,0:T(1,128)S(1)}, u32[]{:S(2)}) copy-start(f32[8,1,128]{2,1,0:T(1,128)S(1)} %convert_element_type.151) | copy-start | bytes 12292
  31.9 88.1 %copy-start.44 = (f32[8,1,128]{2,1,0:T(1,128)}, f32[8,1,128]{2,1,0:T(1,128)S(1)}, u32[]{:S(2)}) copy-start(f32[8,1,128]{2,1,0:T(1,128)S(1)} %convert_element_type.152) | copy-start | bytes 12292
  57.2 71.6 %copy-start.34 = (bf16[1024,16]{0,1:T(8,128)(2,1)}, bf16[1024,16]{0,1:T(8,128)(2,1)S(1)}, u32[]{:S(2)}) copy-start(bf16[1024,16]{0,1:T(8,128)(2,1)S(1)} %all_gather.31) | copy-start | bytes 98308
  58.2 31.3 %copy-start.30 = (f32[256,64]{0,1:T(8,128)}, f32[256,64]{0,1:T(8,128)S(1)}, u32[]{:S(2)}) copy-start(f32[256,64]{0,1:T(8,128)S(1)} %get-tuple-element.43) | copy-start | bytes 196612
  59.0 27.9 %copy-start.46 = (f32[256]{0:T(256)}, f32[256]{0:T(256)S(1)}, u32[]{:S(2)}) copy-start(f32[256]{0:T(256)S(1)} %get-tuple-element.47) | copy-start | bytes 3076
  62.0 30.0 %copy-start.29 = (bf16[256,512]{0,1:T(8,128)(2,1)}, bf16[256,512]{0,1:T(8,128)(2,1)S(1)}, u32[]{:S(2)}) copy-start(bf16[256,512]{0,1:T(8,128)(2,1)S(1)} %copy.66) | copy-start | bytes 786436
  64.1 27.2 %copy-start.24 = (bf16[256,8,64,1]{0,2,3,1:T(8,128)(2,1)}, bf16[256,8,64,1]{0,2,3,1:T(8,128)(2,1)S(1)}, u32[]{:S(2)}) copy-start(bf16[256,8,64,1]{0,2,3,1:T(8,128)(2,1)S(1)} %fusion.68) | copy-start | bytes 786436
  94.2 34.6 %copy-start.28 = (bf16[8,64,2,256]{3,1,2,0:T(8,128)(2,1)}, bf16[8,64,2,256]{3,1,2,0:T(8,128)(2,1)S(1)}, u32[]{:S(2)}) copy-start(bf16[8,64,2,256]{3,1,2,0:T(8,128)(2,1)S(1)} %fusion.41) | copy-start | bytes 1572868
  120.0 8.8 copy-start.50
  567.1 11.4 copy-start.14
  578.5 14.4 copy-start.33
  597.7 79.2 %copy-start.42 = (bf16[256,16]{0,1:T(8,128)(2,1)}, bf16[256,16]{0,1:T(8,128)(2,1)S(1)}, u32[]{:S(2)}) copy-start(bf16[256,16]{0,1:T(8,128)(2,1)S(1)} %select_reduce_fusion) | copy-start | bytes 24580
  632.8 12.3 copy-start.7
  688.9 145.1 %reduce-scatter.9.cloned.1.call-start = ((), (), s32[]{:S(2)}) async-start(), calls=%async_computation.12 | async-start | bytes 2359296 | tf_op jit(solution)/shard_map/reduce_scatter | solution.py:290
  698.4 135.6 %reduce-scatter.13.cloned.1.call-start = ((), (), s32[]{:S(2)}) async-start(), calls=%async_computation.14 | async-start | bytes 4718592 | tf_op jit(solution)/shard_map/reduce_scatter | solution.py:292
  702.6 158.6 %reduce-scatter.7.cloned.1.call-start = ((), (), s32[]{:S(2)}) async-start(), calls=%async_computation.11 | async-start | bytes 4718592 | tf_op jit(solution)/shard_map/reduce_scatter | solution.py:289
  727.8 1089.5 %reduce-scatter.17.cloned.1.call-start = ((), (), s32[]{:S(2)}) async-start(), calls=%async_computation.16 | async-start | bytes 113246208 | tf_op jit(solution)/shard_map/reduce_scatter | solution.py:211
  832.0 1015.8 %reduce-scatter.15.cloned.1.call-start = ((), (), s32[]{:S(2)}) async-start(), calls=%async_computation.15 | async-start | bytes 73728 | tf_op jit(solution)/shard_map/reduce_scatter | solution.py:294
  833.9 1287.9 %all-reduce.7.cloned.1.call-start = ((), (), s32[]{:S(2)}) async-start(), calls=%async_computation.17 | async-start | bytes 28311552 | tf_op jit(solution)/shard_map/psum | solution.py:296
  1819.2 19.6 copy-start.10
  1819.2 19.6 copy-start.52
  (39 other events, 149.0 us)
Sparse Core Ops, SparseCore 0:
  9.7 23.4 all-gather.7
  34.8 21.6 all-gather.9
  58.1 28.6 all-gather.11
  88.3 28.5 all-gather.13
  118.4 424.1 all-gather.15
  689.0 33.1 reduce-scatter.10
  724.5 34.4 reduce-scatter.8
  761.3 48.8 reduce-scatter.12
  813.1 48.0 reduce-scatter.6
  863.4 953.7 reduce-scatter.16
  1820.2 27.6 reduce-scatter.14
  1852.0 269.7 all-reduce.6
where the time goes:
time: 2160 us; the launch traced here: 2150 us
  waiting for transfers between devices  1720 us (80%)
  matrix products  180 us (8%)
  local copies, waits for them, and re-layouts  90.1 us (4%)
  other arithmetic  89.2 us (4%)
  blocking collectives  54.3 us (3%)
    reduce_scatter x1, waiting for transfers between devices, body(): lax.psum_scatter(expert_grads(slot_inputs, slot_grads, gate_pre, up_pre,...  956 us
    all_gather x1, waiting for transfers between devices, body(): lax.all_gather(expert_weights, 'fsdp', axis=0, tiled=True)  413 us
    psum x1, waiting for transfers between devices, body(): lax.psum((shard_gain_one, shard_query, shard_key, shard_value, shard_outp...  265 us
    concatenate x1, other arithmetic, expert_grads(): jnp.concatenate([jnp.einsum('ecf,ecd->efd', grad_gate, slot_inputs, prefe...  66.6 us
  transfers between devices with their start and end apart: 12, of which 7 were waited for; matrix products, arithmetic and copies ran while one was open for 9% of the time, Pallas kernels for 0%

commit v1 on v0

v1 whole, which is shorter than its diff:
```python
import jax
import jax.numpy as jnp
import numpy as np
from jax import lax
from jax.experimental import pallas as pl
from jax.experimental.pallas import tpu as pltpu
from jax.sharding import PartitionSpec as P

D = 1024
H = 16
KVH = 8
HD = 64
FF = 512
TOPK = 8
E = 16
CAP = 144
LANE = 128
QKVO = H * HD + 2 * KVH * HD + D

norm_eps = 1e-06
score_scale = 0.015625
residual_scale = 0.22
rope_base = 10000.0
masked_score = -1e30

BF = jnp.bfloat16
F32 = jnp.float32
VMEM_LIMIT = 60 * 2**20


def dot(a, b):
    return lax.dot_general(a, b, (((1,), (0,)), ((), ())), preferred_element_type=F32)


def dot_nt(a, b):
    return lax.dot_general(a, b, (((1,), (1,)), ((), ())), preferred_element_type=F32)


def dot_tn(a, b):
    return lax.dot_general(a, b, (((0,), (0,)), ((), ())), preferred_element_type=F32)


def lanes_of(rows):
    return lax.broadcasted_iota(jnp.int32, (rows, LANE), 1)


def turned(block, lane):
    return jnp.where(lane % HD < HD // 2, pltpu.roll(block, LANE - HD // 2, 1), pltpu.roll(block, HD // 2, 1))


def halves(block, low):
    zero = jnp.zeros_like(block)
    return jnp.concatenate([jnp.where(low, block, zero), jnp.where(low, zero, block)], axis=0)


def attention_forward(
    x_ref, len_ref, routes_ref, cos_ref, sin_ref, w_ref,
    q_ref, kd_ref, vd_ref, p_ref, o_ref, h1_ref, n2_ref, gd_ref, gt_ref,
):
    tokens = x_ref.shape[0]
    lane = lanes_of(tokens)
    low = lane < HD
    small = w_ref[:, QKVO:].astype(F32).T
    gain_one, gain_two = small[E : E + 1], small[E + 1 : E + 2]
    source = x_ref[...].astype(F32)
    factor = lax.rsqrt(jnp.mean(source * source, axis=1, keepdims=True) + norm_eps)
    normed = (source * factor * gain_one).astype(BF)
    cosines, sines = cos_ref[...], sin_ref[...]
    q_all = dot(normed, w_ref[:, : H * HD])
    for g in range(H // 2):
        at = slice(g * LANE, (g + 1) * LANE)
        block = q_all[:, at]
        q_ref[:, at] = (block * cosines + turned(block, lane) * sines).astype(BF)
    kv = dot(normed, w_ref[:, H * HD : H * HD + 2 * KVH * HD])
    for m in range(KVH // 2):
        block = kv[:, m * LANE : (m + 1) * LANE]
        block = block * cosines + turned(block, lane) * sines
        other = pltpu.roll(block, HD, 1)
        kd_ref[:, 2 * m * LANE : (2 * m + 1) * LANE] = jnp.where(low, block, other).astype(BF)
        kd_ref[:, (2 * m + 1) * LANE : (2 * m + 2) * LANE] = jnp.where(low, other, block).astype(BF)
        block = kv[:, KVH * HD + m * LANE : KVH * HD + (m + 1) * LANE]
        other = pltpu.roll(block, HD, 1)
        vd_ref[:, 2 * m * LANE : (2 * m + 1) * LANE] = jnp.where(low, block, other).astype(BF)
        vd_ref[:, (2 * m + 1) * LANE : (2 * m + 2) * LANE] = jnp.where(low, other, block).astype(BF)

    row = lax.broadcasted_iota(jnp.int32, (tokens, tokens), 0)
    column = lax.broadcasted_iota(jnp.int32, (tokens, tokens), 1)
    row_at = lax.broadcasted_iota(jnp.int32, (tokens, 1), 0)
    column_at = lax.broadcasted_iota(jnp.int32, (1, tokens), 1)
    row_segment = jnp.zeros((tokens, 1), jnp.int32)
    column_segment = jnp.zeros((1, tokens), jnp.int32)
    end = jnp.int32(0)
    for j in range(len_ref.shape[1]):
        end = end + len_ref[0, j]
        row_segment += (row_at >= end).astype(jnp.int32)
        column_segment += (column_at >= end).astype(jnp.int32)
    bias = jnp.where((row_segment == column_segment) & (column <= row), 0.0, masked_score)
    bias = jnp.concatenate([bias, bias], axis=0)

    for g in range(KVH):
        at = slice(g * LANE, (g + 1) * LANE)
        queries = halves(q_ref[:, at].astype(F32), low).astype(BF)
        scores = dot_nt(queries, kd_ref[:, at]) * score_scale + bias
        shifted = jnp.exp(scores - jnp.max(scores, axis=1, keepdims=True))
        weights = shifted * (1.0 / jnp.sum(shifted, axis=1, keepdims=True))
        p_ref[g] = weights
        mixed = dot(weights.astype(BF), vd_ref[:, at])
        o_ref[:, at] = jnp.where(low, mixed[:tokens], mixed[tokens:]).astype(BF)

    after = source + residual_scale * dot(o_ref[...], w_ref[:, QKVO - D : QKVO])
    h1_ref[...] = after
    factor = lax.rsqrt(jnp.mean(after * after, axis=1, keepdims=True) + norm_eps)
    normed = (after * factor * gain_two).astype(BF)
    n2_ref[...] = normed
    logits = dot(normed, w_ref[:, QKVO:])
    routed = jnp.zeros((tokens, LANE), jnp.bool_)
    for j in range(TOPK):
        routed |= routes_ref[:, j : j + 1] == lane
    top = jnp.max(jnp.where(routed, logits, masked_score), axis=1, keepdims=True)
    powers = jnp.where(routed, jnp.exp(logits - top), 0.0)
    gates = powers / jnp.sum(powers, axis=1, keepdims=True)
    gates = jnp.where(routed, gates, -1.0)
    gd_ref[...] = gates
    gt_ref[...] = gates.T[:E]


def experts(base_ref, n2_ref, do_ref, gt_ref, w_ref, yp_ref, dx_ref, xs_ref, dye_ref, dgu_ref, hx_ref):
    local = w_ref.shape[0]
    sources = gt_ref.shape[0]
    tokens = gt_ref.shape[2]
    before = lax.broadcasted_iota(jnp.int32, (tokens, tokens), 0) < lax.broadcasted_iota(jnp.int32, (tokens, tokens), 1)
    before = before.astype(F32).astype(BF)
    slot = lax.broadcasted_iota(jnp.int32, (CAP, tokens), 0).astype(F32)
    picks, gates = [], []
    for s in range(sources):
        rows = [gt_ref[s, pl.ds(base_ref[0] + i, 1), :] for i in range(local)]
        mine = jnp.concatenate(rows, axis=0) if local > 1 else rows[0]
        member = (mine >= 0.0).astype(F32)
        rank = dot(member.astype(BF), before)
        rank = jnp.where(mine >= 0.0, rank, -1.0)
        chosen = [slot == rank[i : i + 1] for i in range(local)]
        gates.append([jnp.sum(jnp.where(chosen[i], mine[i : i + 1], 0.0), axis=1, keepdims=True) for i in range(local)])
        picks.append(jnp.concatenate([c.astype(F32).astype(BF) for c in chosen], axis=0))
    dms = []
    for s in range(sources):
        at = slice(s * tokens, (s + 1) * tokens)
        taken = dot(picks[s], n2_ref[at]).astype(BF)
        grads = dot(picks[s], do_ref[at]) * residual_scale
        dms.append(grads)
        for i in range(local):
            rows = slice(i * CAP, (i + 1) * CAP)
            xs_ref[i, s * CAP : (s + 1) * CAP] = taken[rows]
            dye_ref[i, s * CAP : (s + 1) * CAP] = (gates[s][i] * grads[rows]).astype(BF)
    mixed, back, marks = [], [], []
    lane = lanes_of(CAP)
    for i in range(local):
        slots = xs_ref[i]
        gate_pre = dot_nt(slots, w_ref[i, :FF])
        up_pre = dot_nt(slots, w_ref[i, FF : 2 * FF])
        sigmoid = 1.0 / (1.0 + jnp.exp(-gate_pre))
        silu = gate_pre * sigmoid
        act = (silu * up_pre).astype(BF)
        hx_ref[i] = act
        made = dot(act, w_ref[i, 2 * FF :]).astype(BF).astype(F32)
        grad_act = dot_nt(dye_ref[i], w_ref[i, 2 * FF :])
        dgu_ref[i, :, :FF] = (grad_act * up_pre * (sigmoid * (1.0 + gate_pre * (1.0 - sigmoid)))).astype(BF)
        dgu_ref[i, :, FF:] = (grad_act * silu).astype(BF)
        grad_rows = dot(dgu_ref[i, :, :FF], w_ref[i, :FF]) + dot(dgu_ref[i, :, FF:], w_ref[i, FF : 2 * FF])
        back.append(grad_rows.astype(BF))
        for s in range(sources):
            rows = slice(s * CAP, (s + 1) * CAP)
            mixed.append((gates[s][i] * made[rows]).astype(BF))
            grad_gate = jnp.sum(dms[s][i * CAP : (i + 1) * CAP] * made[rows], axis=1, keepdims=True)
            high = grad_gate.astype(BF).astype(F32)
            expert = base_ref[0] + i
            mark = jnp.where(lane == expert, high, jnp.where(lane == expert + E, grad_gate - high, 0.0))
            marks.append(mark.astype(BF))
    for s in range(sources):
        at = slice(s * tokens, (s + 1) * tokens)
        rows = slice(s * CAP, (s + 1) * CAP)
        sent = jnp.concatenate([mixed[i * sources + s] for i in range(local)], axis=0)
        yp_ref[at] = dot_tn(picks[s], sent).astype(BF)
        sent = jnp.concatenate([back[i][rows] for i in range(local)], axis=0)
        dx_ref[at, :D] = dot_tn(picks[s], sent).astype(BF)
        sent = jnp.concatenate([marks[i * sources + s] for i in range(local)], axis=0)
        dx_ref[at, D:] = dot_tn(picks[s], sent).astype(BF)


def expert_weights_back(xs_ref, dye_ref, dgu_ref, hx_ref, out_ref):
    out_ref[0, : 2 * FF] = dot_tn(dgu_ref[0], xs_ref[0]).astype(BF)
    out_ref[0, 2 * FF :] = dot_tn(hx_ref[0], dye_ref[0]).astype(BF)


def attention_backward(
    x_ref, dout_ref, cos_ref, sin_ref, w_ref, q_ref, kd_ref, vd_ref, p_ref, o_ref, h1_ref, n2_ref, gd_ref, dx_ref,
    gin_ref, gw_ref, gs_ref, do_ref, dqkv_ref,
):
    tokens = x_ref.shape[0]
    lane = lanes_of(tokens)
    low = lane < HD
    small = w_ref[:, QKVO:].astype(F32).T
    gain_one, gain_two = small[E : E + 1], small[E + 1 : E + 2]
    after = h1_ref[...]
    factor_two = lax.rsqrt(jnp.mean(after * after, axis=1, keepdims=True) + norm_eps)
    gates = jnp.maximum(gd_ref[...], 0.0)
    tail = dx_ref[:, D:].astype(F32)
    grad_gates = jnp.where(lane < E, tail + pltpu.roll(tail, LANE - E, 1), 0.0)
    chosen = gates * (grad_gates - jnp.sum(gates * grad_gates, axis=1, keepdims=True))
    grad_logits = chosen.astype(BF)
    grad_normed = dx_ref[:, :D].astype(F32) + dot_nt(grad_logits, w_ref[:, QKVO:])
    scaled = grad_normed * gain_two
    grad_after = dout_ref[...].astype(F32) + (
        factor_two * scaled - after * factor_two**3 * jnp.mean(scaled * after, axis=1, keepdims=True)
    )
    grad_gain_two = jnp.sum(grad_normed * after * factor_two, axis=0, keepdims=True)
    grad_branch = (residual_scale * grad_after).astype(BF)
    gw_ref[:, QKVO - D :] = dot_tn(o_ref[...], grad_branch).astype(BF)
    do_ref[...] = dot_nt(grad_branch, w_ref[:, QKVO - D : QKVO]).astype(BF)
    grad_router = dot_tn(n2_ref[...], grad_logits)

    cosines, sines = cos_ref[...], sin_ref[...]
    key_back, value_back = [], []
    for g in range(KVH):
        at = slice(g * LANE, (g + 1) * LANE)
        queries = halves(q_ref[:, at].astype(F32), low).astype(BF)
        outs = halves(do_ref[:, at].astype(F32), low).astype(BF)
        weights = p_ref[g]
        grad_weights = dot_nt(outs, vd_ref[:, at])
        total = jnp.sum(weights * grad_weights, axis=1, keepdims=True)
        grad_scores = (weights * (grad_weights - total)).astype(BF)
        block = dot(grad_scores, kd_ref[:, at])
        block = jnp.where(low, block[:tokens], block[tokens:]) * score_scale
        dqkv_ref[:, at] = (block * cosines - turned(block, lane) * sines).astype(BF)
        block = dot_tn(grad_scores, queries) * score_scale
        key_back.append(block + pltpu.roll(block, HD, 1))
        block = dot_tn(weights.astype(BF), outs)
        value_back.append(block + pltpu.roll(block, HD, 1))
    for m in range(KVH // 2):
        block = jnp.where(low, key_back[2 * m], key_back[2 * m + 1])
        at = slice(H * HD + m * LANE, H * HD + (m + 1) * LANE)
        dqkv_ref[:, at] = (block * cosines - turned(block, lane) * sines).astype(BF)
        at = slice(H * HD + KVH * HD + m * LANE, H * HD + KVH * HD + (m + 1) * LANE)
        dqkv_ref[:, at] = jnp.where(low, value_back[2 * m], value_back[2 * m + 1]).astype(BF)

    source = x_ref[...].astype(F32)
    factor_one = lax.rsqrt(jnp.mean(source * source, axis=1, keepdims=True) + norm_eps)
    normed = (source * factor_one * gain_one).astype(BF)
    gw_ref[:, : QKVO - D] = dot_tn(normed, dqkv_ref[...]).astype(BF)
    grad_normed = dot_nt(dqkv_ref[...], w_ref[:, : QKVO - D])
    scaled = grad_normed * gain_one
    grad_vector = factor_one * scaled - source * factor_one**3 * jnp.mean(scaled * source, axis=1, keepdims=True)
    gin_ref[...] = grad_after + grad_vector
    grad_gain_one = jnp.sum(grad_normed * source * factor_one, axis=0, keepdims=True)
    pad = jnp.zeros((6, D), F32)
    gains = jnp.concatenate([grad_gain_one, grad_gain_two, pad], axis=0).T
    gs_ref[:, :LANE] = grad_router
    gs_ref[:, LANE:] = jnp.concatenate([gains, jnp.zeros((D, LANE - 8), F32)], axis=1)


def call(kernel, out_shape, args, scratch=(), **more):
    smem = [a.dtype == jnp.int32 and a.size <= 16 for a in args]
    return pl.pallas_call(
        kernel,
        out_shape=out_shape,
        in_specs=[pl.BlockSpec(memory_space=pltpu.SMEM if s else pltpu.VMEM) for s in smem],
        out_specs=jax.tree.map(lambda _: pl.BlockSpec(memory_space=pltpu.VMEM), out_shape),
        scratch_shapes=list(scratch),
        compiler_params=pltpu.CompilerParams(vmem_limit_bytes=VMEM_LIMIT),
        **more,
    )(*args)


def shape(dims, dtype):
    return jax.ShapeDtypeStruct(dims, dtype)


def rope_tables(seq_lengths, tokens):
    ends = jnp.sum(jnp.where(np.tri(seq_lengths.shape[1], dtype=bool), seq_lengths[0][None, :], 0), axis=1)
    token = jnp.arange(tokens, dtype=jnp.int32)
    start = jnp.max(jnp.where(token[:, None] >= ends[None, :], ends[None, :], 0), axis=1)
    position = (token - start).astype(F32)
    frequency = rope_base ** (-jnp.arange(0, HD, 2, dtype=F32) / HD)
    frequency = jnp.concatenate([frequency] * (LANE // (HD // 2)))
    sign = jnp.where(jnp.arange(LANE) % HD < HD // 2, -1.0, 1.0)
    angles = position[:, None] * frequency[None, :]
    return jnp.cos(angles), jnp.sin(angles) * sign[None, :]


def make_body(mesh):
    group = mesh.shape["fsdp"]
    local = E // group
    chunk = 2

    def body(
        hidden_in, seq_lengths, routes, norm1_gain, w_query, w_key, w_value, w_output, norm2_gain, w_router,
        expert_weights, out_cotangent,
    ):
        tokens = hidden_in.shape[0]
        rows = w_query.shape[0]
        packed = jnp.concatenate(
            [
                w_query, w_key, w_value, w_output, w_router, norm1_gain[:, None], norm2_gain[:, None],
                jnp.zeros((rows, LANE - E - 2), BF),
            ],
            axis=1,
        )
        weights = lax.all_gather(packed, "fsdp", axis=0, tiled=True)
        dout_all = lax.all_gather(out_cotangent, "fsdp", axis=0, tiled=True)
        cosines, sines = rope_tables(seq_lengths, tokens)
        q, kd, vd, p, o, h1, n2, gd, gt = call(
            attention_forward,
            (
                shape((tokens, D), BF), shape((tokens, D), BF), shape((tokens, D), BF),
                shape((KVH, 2 * tokens, tokens), F32), shape((tokens, D), BF), shape((tokens, D), F32),
                shape((tokens, D), BF), shape((tokens, LANE), F32), shape((E, tokens), F32),
            ),
            (hidden_in, seq_lengths, routes, cosines, sines, weights),
        )
        n2_all = lax.all_gather(n2, "fsdp", axis=0, tiled=True)
        gt_all = lax.all_gather(gt, "fsdp", axis=0, tiled=False)
        base = (lax.axis_index("fsdp") * local).astype(jnp.int32).reshape(1)
        whole = pl.Buffered(1)
        token_block = pl.BlockSpec((chunk * tokens, D), lambda c: (c, 0))
        slot_block = pl.BlockSpec((local, chunk * CAP, D), lambda c: (0, c, 0))
        yp, dxp, xs, dye, dgu, hx = pl.pallas_call(
            experts,
            grid=(group // chunk,),
            in_specs=[
                pl.BlockSpec(memory_space=pltpu.SMEM), token_block, token_block,
                pl.BlockSpec((chunk, E, tokens), lambda c: (c, 0, 0)),
                pl.BlockSpec((local, 3 * FF, D), lambda c: (0, 0, 0), pipeline_mode=whole),
            ],
            out_specs=[
                token_block, pl.BlockSpec((chunk * tokens, D + LANE), lambda c: (c, 0)),
                slot_block, slot_block, slot_block,
                pl.BlockSpec((local, chunk * CAP, FF), lambda c: (0, c, 0)),
            ],
            out_shape=[
                shape((group * tokens, D), BF), shape((group * tokens, D + LANE), BF),
                shape((local, group * CAP, D), BF), shape((local, group * CAP, D), BF),
                shape((local, group * CAP, D), BF), shape((local, group * CAP, FF), BF),
            ],
            compiler_params=pltpu.CompilerParams(vmem_limit_bytes=VMEM_LIMIT),
        )(base, n2_all, dout_all, gt_all, expert_weights)
        dx = lax.psum_scatter(dxp, "fsdp", scatter_dimension=0, tiled=True)
        wide = pl.BlockSpec((1, group * CAP, D), lambda i: (i, 0, 0))
        grad_experts = pl.pallas_call(
            expert_weights_back,
            grid=(local,),
            in_specs=[wide, wide, wide, pl.BlockSpec((1, group * CAP, FF), lambda i: (i, 0, 0))],
            out_specs=pl.BlockSpec((1, 3 * FF, D), lambda i: (i, 0, 0)),
            out_shape=shape((local, 3 * FF, D), BF),
            compiler_params=pltpu.CompilerParams(vmem_limit_bytes=VMEM_LIMIT),
        )(xs, dye, dgu, hx)
        moe = lax.psum_scatter(yp, "fsdp", scatter_dimension=0, tiled=True)
        layer_out = (h1 + residual_scale * moe.astype(F32)).astype(BF)
        grad_experts = lax.psum(grad_experts, "replica")
        grad_in, gw, gs = call(
            attention_backward,
            (shape((tokens, D), F32), shape((D, QKVO), BF), shape((D, 2 * LANE), F32)),
            (hidden_in, out_cotangent, cosines, sines, weights, q, kd, vd, p, o, h1, n2, gd, dx),
            [pltpu.VMEM((tokens, D), BF), pltpu.VMEM((tokens, QKVO - D), BF)],
        )
        gw = lax.psum_scatter(gw, "fsdp", scatter_dimension=0, tiled=True)
        gs = lax.psum_scatter(gs, "fsdp", scatter_dimension=0, tiled=True)
        gw, grad_experts = lax.optimization_barrier((gw, grad_experts))
        gw = lax.psum(gw, "replica").astype(F32)
        gs = lax.psum(gs, "replica")
        grad_experts = grad_experts.astype(F32)
        a, b, c = H * HD, H * HD + KVH * HD, H * HD + 2 * KVH * HD
        return (
            layer_out, grad_in, gs[:, LANE], gw[:, :a], gw[:, a:b], gw[:, b:c], gw[:, c:], gs[:, LANE + 1],
            gs[:, :E], grad_experts,
        )

    return body


def solution(mesh):
    tokens, weights = P(("replica", "fsdp"), None), P("fsdp", None)
    return jax.shard_map(
        make_body(mesh),
        mesh=mesh,
        in_specs=(
            tokens, tokens, tokens, P("fsdp"), weights, weights, weights, weights, P("fsdp"), weights,
            P("fsdp", None, None), tokens,
        ),
        out_specs=(
            tokens, tokens, P("fsdp"), weights, weights, weights, weights, P("fsdp"), weights, P("fsdp", None, None),
        ),
        check_vma=False,
    )
```

time: 2160 us -> 682 us (0.32)
  waiting for transfers between devices: 1720 us -> 548 us
  matrix products: 180 us -> 0 us
  local copies, waits for them, and re-layouts: 90.1 us -> 13 us
  other arithmetic: 89.2 us -> 13.3 us
  Pallas kernels: 0 us -> 74.2 us
  blocking collectives: 54.3 us -> 15.8 us
    reduce_scatter x6 -> x4, waiting for transfers between devices: 991 us -> 187 us  [the longest x1 69.9 us: body(): gw = lax.psum_scatter(gw, 'fsdp', scatter_dimension=0, tiled=True)]
    all_gather x5 -> x3, waiting for transfers between devices: 458 us -> 131 us  [the longest x1 61.4 us: body(): weights = lax.all_gather(packed, 'fsdp', axis=0, tiled=True)]
    dot_general x32 -> x0, matrix products: 180 us -> none  [the longest x1 19.2 us: expert_grads(): jnp.einsum('ecf,ecd->efd', grad_gate, slot_inputs, preferred_element_type...]
    pallas_call x0 -> x4, Pallas kernels: none -> 74.2 us  [the longest x1 33 us: body(): pl.pallas_call(experts, grid=(group // chunk,), in_specs=[pl.BlockSpec(me...]
    concatenate x1 -> x0, other arithmetic: 66.6 us -> none  [expert_grads(): jnp.concatenate([jnp.einsum('ecf,ecd->efd', grad_gate, slot_inputs, prefe...]
    gather x4 -> x0, local copies, waits for them, and re-layouts: 50.3 us -> none  [the longest x1 14.4 us: body(): picked = produced.reshape(E * CAP, D)[slot_ids].reshape(tokens, TOPK, D)]
    psum x1 -> x3, waiting for transfers between devices: 265 us -> 228 us  [the longest x1 143 us: body(): grad_experts = lax.psum(grad_experts, 'replica')]
    unnamed x127 -> x5, local copies, waits for them, and re-layouts: 29 us -> 2.96 us
  transfers between devices with their start and end apart: 12 -> 10, of which waited for: 7 -> 10; matrix products, arithmetic and copies ran while one was open for 9% -> 3% of each run, Pallas kernels for 0% -> 4%
where the time goes in v1:
time: 682 us; the launch traced here: 680 us
  waiting for transfers between devices  548 us (80%)
  Pallas kernels  74.2 us (11%)
  blocking collectives  15.8 us (2%)
  between operations  14.2 us (2%)
  other arithmetic  13.3 us (2%)
  local copies, waits for them, and re-layouts  13 us (2%)
    psum x1, waiting for transfers between devices, body(): grad_experts = lax.psum(grad_experts, 'replica')  143 us
    reduce_scatter x1, waiting for transfers between devices, body(): gw = lax.psum_scatter(gw, 'fsdp', scatter_dimension=0, tiled=True)  69.9 us
    all_gather x1, waiting for transfers between devices, body(): weights = lax.all_gather(packed, 'fsdp', axis=0, tiled=True)  61.4 us
    reduce_scatter x1, waiting for transfers between devices, body(): dx = lax.psum_scatter(dxp, 'fsdp', scatter_dimension=0, tiled=True)  52.3 us
    reduce_scatter x1, waiting for transfers between devices, body(): moe = lax.psum_scatter(yp, 'fsdp', scatter_dimension=0, tiled=True)  50.1 us
    all_gather x1, waiting for transfers between devices, body(): n2_all = lax.all_gather(n2, 'fsdp', axis=0, tiled=True)  47.4 us
    psum x1, waiting for transfers between devices, body(): gs = lax.psum(gs, 'replica')  44.4 us
    psum x1, waiting for transfers between devices, body(): gw = lax.psum(gw, 'replica').astype(F32)  39.7 us
  transfers between devices with their start and end apart: 10, of which 10 were waited for; matrix products, arithmetic and copies ran while one was open for 3% of the time, Pallas kernels for 4%

profile of v1, /device:TPU:10, one launch (start us, length us, event | category | flops | bytes accessed | tf_op | source)
XLA Modules:
  0.0 679.6 jit_solution(1486710821900034341)
XLA Ops:
  7.2 0.8 copy.34
  8.0 0.8 copy.35
  8.8 0.8 copy.33
  9.6 2.1 concatenate.7
  11.8 0.7 all-gather.9.cloned.1.call-update
  12.5 1.5 copy.36.routes_ref
  14.1 0.8 select_reduce_fusion.1
  15.0 1.2 fusion
  16.2 61.4 %all-gather.5.cloned.1.call-done.w_ref = bf16[1024,3200]{1,0:T(8,128)(2,1)} async-done(((bf16[128,3200]{1,0:T(8,128)(2,1)}), bf16[1024,3200]{1,0:T(8,128)(2,1)}) %all-gather.5.cloned.1.call-update) | async-done | bytes 6553616 | tf_op jit(solution)/shard_map/all_gather | solution.py:307
  77.6 10.8 %shard_map.204 = (bf16[256,1024]{1,0:T(8,128)(2,1)}, bf16[256,1024]{1,0:T(8,128)(2,1)}, bf16[256,1024]{1,0:T(8,128)(2,1)}, f32[8,512,256]{2,1,0:T(8,128)}, bf16[...) custom-call(bf16[256,1024]{1,0:T(8,128)(2,1)} %x_ref.3, ...), custom_call_target="tpu_custom_call" | custom-call | tf_op jit(solution)/shard_map/pallas_call | solution.py:262
  88.5 15.8 %all-gather = f32[128,256]{1,0:T(8,128)} all-gather(f32[16,256]{1,0:T(8,128)} %get-tuple-element.32), channel_id=2, replica_groups=mesh['replica'=4,'fsdp'=8] {'fsdp'}, dimensions={0}, use_global_device_ids=true | all-gather | bytes 147456 | tf_op jit(solution)/shard_map/all_gather | solution.py:320
  104.4 22.5 %all-gather.9.cloned.1.call-done.do_ref = bf16[2048,1024]{1,0:T(8,128)(2,1)} async-done(((bf16[256,1024]{1,0:T(8,128)(2,1)}), bf16[2048,1024]{1,0:T(8,128)(2,1)}) %all-gather.9.cloned.1.call-update) | async-done | bytes 4194320 | tf_op jit(solution)/shard_map/all_gather | solution.py:308
  126.9 47.4 %all-gather.7.cloned.1.call-done.n2_ref = bf16[2048,1024]{1,0:T(8,128)(2,1)} async-done(((bf16[256,1024]{1,0:T(8,128)(2,1)}), bf16[2048,1024]{1,0:T(8,128)(2,1)}) %all-gather.7.cloned.1.call-update) | async-done | bytes 4194320 | tf_op jit(solution)/shard_map/all_gather | solution.py:319
  174.3 33.0 %shard_map.205 = (bf16[2048,1024]{1,0:T(8,128)(2,1)}, bf16[2048,1152]{1,0:T(8,128)(2,1)}, bf16[2,1152,1024]{2,1,0:T(8,128)(2,1)}, bf16[2,1152,1024]{2,1,0:T(8,12...) custom-call(s32[1]{0:T(128)} %bitcast.3.base_ref, ...), custom_call_target="tpu_custom_call" | custom-call | tf_op jit(solution)/shard_map/pallas_call | solution.py:325
  207.6 52.3 %reduce-scatter.7.cloned.1.call-done.dx_ref = bf16[256,1152]{1,0:T(8,128)(2,1)} async-done(((bf16[2048,1152]{1,0:T(8,128)(2,1)}), bf16[256,1152]{1,0:T(8,128)(2,1)}) %reduce-scatter.7.cloned.1.call-update) | async-done | bytes 589840 | tf_op jit(solution)/shard_map/reduce_scatter | solution.py:345
  259.9 16.9 %shard_map.206 = (f32[256,1024]{1,0:T(8,128)}, bf16[1024,3072]{1,0:T(8,128)(2,1)}, f32[1024,256]{1,0:T(8,128)}) custom-call(bf16[256,1024]{1,0:T(8,128)(2,1)} %x_ref.3, bf16[256,1024]{1,0:T(8,128)(2,1)} %dout_ref.1, f32[256,128]{1,0:T(8,128)} %get-tuple-element.87.cos_ref, f32[256,128]{1,0:T(8,128)} %get-tuple-element.86.sin_ref, ...), custom_call_target="tpu_custom_call" | custom-call | tf_op jit(solution)/shard_map/pallas_call | solution.py:262
  276.9 13.6 %shard_map.207 = bf16[2,1536,1024]{2,1,0:T(8,128)(2,1)} custom-call(bf16[2,1152,1024]{2,1,0:T(8,128)(2,1)} %get-tuple-element.44.xs_ref, bf16[2,1152,1024]{2,1,0:T(8,128)(2,1)} %get-tuple-element.45.dye_ref, bf16[2,1152,1024]{2,1,0:T(8,128)(2,1)} %get-tuple-element.46.dgu_ref, bf16[2,1152,512]{2,1,0:T(8,128)(2,1)} %get-tuple-element.47.hx_ref), custom_call_target="tpu_custom_call" | custom-call | tf_op jit(solution)/shard_map/pallas_call | solution.py:347
  290.5 0.7 reduce-scatter.11.cloned.1.call-update
  291.3 0.7 reduce-scatter.5.cloned.1.call-update
  292.0 14.9 %reduce-scatter.9.cloned.1.call-done = f32[128,256]{1,0:T(8,128)} async-done(((f32[1024,256]{1,0:T(8,128)}), f32[128,256]{1,0:T(8,128)}) %reduce-scatter.9.cloned.1.call-update) | async-done | bytes 131088 | tf_op jit(solution)/shard_map/reduce_scatter | solution.py:365
  307.0 143.4 %all-reduce.6.cloned.1.call-done = bf16[2,1536,1024]{2,1,0:T(8,128)(2,1)} async-done(((bf16[2,1536,1024]{2,1,0:T(8,128)(2,1)}), bf16[2,1536,1024]{2,1,0:T(8,128)(2,1)}) %all-reduce.6.cloned.1.call-update) | async-done | bytes 6291472 | tf_op jit(solution)/shard_map/psum | solution.py:357
  450.4 69.9 %reduce-scatter.11.cloned.1.call-done = bf16[128,3072]{1,0:T(8,128)(2,1)} async-done(((bf16[1024,3072]{1,0:T(8,128)(2,1)}), bf16[128,3072]{1,0:T(8,128)(2,1)}) %reduce-scatter.11.cloned.1.call-update) | async-done | bytes 786448 | tf_op jit(solution)/shard_map/reduce_scatter | solution.py:364
  520.4 50.1 %reduce-scatter.5.cloned.1.call-done = bf16[256,1024]{1,0:T(8,128)(2,1)} async-done(((bf16[2048,1024]{1,0:T(8,128)(2,1)}), bf16[256,1024]{1,0:T(8,128)(2,1)}) %reduce-scatter.5.cloned.1.call-update) | async-done | bytes 524304 | tf_op jit(solution)/shard_map/reduce_scatter | solution.py:355
  570.5 2.0 add_convert_fusion
  572.5 44.4 %all-reduce.4.cloned.1.call-done = f32[128,256]{1,0:T(8,128)} async-done(((f32[128,256]{1,0:T(8,128)}), f32[128,256]{1,0:T(8,128)}) %all-reduce.4.cloned.1.call-update) | async-done | bytes 131088 | tf_op jit(solution)/shard_map/psum | solution.py:368
  616.9 0.8 slice.34
  617.7 0.7 copy.37
  618.4 1.6 slice_reduce_fusion
  620.0 9.1 %convert_element_type.23 = f32[2,1536,1024]{2,1,0:T(8,128)} convert(bf16[2,1536,1024]{2,1,0:T(8,128)(2,1)} %all-reduce.6.cloned.1.call-done) | non-fusion elementwise | flops 3145728 | bytes 18874368 | tf_op jit(solution)/shard_map/convert_element_type | solution.py:369
  629.1 39.7 %all-reduce.8.cloned.1.call-done = bf16[128,3072]{1,0:T(8,128)(2,1)} async-done(((bf16[128,3072]{1,0:T(8,128)(2,1)}), bf16[128,3072]{1,0:T(8,128)(2,1)}) %all-reduce.8.cloned.1.call-update) | async-done | bytes 786448 | tf_op jit(solution)/shard_map/psum | solution.py:367
  668.9 1.8 fusion.2
  670.7 2.1 fusion.1
  (24 shorter events, 0.9 us)
Async XLA Ops:
  7.2 70.5 %all-gather.5.cloned.1.call-start = ((), (), s32[]{:S(2)}) async-start(), calls=%async_computation.4 | async-start | bytes 7372800 | tf_op jit(solution)/shard_map/all_gather | solution.py:307
  11.7 115.2 %all-gather.9.cloned.1.call-start = ((), (), s32[]{:S(2)}) async-start(), calls=%async_computation.6 | async-start | bytes 4718592 | tf_op jit(solution)/shard_map/all_gather | solution.py:308
  12.5 161.9 %all-gather.7.cloned.1.call-start = ((), (), s32[]{:S(2)}) async-start(), calls=%async_computation.5 | async-start | bytes 4718592 | tf_op jit(solution)/shard_map/all_gather | solution.py:319
  88.5 171.5 %reduce-scatter.7.cloned.1.call-start = ((), (), s32[]{:S(2)}) async-start(), calls=%async_computation.8 | async-start | bytes 5308416 | tf_op jit(solution)/shard_map/reduce_scatter | solution.py:345
  207.3 99.6 %reduce-scatter.9.cloned.1.call-start = ((), (), s32[]{:S(2)}) async-start(), calls=%async_computation.9 | async-start | bytes 1179648 | tf_op jit(solution)/shard_map/reduce_scatter | solution.py:365
  276.8 173.6 %all-reduce.6.cloned.1.call-start = ((), (), s32[]{:S(2)}) async-start(), calls=%async_computation.12 | async-start | bytes 12582912 | tf_op jit(solution)/shard_map/psum | solution.py:357
  290.5 229.9 %reduce-scatter.11.cloned.1.call-start = ((), (), s32[]{:S(2)}) async-start(), calls=%async_computation.11 | async-start | bytes 7077888 | tf_op jit(solution)/shard_map/reduce_scatter | solution.py:364
  290.5 280.0 %copy-start = (f32[256,1024]{1,0:T(8,128)S(1)}, f32[256,1024]{1,0:T(8,128)}, u32[]{:S(2)}) copy-start(f32[256,1024]{1,0:T(8,128)} %get-tuple-element.30.h1_ref) | copy-start | bytes 3145732
  291.2 279.3 %reduce-scatter.5.cloned.1.call-start = ((), (), s32[]{:S(2)}) async-start(), calls=%async_computation.7 | async-start | bytes 4718592 | tf_op jit(solution)/shard_map/reduce_scatter | solution.py:355
  292.0 324.9 %all-reduce.4.cloned.1.call-start = ((), (), s32[]{:S(2)}) async-start(), calls=%async_computation.10 | async-start | bytes 262144 | tf_op jit(solution)/shard_map/psum | solution.py:368
  307.0 361.9 %all-reduce.8.cloned.1.call-start = ((), (), s32[]{:S(2)}) async-start(), calls=%async_computation.13 | async-start | bytes 1572864 | tf_op jit(solution)/shard_map/psum | solution.py:367
Sparse Core Ops, SparseCore 0:
  11.8 65.7 all-gather.4
  79.2 47.6 all-gather.8
  128.5 45.7 all-gather.6
  207.5 52.4 reduce-scatter.6
  277.0 29.9 reduce-scatter.8
  310.1 140.2 all-reduce.5
  453.3 67.0 reduce-scatter.10
  522.7 47.7 reduce-scatter.4
  573.4 43.4 all-reduce.3
  620.1 48.7 all-reduce.7

commit v2 on v1

--- a/solution.py
+++ b/solution.py
@@ -1,3 +1,5 @@
+import functools
+
 import jax
 import jax.numpy as jnp
 import numpy as np
@@ -25,7 +27,7 @@
 
 BF = jnp.bfloat16
 F32 = jnp.float32
-VMEM_LIMIT = 60 * 2**20
+VMEM_LIMIT = 63 * 2**20
 
 
 def dot(a, b):
@@ -193,11 +195,15 @@
 
 def attention_backward(
     x_ref, dout_ref, cos_ref, sin_ref, w_ref, q_ref, kd_ref, vd_ref, p_ref, o_ref, h1_ref, n2_ref, gd_ref, dx_ref,
-    gin_ref, gw_ref, gs_ref, do_ref, dqkv_ref,
+    gin_ref, gw_ref, do_ref, dqkv_ref,
 ):
     tokens = x_ref.shape[0]
     lane = lanes_of(tokens)
     low = lane < HD
+
+    def put(at, value):
+        gw_ref[:, :, :, at] = value.astype(BF).reshape(*gw_ref.shape[:3], value.shape[1])
+
     small = w_ref[:, QKVO:].astype(F32).T
     gain_one, gain_two = small[E : E + 1], small[E + 1 : E + 2]
     after = h1_ref[...]
@@ -214,7 +220,7 @@
     )
     grad_gain_two = jnp.sum(grad_normed * after * factor_two, axis=0, keepdims=True)
     grad_branch = (residual_scale * grad_after).astype(BF)
-    gw_ref[:, QKVO - D :] = dot_tn(o_ref[...], grad_branch).astype(BF)
+    put(slice(QKVO - D, QKVO), dot_tn(o_ref[...], grad_branch))
     do_ref[...] = dot_nt(grad_branch, w_ref[:, QKVO - D : QKVO]).astype(BF)
     grad_router = dot_tn(n2_ref[...], grad_logits)
 
@@ -245,19 +251,285 @@
     source = x_ref[...].astype(F32)
     factor_one = lax.rsqrt(jnp.mean(source * source, axis=1, keepdims=True) + norm_eps)
     normed = (source * factor_one * gain_one).astype(BF)
-    gw_ref[:, : QKVO - D] = dot_tn(normed, dqkv_ref[...]).astype(BF)
+    put(slice(0, QKVO - D), dot_tn(normed, dqkv_ref[...]))
     grad_normed = dot_nt(dqkv_ref[...], w_ref[:, : QKVO - D])
     scaled = grad_normed * gain_one
     grad_vector = factor_one * scaled - source * factor_one**3 * jnp.mean(scaled * source, axis=1, keepdims=True)
     gin_ref[...] = grad_after + grad_vector
     grad_gain_one = jnp.sum(grad_normed * source * factor_one, axis=0, keepdims=True)
-    pad = jnp.zeros((6, D), F32)
-    gains = jnp.concatenate([grad_gain_one, grad_gain_two, pad], axis=0).T
-    gs_ref[:, :LANE] = grad_router
-    gs_ref[:, LANE:] = jnp.concatenate([gains, jnp.zeros((D, LANE - 8), F32)], axis=1)
-
-
-def call(kernel, out_shape, args, scratch=(), **more):
+    gains = jnp.concatenate([grad_gain_one, grad_gain_two, jnp.zeros((6, D), F32)], axis=0).T
+    at = lanes_of(D)
+    extra = jnp.where(at == E, gains[:, 0:1], jnp.where(at == E + 1, gains[:, 1:2], grad_router))
+    put(slice(QKVO, QKVO + LANE), extra)
+
+
+def add_rows(target, first, second, rows, step):
+    def some(i, carry):
+        at = pl.ds(pl.multiple_of(i * step, step), step)
+        target(at, first(at).astype(F32) + second(at).astype(F32))
+        return carry
+
+    lax.fori_loop(0, rows // step, some, 0)
+
+
+class Copies:
+    def __init__(self):
+        self.sent = []
+
+    def make(self, src, dst, send, recv, device):
+        return pltpu.make_async_remote_copy(
+            src_ref=src, dst_ref=dst, send_sem=send, recv_sem=recv, device_id=device, device_id_type=pl.DeviceIdType.MESH
+        )
+
+
+def tail(
+    replicas, chips,
+    x_ref, dout_ref, cos_ref, sin_ref, w_ref, q_ref, kd_ref, vd_ref, p_ref, o_ref, h1_ref, n2_ref, gd_ref, dx_ref, ge_ref,
+    gin_ref, gexp_ref, gproj_ref,
+    do_ref, dqkv_ref, gw_ref, core_ref, up_ref, down_ref, parts_ref, smalls_ref, result_ref, *rest,
+):
+    bits = replicas.bit_length() - 1
+    jobs = ge_ref.shape[0] * bits
+    arrived = rest[:bits]
+    kept = rest[bits : 2 * bits - 1] if bits else ()
+    rest = rest[2 * bits - 1 if bits else 0 :]
+    (ar_send, ar_recv, core_send, core_recv, up_send, up_recv, down_send, down_recv,
+     part_send, part_recv, small_send, small_recv, result_send, result_recv) = rest
+    r, f = lax.axis_index("replica"), lax.axis_index("fsdp")
+    z, c = f // 2, f % 2
+    mate = (r, z * 2 + 1 - c)
+    above, below = (r, f + 2), (r, f - 2)
+    rows = gw_ref.shape[2]
+    make = Copies().make
+
+    barrier = pltpu.get_barrier_semaphore()
+    expected = 1 + (replicas - 1) + jnp.where(z > 0, 1, 0) + jnp.where(z < chips - 1, 1, 0)
+    pl.semaphore_signal(barrier, inc=1, device_id=mate, device_id_type=pl.DeviceIdType.MESH)
+    for d in range(1, replicas):
+        pl.semaphore_signal(barrier, inc=1, device_id=((r + d) % replicas, f), device_id_type=pl.DeviceIdType.MESH)
+
+    @pl.when(z > 0)
+    def _():
+        pl.semaphore_signal(barrier, inc=1, device_id=below, device_id_type=pl.DeviceIdType.MESH)
+
+    @pl.when(z < chips - 1)
+    def _():
+        pl.semaphore_signal(barrier, inc=1, device_id=above, device_id_type=pl.DeviceIdType.MESH)
+
+    pl.semaphore_wait(barrier, expected)
+
+    def bit_of(b):
+        return (r // (1 << b)) % 2
+
+    def partner(b):
+        return (r + (1 - 2 * bit_of(b)) * (1 << b), f)
+
+    def halving(e):
+        size = ge_ref.shape[1] // bits
+        orders = [[(g + k) % bits for k in range(bits)] for g in range(bits)]
+        starts = [[] for _ in range(bits)]
+        for g in range(bits):
+            at = g * size
+            for k in range(bits):
+                starts[g].append(at)
+                at = at + bit_of(orders[g][k]) * (size >> (k + 1))
+            starts[g].append(at)
+        copies = {}
+
+        def source(g, k, at, length):
+            return ge_ref.at[e, pl.ds(g * size + at, length)] if k == 0 else kept[k - 1].at[e * bits + g, pl.ds(at, length)]
+
+        def exchange(g, k):
+            half = size >> (k + 1)
+            give = pl.multiple_of((1 - bit_of(orders[g][k])) * half, half)
+            copies[g, k] = make(
+                source(g, k, give, half), arrived[k].at[e * bits + g], ar_send.at[e * bits + g, k],
+                ar_recv.at[e * bits + g, k], partner(orders[g][k]),
+            )
+            copies[g, k].start()
+
+        def spread(g, k):
+            half = size >> (k + 1)
+            at = pl.ds(pl.multiple_of(starts[g][k + 1], half), half)
+            copies[g, bits + k] = make(
+                gexp_ref.at[e, at], gexp_ref.at[e, at], ar_send.at[e * bits + g, bits + k],
+                ar_recv.at[e * bits + g, bits + k], partner(orders[g][k]),
+            )
+            copies[g, bits + k].start()
+
+        for g in range(bits):
+            exchange(g, 0)
+        yield
+        for k in range(bits):
+            half = size >> (k + 1)
+            for g in range(bits):
+                copies[g, k].wait_recv()
+                keep = pl.multiple_of(bit_of(orders[g][k]) * half, half)
+                own = source(g, k, keep, half)
+                there = arrived[k].at[e * bits + g]
+                if k < bits - 1:
+                    into = kept[k].at[e * bits + g]
+                else:
+                    into = gexp_ref.at[e, pl.ds(pl.multiple_of(starts[g][bits], half), half)]
+
+                def write(at, value, into=into):
+                    into[at] = value.astype(BF)
+
+                add_rows(write, lambda at: own[at], lambda at: there[at], half, min(half, 64))
+                if k < bits - 1:
+                    exchange(g, k + 1)
+                else:
+                    spread(g, k)
+            yield
+        for k in range(bits - 1, -1, -1):
+            for g in range(bits):
+                copies[g, bits + k].wait_recv()
+                if k > 0:
+                    spread(g, k - 1)
+            yield
+        for copy in copies.values():
+            copy.wait_send()
+
+    def line():
+        crossing = make(gw_ref.at[:, 1 - c], core_ref, core_send.at[0], core_recv.at[0], mate)
+        crossing.start()
+        yield
+        crossing.wait_recv()
+
+        def add_block(block, other):
+            def write(at, value):
+                gw_ref[block, c, at] = value.astype(BF)
+
+            add_rows(write, lambda at: gw_ref[block, c, at], lambda at: other[block, at], rows, 16)
+
+        def send(block, up):
+            there, send_sem, recv_sem = (up_ref, up_send, up_recv) if up else (down_ref, down_send, down_recv)
+            return make(
+                gw_ref.at[block, c], there.at[block], send_sem.at[block], recv_sem.at[block], above if up else below
+            )
+
+        for k in range(chips):
+            add_block(k, core_ref)
+        for k in range(chips - 1):
+            owner = chips - 1 - k
+
+            @pl.when(z == 0)
+            def _():
+                send(owner, True).start()
+
+            @pl.when(z == chips - 1)
+            def _():
+                send(k, False).start()
+
+        yield
+        for k in range(chips - 2):
+            owner = chips - 1 - k
+
+            @pl.when((z > 0) & (z < owner))
+            def _():
+                send(owner, True).wait_recv()
+                add_block(owner, up_ref)
+                send(owner, True).start()
+
+            @pl.when((z < chips - 1) & (z > k))
+            def _():
+                send(k, False).wait_recv()
+                add_block(k, down_ref)
+                send(k, False).start()
+
+            yield
+
+        @pl.when(z > 0)
+        def _():
+            send(z, True).wait_recv()
+            add_block(z, up_ref)
+
+        @pl.when(z < chips - 1)
+        def _():
+            send(z, False).wait_recv()
+            add_block(z, down_ref)
+
+        wide = QKVO // replicas
+
+        def columns(part):
+            return pl.ds(pl.multiple_of(part * wide, LANE), wide)
+
+        own = gw_ref.at[z, c]
+
+        def part_copy(d):
+            to = (r + d) % replicas
+            return make(own.at[:, columns(to)], parts_ref.at[r], part_send.at[d], part_recv.at[r], (to, f))
+
+        def small_copy(d):
+            to = (r + d) % replicas
+            return make(own.at[:, pl.ds(QKVO, LANE)], smalls_ref.at[r], small_send.at[d], small_recv.at[r], (to, f))
+
+        for d in range(1, replicas):
+            part_copy(d).start()
+            small_copy(d).start()
+        parts_ref[r] = own[:, columns(r)]
+        smalls_ref[r] = own[:, pl.ds(QKVO, LANE)]
+        yield
+        for d in range(1, replicas):
+            peer = (r + d) % replicas
+            make(parts_ref.at[peer], parts_ref.at[peer], part_send.at[d], part_recv.at[peer], (peer, f)).wait_recv()
+            make(smalls_ref.at[peer], smalls_ref.at[peer], small_send.at[d], small_recv.at[peer], (peer, f)).wait_recv()
+        total = parts_ref[0].astype(F32)
+        small = smalls_ref[0].astype(F32)
+        for k in range(1, replicas):
+            total = total + parts_ref[k].astype(F32)
+            small = small + smalls_ref[k].astype(F32)
+        result_ref[r] = total.astype(BF)
+        gproj_ref[:, QKVO:] = small
+
+        def result_copy(d):
+            to = (r + d) % replicas
+            return make(result_ref.at[r], result_ref.at[r], result_send.at[d], result_recv.at[r], (to, f))
+
+        for d in range(1, replicas):
+            result_copy(d).start()
+        yield
+        for d in range(1, replicas):
+            peer = (r + d) % replicas
+            make(result_ref.at[peer], result_ref.at[peer], result_send.at[d], result_recv.at[peer], (peer, f)).wait_recv()
+        for k in range(replicas):
+            gproj_ref[:, k * wide : (k + 1) * wide] = result_ref[k].astype(F32)
+        crossing.wait_send()
+        for k in range(chips):
+
+            @pl.when(z < k)
+            def _():
+                send(k, True).wait_send()
+
+            @pl.when(z > k)
+            def _():
+                send(k, False).wait_send()
+
+        for d in range(1, replicas):
+            part_copy(d).wait_send()
+            small_copy(d).wait_send()
+            result_copy(d).wait_send()
+
+    experts_sums = [halving(e) for e in range(ge_ref.shape[0])] if bits else []
+    for e, sums in enumerate(experts_sums):
+        next(sums)
+    if not bits:
+        gexp_ref[...] = ge_ref[...]
+    attention_backward(
+        x_ref, dout_ref, cos_ref, sin_ref, w_ref, q_ref, kd_ref, vd_ref, p_ref, o_ref, h1_ref, n2_ref, gd_ref, dx_ref,
+        gin_ref, gw_ref, do_ref, dqkv_ref,
+    )
+    projections = line()
+    first, last = experts_sums[:1], experts_sums[1:]
+    order = [[projections], first, [projections], last, [projections], first, last, [projections], first, last]
+    order += [[projections], first, [projections], last, [projections]]
+    order += [[projections] + experts_sums] * (chips + 2 * bits)
+    for turn in order:
+        for process in turn:
+            next(process, None)
+
+
+def call(kernel, out_shape, args, scratch=(), **params):
     smem = [a.dtype == jnp.int32 and a.size <= 16 for a in args]
     return pl.pallas_call(
         kernel,
@@ -265,8 +537,9 @@
         in_specs=[pl.BlockSpec(memory_space=pltpu.SMEM if s else pltpu.VMEM) for s in smem],
         out_specs=jax.tree.map(lambda _: pl.BlockSpec(memory_space=pltpu.VMEM), out_shape),
         scratch_shapes=list(scratch),
-        compiler_params=pltpu.CompilerParams(vmem_limit_bytes=VMEM_LIMIT),
-        **more,
+        compiler_params=pltpu.CompilerParams(
+            vmem_limit_bytes=VMEM_LIMIT, has_side_effects="collective_id" in params, **params
+        ),
     )(*args)
 
 
@@ -287,7 +560,7 @@
 
 
 def make_body(mesh):
-    group = mesh.shape["fsdp"]
+    group, replicas = mesh.shape["fsdp"], mesh.shape["replica"]
     local = E // group
     chunk = 2
 
@@ -354,23 +627,31 @@
         )(xs, dye, dgu, hx)
         moe = lax.psum_scatter(yp, "fsdp", scatter_dimension=0, tiled=True)
         layer_out = (h1 + residual_scale * moe.astype(F32)).astype(BF)
-        grad_experts = lax.psum(grad_experts, "replica")
-        grad_in, gw, gs = call(
-            attention_backward,
-            (shape((tokens, D), F32), shape((D, QKVO), BF), shape((D, 2 * LANE), F32)),
-            (hidden_in, out_cotangent, cosines, sines, weights, q, kd, vd, p, o, h1, n2, gd, dx),
-            [pltpu.VMEM((tokens, D), BF), pltpu.VMEM((tokens, QKVO - D), BF)],
+        bits = replicas.bit_length() - 1
+        rows = D // group
+        size = 3 * FF // bits if bits else 0
+        dma = pltpu.SemaphoreType.DMA
+        grad_in, grad_experts, gw = call(
+            functools.partial(tail, replicas, group // 2),
+            (shape((tokens, D), F32), shape((local, 3 * FF, D), BF), shape((rows, QKVO + LANE), F32)),
+            (hidden_in, out_cotangent, cosines, sines, weights, q, kd, vd, p, o, h1, n2, gd, dx, grad_experts),
+            [
+                pltpu.VMEM((tokens, D), BF), pltpu.VMEM((tokens, QKVO - D), BF),
+                pltpu.VMEM((group // 2, 2, rows, QKVO + LANE), BF), pltpu.VMEM((group // 2, rows, QKVO + LANE), BF),
+                pltpu.VMEM((group // 2, rows, QKVO + LANE), BF), pltpu.VMEM((group // 2, rows, QKVO + LANE), BF),
+                pltpu.VMEM((replicas, rows, QKVO // replicas), BF), pltpu.VMEM((replicas, rows, LANE), BF),
+                pltpu.VMEM((replicas, rows, QKVO // replicas), BF),
+            ]
+            + [pltpu.VMEM((local * bits, size >> (k + 1), D), BF) for k in range(bits)]
+            + [pltpu.VMEM((local * bits, size >> (k + 1), D), BF) for k in range(bits - 1)]
+            + [dma((max(local * bits, 1), max(2 * bits, 1)))] * 2 + [dma((1,))] * 2 + [dma((group // 2,))] * 4
+            + [dma((replicas,))] * 6,
+            collective_id=0,
         )
-        gw = lax.psum_scatter(gw, "fsdp", scatter_dimension=0, tiled=True)
-        gs = lax.psum_scatter(gs, "fsdp", scatter_dimension=0, tiled=True)
-        gw, grad_experts = lax.optimization_barrier((gw, grad_experts))
-        gw = lax.psum(gw, "replica").astype(F32)
-        gs = lax.psum(gs, "replica")
-        grad_experts = grad_experts.astype(F32)
         a, b, c = H * HD, H * HD + KVH * HD, H * HD + 2 * KVH * HD
         return (
-            layer_out, grad_in, gs[:, LANE], gw[:, :a], gw[:, a:b], gw[:, b:c], gw[:, c:], gs[:, LANE + 1],
-            gs[:, :E], grad_experts,
+            layer_out, grad_in, gw[:, QKVO + E], gw[:, :a], gw[:, a:b], gw[:, b:c], gw[:, c:QKVO], gw[:, QKVO + E + 1],
+            gw[:, QKVO : QKVO + E], grad_experts.astype(F32),
         )
 
     return body

time: 682 us -> 487 us (0.71)
  waiting for transfers between devices: 548 us -> 219 us
  Pallas kernels: 74.2 us -> 208 us
    psum x3 -> x0, waiting for transfers between devices: 228 us -> none  [the longest x1 143 us: body(): grad_experts = lax.psum(grad_experts, 'replica')]
    pallas_call x2, Pallas kernels: 27.7 us -> 161 us  [call(): pl.pallas_call(kernel, out_shape=out_shape, in_specs=[pl.BlockSpec(memory...]
    reduce_scatter x2 -> x0, waiting for transfers between devices: 84.9 us -> none  [the longest x1 69.9 us: body(): gw = lax.psum_scatter(gw, 'fsdp', scatter_dimension=0, tiled=True)]
    reduce_scatter x1, waiting for transfers between devices: 50.1 us -> 32.9 us  [body(): moe = lax.psum_scatter(yp, 'fsdp', scatter_dimension=0, tiled=True)]
  transfers between devices with their start and end apart: 10 -> 5, of which waited for: 10 -> 5; matrix products, arithmetic and copies ran while one was open for 3% -> 1% of each run, Pallas kernels for 4% -> 5%
where the time goes in v2:
time: 487 us; the launch traced here: 485 us
  waiting for transfers between devices  219 us (45%)
  Pallas kernels  208 us (43%)
  blocking collectives  15.8 us (3%)
  local copies, waits for them, and re-layouts  14.2 us (3%)
  between operations  13.8 us (3%)
  other arithmetic  13.7 us (3%)
    pallas_call x2, Pallas kernels, call(): pl.pallas_call(kernel, out_shape=out_shape, in_specs=[pl.BlockSpec(memory...  161 us
    all_gather x1, waiting for transfers between devices, body(): weights = lax.all_gather(packed, 'fsdp', axis=0, tiled=True)  61.4 us
    reduce_scatter x1, waiting for transfers between devices, body(): dx = lax.psum_scatter(dxp, 'fsdp', scatter_dimension=0, tiled=True)  53.5 us
    all_gather x1, waiting for transfers between devices, body(): n2_all = lax.all_gather(n2, 'fsdp', axis=0, tiled=True)  47.4 us
    pallas_call x1, Pallas kernels, body(): pl.pallas_call(experts, grid=(group // chunk,), in_specs=[pl.BlockSpec(me...  33 us
    reduce_scatter x1, waiting for transfers between devices, body(): moe = lax.psum_scatter(yp, 'fsdp', scatter_dimension=0, tiled=True)  32.9 us
    all_gather x1, waiting for transfers between devices, body(): dout_all = lax.all_gather(out_cotangent, 'fsdp', axis=0, tiled=True)  22.5 us
    all_gather x1, blocking collectives, body(): gt_all = lax.all_gather(gt, 'fsdp', axis=0, tiled=False)  15.8 us
  transfers between devices with their start and end apart: 5, of which 5 were waited for; matrix products, arithmetic and copies ran while one was open for 1% of the time, Pallas kernels for 5%

profile of v2, /device:TPU:10, one launch (start us, length us, event | category | flops | bytes accessed | tf_op | source)
XLA Modules:
  0.0 484.8 jit_solution(5901817942202852359)
XLA Ops:
  7.2 0.8 copy.34
  8.0 0.8 copy.35
  8.8 0.8 copy.33
  9.6 2.1 concatenate.7
  11.7 0.0 all-gather.9.cloned.1.call-start
  11.8 0.7 all-gather.9.cloned.1.call-update
  12.5 1.5 copy.36.routes_ref
  14.0 0.1 compare_select_fusion
  14.1 0.8 select_reduce_fusion.1
  14.9 0.1 select_reduce_fusion
  15.0 1.2 fusion
  16.2 61.4 %all-gather.5.cloned.1.call-done.w_ref = bf16[1024,3200]{1,0:T(8,128)(2,1)} async-done(((bf16[128,3200]{1,0:T(8,128)(2,1)}), bf16[1024,3200]{1,0:T(8,128)(2,1)}) %all-gather.5.cloned.1.call-update) | async-done | bytes 6553616 | tf_op jit(solution)/shard_map/all_gather | solution.py:580
  77.6 10.8 %shard_map.204 = (bf16[256,1024]{1,0:T(8,128)(2,1)}, bf16[256,1024]{1,0:T(8,128)(2,1)}, bf16[256,1024]{1,0:T(8,128)(2,1)}, f32[8,512,256]{2,1,0:T(8,128)}, bf16[...) custom-call(bf16[256,1024]{1,0:T(8,128)(2,1)} %x_ref.3, ...), custom_call_target="tpu_custom_call" | custom-call | tf_op jit(solution)/shard_map/pallas_call | solution.py:534
  88.5 0.0 reduce-scatter.3.cloned.1.call-start
  88.5 15.8 %all-gather = f32[128,256]{1,0:T(8,128)} all-gather(f32[16,256]{1,0:T(8,128)} %get-tuple-element.30), channel_id=2, replica_groups=mesh['replica'=4,'fsdp'=8] {'fsdp'}, dimensions={0}, use_global_device_ids=true | all-gather | bytes 147456 | tf_op jit(solution)/shard_map/all_gather | solution.py:593
  104.4 22.5 %all-gather.9.cloned.1.call-done.do_ref = bf16[2048,1024]{1,0:T(8,128)(2,1)} async-done(((bf16[256,1024]{1,0:T(8,128)(2,1)}), bf16[2048,1024]{1,0:T(8,128)(2,1)}) %all-gather.9.cloned.1.call-update) | async-done | bytes 4194320 | tf_op jit(solution)/shard_map/all_gather | solution.py:581
  126.9 47.4 %all-gather.7.cloned.1.call-done.n2_ref = bf16[2048,1024]{1,0:T(8,128)(2,1)} async-done(((bf16[256,1024]{1,0:T(8,128)(2,1)}), bf16[2048,1024]{1,0:T(8,128)(2,1)}) %all-gather.7.cloned.1.call-update) | async-done | bytes 4194320 | tf_op jit(solution)/shard_map/all_gather | solution.py:592
  174.3 33.0 %shard_map.205 = (bf16[2048,1024]{1,0:T(8,128)(2,1)}, bf16[2048,1152]{1,0:T(8,128)(2,1)}, bf16[2,1152,1024]{2,1,0:T(8,128)(2,1)}, bf16[2,1152,1024]{2,1,0:T(8,12...) custom-call(s32[1]{0:T(128)} %bitcast.3.base_ref, ...), custom_call_target="tpu_custom_call" | custom-call | tf_op jit(solution)/shard_map/pallas_call | solution.py:598
  207.3 0.0 reduce-scatter.5.cloned.1.call-start
  207.4 0.5 reduce-scatter.5.cloned.1.call-update
  207.9 13.6 %shard_map.206.ge_ref = bf16[2,1536,1024]{2,1,0:T(8,128)(2,1)} custom-call(bf16[2,1152,1024]{2,1,0:T(8,128)(2,1)} %get-tuple-element.39.xs_ref, bf16[2,1152,1024]{2,1,0:T(8,128)(2,1)} %get-tuple-element.40.dye_ref, bf16[2,1152,1024]{2,1,0:T(8,128)(2,1)} %get-tuple-element.41.dgu_ref, bf16[2,1152,512]{2,1,0:T(8,128)(2,1)} %get-tuple-element.42.hx_ref), custom_call_target="tpu_custom_call" | custom-call | tf_op jit(solution)/shard_map/pallas_call | solution.py:620
  221.5 32.9 %reduce-scatter.3.cloned.1.call-done = bf16[256,1024]{1,0:T(8,128)(2,1)} async-done(((bf16[2048,1024]{1,0:T(8,128)(2,1)}), bf16[256,1024]{1,0:T(8,128)(2,1)}) %reduce-scatter.3.cloned.1.call-update) | async-done | bytes 524304 | tf_op jit(solution)/shard_map/reduce_scatter | solution.py:628
  254.4 2.3 add_convert_fusion
  256.7 53.5 %reduce-scatter.5.cloned.1.call-done.dx_ref = bf16[256,1152]{1,0:T(8,128)(2,1)} async-done(((bf16[2048,1152]{1,0:T(8,128)(2,1)}), bf16[256,1152]{1,0:T(8,128)(2,1)}) %reduce-scatter.5.cloned.1.call-update) | async-done | bytes 589840 | tf_op jit(solution)/shard_map/reduce_scatter | solution.py:618
  310.3 150.5 %shard_map.207 = (f32[256,1024]{1,0:T(8,128)}, bf16[2,1536,1024]{2,1,0:T(8,128)(2,1)}, f32[128,3200]{1,0:T(8,128)}) custom-call(bf16[256,1024]{1,0:T(8,128)(2,1)} %x_ref.3, bf16[256,1024]{1,0:T(8,128)(2,1)} %dout_ref.1, f32[256,128]{1,0:T(8,128)} %get-tuple-element.83.cos_ref, f32[256,128]{1,0:T(8,128)} %get-tuple-element.82.sin_ref, ...), custom_call_target="tpu_custom_call" | custom-call | tf_op jit(solution)/shard_map/pallas_call | solution.py:534
  460.8 1.6 slice_reduce_fusion
  462.4 0.8 slice.27
  463.3 1.9 fusion.2
  465.1 2.3 fusion.1
  467.4 0.7 copy.37
  468.1 9.2 %convert_element_type.19 = f32[2,1536,1024]{2,1,0:T(8,128)} convert(bf16[2,1536,1024]{2,1,0:T(8,128)(2,1)} %get-tuple-element.45) | non-fusion elementwise | flops 3145728 | bytes 18874368 | tf_op jit(solution)/shard_map/convert_element_type | solution.py:654
  477.3 1.0 copy.39
  (10 shorter events, 0.2 us)
Async XLA Ops:
  7.2 70.5 %all-gather.5.cloned.1.call-start = ((), (), s32[]{:S(2)}) async-start(), calls=%async_computation.2 | async-start | bytes 7372800 | tf_op jit(solution)/shard_map/all_gather | solution.py:580
  11.7 115.2 %all-gather.9.cloned.1.call-start = ((), (), s32[]{:S(2)}) async-start(), calls=%async_computation.4 | async-start | bytes 4718592 | tf_op jit(solution)/shard_map/all_gather | solution.py:581
  12.5 161.9 %all-gather.7.cloned.1.call-start = ((), (), s32[]{:S(2)}) async-start(), calls=%async_computation.3 | async-start | bytes 4718592 | tf_op jit(solution)/shard_map/all_gather | solution.py:592
  88.5 166.0 %reduce-scatter.3.cloned.1.call-start = ((), (), s32[]{:S(2)}) async-start(), calls=%async_computation.5 | async-start | bytes 4718592 | tf_op jit(solution)/shard_map/reduce_scatter | solution.py:628
  207.3 102.9 %reduce-scatter.5.cloned.1.call-start = ((), (), s32[]{:S(2)}) async-start(), calls=%async_computation.6 | async-start | bytes 5308416 | tf_op jit(solution)/shard_map/reduce_scatter | solution.py:618
  468.1 9.2 %copy-start = (f32[256,1024]{1,0:T(8,128)S(1)}, f32[256,1024]{1,0:T(8,128)}, u32[]{:S(2)}) copy-start(f32[256,1024]{1,0:T(8,128)} %get-tuple-element.97) | copy-start | bytes 3145732
Sparse Core Ops, SparseCore 0:
  11.8 65.7 all-gather.4
  79.2 47.6 all-gather.8
  128.5 45.7 all-gather.6
  207.5 46.9 reduce-scatter.2
  256.6 53.6 reduce-scatter.4

commit v3 on v2

--- a/solution.py
+++ b/solution.py
@@ -126,80 +126,245 @@
     gt_ref[...] = gates.T[:E]
 
 
-def experts(base_ref, n2_ref, do_ref, gt_ref, w_ref, yp_ref, dx_ref, xs_ref, dye_ref, dgu_ref, hx_ref):
+def middle(
+    chips, n2_ref, gt_ref, do_hbm, w_hbm,
+    dx_ref, yp_hbm, ge_ref,
+    n2_all, gt_all, do_buf, w_ref, xs_ref, dye_ref, dgu_ref, hx_ref, dxp_ref, yps_ref, core_ref, from_ref,
+    n2_up, n2_down, n2_mate, n2_recv, gt_up, gt_down, gt_mate, gt_recv,
+    core_send, core_recv, far_send, far_recv, do_sem, yp_sem, w_sem,
+):
     local = w_ref.shape[0]
-    sources = gt_ref.shape[0]
-    tokens = gt_ref.shape[2]
+    tokens = n2_ref.shape[0]
+    r, f = lax.axis_index("replica"), lax.axis_index("fsdp")
+    z, c = f // 2, f % 2
+    mate, above, below = (r, z * 2 + 1 - c), (r, f + 2), (r, f - 2)
+    make = Copies().make
+
+    pltpu.make_async_copy(w_hbm, w_ref, w_sem.at[0]).start()
+
+    def do_copy(zc, slot):
+        return pltpu.make_async_copy(do_hbm.at[zc], do_buf.at[slot], do_sem.at[slot])
+
+    do_copy(z, 0).start()
+
+    barrier = pltpu.get_barrier_semaphore()
+    pl.semaphore_signal(barrier, inc=1, device_id=mate, device_id_type=pl.DeviceIdType.MESH)
+    for k in range(1, chips):
+        to = (r, (z + k) % chips * 2 + c)
+        pl.semaphore_signal(barrier, inc=1, device_id=to, device_id_type=pl.DeviceIdType.MESH)
+    n2_all[z, c] = n2_ref[...]
+    gt_all[z, c] = gt_ref[...]
+    pl.semaphore_wait(barrier, chips)
+
+    def pass_on(zb, how):
+        to = {"up": above, "down": below, "mate": mate}[how]
+        sems = {"up": (n2_up, gt_up), "down": (n2_down, gt_down), "mate": (n2_mate, gt_mate)}[how]
+        return [
+            make(ref.at[zb, c], ref.at[zb, c], sem.at[zb], recv.at[zb, c], to)
+            for ref, sem, recv in ((gt_all, sems[1], gt_recv), (n2_all, sems[0], n2_recv))
+        ]
+
+    def got(zb, core):
+        for ref, sem, recv in ((gt_all, gt_mate, gt_recv), (n2_all, n2_mate, n2_recv)):
+            make(ref.at[zb, core], ref.at[zb, core], sem.at[zb], recv.at[zb, core], mate).wait_recv()
+
+    def start(copies):
+        for copy in copies:
+            copy.start()
+
+    @pl.when(z < chips - 1)
+    def _():
+        start(pass_on(z, "up"))
+
+    @pl.when(z > 0)
+    def _():
+        start(pass_on(z, "down"))
+
+    start(pass_on(z, "mate"))
+    inner = jnp.minimum(z, chips - 1 - z)
+
+    def place(t):
+        k = (t + 1) // 2
+        near = jnp.where(t % 2 == 1, z - k, z + k)
+        return jnp.where(t <= 2 * inner, near, jnp.where(2 * z < chips - 1, t, chips - 1 - t))
+
     before = lax.broadcasted_iota(jnp.int32, (tokens, tokens), 0) < lax.broadcasted_iota(jnp.int32, (tokens, tokens), 1)
     before = before.astype(F32).astype(BF)
-    slot = lax.broadcasted_iota(jnp.int32, (CAP, tokens), 0).astype(F32)
-    picks, gates = [], []
-    for s in range(sources):
-        rows = [gt_ref[s, pl.ds(base_ref[0] + i, 1), :] for i in range(local)]
-        mine = jnp.concatenate(rows, axis=0) if local > 1 else rows[0]
-        member = (mine >= 0.0).astype(F32)
-        rank = dot(member.astype(BF), before)
-        rank = jnp.where(mine >= 0.0, rank, -1.0)
-        chosen = [slot == rank[i : i + 1] for i in range(local)]
-        gates.append([jnp.sum(jnp.where(chosen[i], mine[i : i + 1], 0.0), axis=1, keepdims=True) for i in range(local)])
-        picks.append(jnp.concatenate([c.astype(F32).astype(BF) for c in chosen], axis=0))
-    dms = []
-    for s in range(sources):
-        at = slice(s * tokens, (s + 1) * tokens)
-        taken = dot(picks[s], n2_ref[at]).astype(BF)
-        grads = dot(picks[s], do_ref[at]) * residual_scale
-        dms.append(grads)
+    slot_index = lax.broadcasted_iota(jnp.int32, (CAP, tokens), 0).astype(F32)
+    lane = lanes_of(CAP)
+    pair = 2 * CAP
+
+    def far_copy(zc, slot, t):
+        return make(
+            dxp_ref.at[slot, c], from_ref.at[z], far_send.at[t], far_recv.at[z], (r, zc * 2 + c)
+        )
+
+    def core_copy(zc, slot, t):
+        return make(dxp_ref.at[slot, 1 - c], core_ref.at[zc], core_send.at[t], core_recv.at[zc], mate)
+
+    def yp_copy(zc, slot):
+        return pltpu.make_async_copy(yps_ref.at[slot], yp_hbm.at[zc], yp_sem.at[slot])
+
+    def chunk(t, carry):
+        zc = place(t)
+        slot = t % 2
+        k = jnp.where(zc > z, zc - z, z - zc)
+        both = (t % 2 == 1) & (t <= 2 * inner)
+        single = t > 2 * inner
+
+        @pl.when(both | (single & (zc < z)))
+        def _():
+            got(z - k, c)
+
+            @pl.when(z < chips - 1)
+            def _():
+                start(pass_on(z - k, "up"))
+
+            start(pass_on(z - k, "mate"))
+
+        @pl.when(both | (single & (zc > z)))
+        def _():
+            got(z + k, c)
+
+            @pl.when(z > 0)
+            def _():
+                start(pass_on(z + k, "down"))
+
+            start(pass_on(z + k, "mate"))
+
+        got(zc, 1 - c)
+
+        @pl.when(t < chips - 1)
+        def _():
+            do_copy(place(t + 1), 1 - slot).start()
+
+        do_copy(zc, slot).wait()
+
+        @pl.when(t == 0)
+        def _():
+            pltpu.make_async_copy(w_hbm, w_ref, w_sem.at[0]).wait()
+
+        @pl.when(t >= 2)
+        def _():
+            core_copy(z, slot, t - 2).wait_send()
+            yp_copy(z, slot).wait()
+
+        @pl.when(t >= 3)
+        def _():
+            far_copy(z, slot, t - 2).wait_send()
+
+        picks, gates, dms = [], [], []
+        at_chip = pl.multiple_of(zc * pair, 16)
+        for core in range(2):
+            rows = [gt_all[zc, core, pl.ds(f * local + i, 1), :] for i in range(local)]
+            mine = jnp.concatenate(rows, axis=0) if local > 1 else rows[0]
+            rank = jnp.where(mine >= 0.0, dot((mine >= 0.0).astype(F32).astype(BF), before), -1.0)
+            chosen = [slot_index == rank[i : i + 1] for i in range(local)]
+            gates.append([jnp.sum(jnp.where(chosen[i], mine[i : i + 1], 0.0), axis=1, keepdims=True) for i in range(local)])
+            picks.append(jnp.concatenate([one.astype(F32).astype(BF) for one in chosen], axis=0))
+            taken = dot(picks[core], n2_all[zc, core]).astype(BF)
+            grads = dot(picks[core], do_buf[slot, core]) * residual_scale
+            dms.append(grads)
+            at = pl.ds(pl.multiple_of(at_chip + core * CAP, 16), CAP)
+            for i in range(local):
+                part = slice(i * CAP, (i + 1) * CAP)
+                xs_ref[i, at] = taken[part]
+                dye_ref[i, at] = (gates[core][i] * grads[part]).astype(BF)
+        at = pl.ds(at_chip, pair)
+        mades, backs, marks = [], [], []
         for i in range(local):
-            rows = slice(i * CAP, (i + 1) * CAP)
-            xs_ref[i, s * CAP : (s + 1) * CAP] = taken[rows]
-            dye_ref[i, s * CAP : (s + 1) * CAP] = (gates[s][i] * grads[rows]).astype(BF)
-    mixed, back, marks = [], [], []
-    lane = lanes_of(CAP)
+            slots = xs_ref[i, at]
+            gate_pre = dot_nt(slots, w_ref[i, :FF])
+            up_pre = dot_nt(slots, w_ref[i, FF : 2 * FF])
+            grad_act = dot_nt(dye_ref[i, at], w_ref[i, 2 * FF :])
+            sigmoid = 1.0 / (1.0 + jnp.exp(-gate_pre))
+            silu = gate_pre * sigmoid
+            act = (silu * up_pre).astype(BF)
+            hx_ref[i, at] = act
+            grad_gate = (grad_act * up_pre * (sigmoid * (1.0 + gate_pre * (1.0 - sigmoid)))).astype(BF)
+            grad_up = (grad_act * silu).astype(BF)
+            dgu_ref[i, at, :FF] = grad_gate
+            dgu_ref[i, at, FF:] = grad_up
+            made = dot(act, w_ref[i, 2 * FF :]).astype(BF).astype(F32)
+            mades.append(made)
+            backs.append((dot(grad_gate, w_ref[i, :FF]) + dot(grad_up, w_ref[i, FF : 2 * FF])).astype(BF))
+            for core in range(2):
+                part = slice(core * CAP, (core + 1) * CAP)
+                value = jnp.sum(dms[core][i * CAP : (i + 1) * CAP] * made[part], axis=1, keepdims=True)
+                high = value.astype(BF).astype(F32)
+                expert = f * local + i
+                mark = jnp.where(lane == expert, high, jnp.where(lane == expert + E, value - high, 0.0))
+                marks.append(mark.astype(BF))
+        for core in range(2):
+            part = slice(core * CAP, (core + 1) * CAP)
+            sent = jnp.concatenate([backs[i][part] for i in range(local)], axis=0)
+            dxp_ref[slot, core, :, :D] = dot_tn(picks[core], sent).astype(BF)
+            sent = jnp.concatenate([marks[2 * i + core] for i in range(local)], axis=0)
+            dxp_ref[slot, core, :, D:] = dot_tn(picks[core], sent).astype(BF)
+        core_copy(zc, slot, t).start()
+        for core in range(2):
+            part = slice(core * CAP, (core + 1) * CAP)
+            sent = jnp.concatenate([(gates[core][i] * mades[i][part]).astype(BF) for i in range(local)], axis=0)
+            yps_ref[slot, core] = dot_tn(picks[core], sent).astype(BF)
+        yp_copy(zc, slot).start()
+        core_copy(zc, slot, t).wait_recv()
+        total = dxp_ref[slot, c].astype(F32) + core_ref[zc].astype(F32)
+
+        @pl.when(t == 0)
+        def _():
+            dx_ref[...] = total
+
+        @pl.when(t > 0)
+        def _():
+            dxp_ref[slot, c] = total.astype(BF)
+            far_copy(zc, slot, t).start()
+
+        return carry
+
+    lax.fori_loop(0, chips, chunk, 0)
     for i in range(local):
-        slots = xs_ref[i]
-        gate_pre = dot_nt(slots, w_ref[i, :FF])
-        up_pre = dot_nt(slots, w_ref[i, FF : 2 * FF])
-        sigmoid = 1.0 / (1.0 + jnp.exp(-gate_pre))
-        silu = gate_pre * sigmoid
-        act = (silu * up_pre).astype(BF)
-        hx_ref[i] = act
-        made = dot(act, w_ref[i, 2 * FF :]).astype(BF).astype(F32)
-        grad_act = dot_nt(dye_ref[i], w_ref[i, 2 * FF :])
-        dgu_ref[i, :, :FF] = (grad_act * up_pre * (sigmoid * (1.0 + gate_pre * (1.0 - sigmoid)))).astype(BF)
-        dgu_ref[i, :, FF:] = (grad_act * silu).astype(BF)
-        grad_rows = dot(dgu_ref[i, :, :FF], w_ref[i, :FF]) + dot(dgu_ref[i, :, FF:], w_ref[i, FF : 2 * FF])
-        back.append(grad_rows.astype(BF))
-        for s in range(sources):
-            rows = slice(s * CAP, (s + 1) * CAP)
-            mixed.append((gates[s][i] * made[rows]).astype(BF))
-            grad_gate = jnp.sum(dms[s][i * CAP : (i + 1) * CAP] * made[rows], axis=1, keepdims=True)
-            high = grad_gate.astype(BF).astype(F32)
-            expert = base_ref[0] + i
-            mark = jnp.where(lane == expert, high, jnp.where(lane == expert + E, grad_gate - high, 0.0))
-            marks.append(mark.astype(BF))
-    for s in range(sources):
-        at = slice(s * tokens, (s + 1) * tokens)
-        rows = slice(s * CAP, (s + 1) * CAP)
-        sent = jnp.concatenate([mixed[i * sources + s] for i in range(local)], axis=0)
-        yp_ref[at] = dot_tn(picks[s], sent).astype(BF)
-        sent = jnp.concatenate([back[i][rows] for i in range(local)], axis=0)
-        dx_ref[at, :D] = dot_tn(picks[s], sent).astype(BF)
-        sent = jnp.concatenate([marks[i * sources + s] for i in range(local)], axis=0)
-        dx_ref[at, D:] = dot_tn(picks[s], sent).astype(BF)
-
-
-def expert_weights_back(xs_ref, dye_ref, dgu_ref, hx_ref, out_ref):
-    out_ref[0, : 2 * FF] = dot_tn(dgu_ref[0], xs_ref[0]).astype(BF)
-    out_ref[0, 2 * FF :] = dot_tn(hx_ref[0], dye_ref[0]).astype(BF)
+        ge_ref[i, : 2 * FF] = dot_tn(dgu_ref[i], xs_ref[i]).astype(BF)
+        ge_ref[i, 2 * FF :] = dot_tn(hx_ref[i], dye_ref[i]).astype(BF)
+    for k in range(chips):
+
+        @pl.when(z != k)
+        def _():
+            make(from_ref.at[k], from_ref.at[k], far_send.at[k], far_recv.at[k], (r, k * 2 + c)).wait_recv()
+            dx_ref[...] += from_ref[k].astype(F32)
+
+    for t in range(max(chips - 2, 0), chips):
+        core_copy(z, t % 2, t).wait_send()
+        yp_copy(z, t % 2).wait()
+        if t > 0:
+            far_copy(z, t % 2, t).wait_send()
+    for k in range(chips):
+
+        @pl.when((z >= k) & (z < chips - 1))
+        def _():
+            for copy in pass_on(k, "up"):
+                copy.wait_send()
+
+        @pl.when((z <= k) & (z > 0))
+        def _():
+            for copy in pass_on(k, "down"):
+                copy.wait_send()
+
+        for copy in pass_on(k, "mate"):
+            copy.wait_send()
 
 
 def attention_backward(
-    x_ref, dout_ref, cos_ref, sin_ref, w_ref, q_ref, kd_ref, vd_ref, p_ref, o_ref, h1_ref, n2_ref, gd_ref, dx_ref,
-    gin_ref, gw_ref, do_ref, dqkv_ref,
+    x_ref, dout_ref, cos_ref, sin_ref, w_ref, q_ref, kd_ref, vd_ref, p_hbm, o_ref, h1_ref, n2_ref, gd_ref, dx_ref,
+    gin_ref, gw_ref, do_ref, dqkv_ref, p_ref, p_sem,
 ):
     tokens = x_ref.shape[0]
     lane = lanes_of(tokens)
     low = lane < HD
+
+    def p_copy(g):
+        return pltpu.make_async_copy(p_hbm.at[g], p_ref.at[g % 2], p_sem.at[g % 2])
+
+    p_copy(0).start()
 
     def put(at, value):
         gw_ref[:, :, :, at] = value.astype(BF).reshape(*gw_ref.shape[:3], value.shape[1])
@@ -230,7 +395,10 @@
         at = slice(g * LANE, (g + 1) * LANE)
         queries = halves(q_ref[:, at].astype(F32), low).astype(BF)
         outs = halves(do_ref[:, at].astype(F32), low).astype(BF)
-        weights = p_ref[g]
+        if g + 1 < KVH:
+            p_copy(g + 1).start()
+        p_copy(g).wait()
+        weights = p_ref[g % 2]
         grad_weights = dot_nt(outs, vd_ref[:, at])
         total = jnp.sum(weights * grad_weights, axis=1, keepdims=True)
         grad_scores = (weights * (grad_weights - total)).astype(BF)
@@ -284,9 +452,9 @@
 
 def tail(
     replicas, chips,
-    x_ref, dout_ref, cos_ref, sin_ref, w_ref, q_ref, kd_ref, vd_ref, p_ref, o_ref, h1_ref, n2_ref, gd_ref, dx_ref, ge_ref,
+    x_ref, dout_ref, cos_ref, sin_ref, w_ref, q_ref, kd_ref, vd_ref, o_ref, h1_ref, n2_ref, gd_ref, dx_ref, ge_ref, p_hbm,
     gin_ref, gexp_ref, gproj_ref,
-    do_ref, dqkv_ref, gw_ref, core_ref, up_ref, down_ref, parts_ref, smalls_ref, result_ref, *rest,
+    p_ref, p_sem, do_ref, dqkv_ref, gw_ref, core_ref, up_ref, down_ref, parts_ref, smalls_ref, result_ref, *rest,
 ):
     bits = replicas.bit_length() - 1
     jobs = ge_ref.shape[0] * bits
@@ -516,8 +684,8 @@
     if not bits:
         gexp_ref[...] = ge_ref[...]
     attention_backward(
-        x_ref, dout_ref, cos_ref, sin_ref, w_ref, q_ref, kd_ref, vd_ref, p_ref, o_ref, h1_ref, n2_ref, gd_ref, dx_ref,
-        gin_ref, gw_ref, do_ref, dqkv_ref,
+        x_ref, dout_ref, cos_ref, sin_ref, w_ref, q_ref, kd_ref, vd_ref, p_hbm, o_ref, h1_ref, n2_ref, gd_ref, dx_ref,
+        gin_ref, gw_ref, do_ref, dqkv_ref, p_ref, p_sem,
     )
     projections = line()
     first, last = experts_sums[:1], experts_sums[1:]
@@ -529,12 +697,13 @@
             next(process, None)
 
 
-def call(kernel, out_shape, args, scratch=(), **params):
-    smem = [a.dtype == jnp.int32 and a.size <= 16 for a in args]
+def call(kernel, out_shape, args, scratch=(), outside=0, **params):
+    spaces = [pltpu.SMEM if a.dtype == jnp.int32 and a.size <= 16 else pltpu.VMEM for a in args]
+    spaces[len(args) - outside :] = [pl.ANY] * outside
     return pl.pallas_call(
         kernel,
         out_shape=out_shape,
-        in_specs=[pl.BlockSpec(memory_space=pltpu.SMEM if s else pltpu.VMEM) for s in smem],
+        in_specs=[pl.BlockSpec(memory_space=space) for space in spaces],
         out_specs=jax.tree.map(lambda _: pl.BlockSpec(memory_space=pltpu.VMEM), out_shape),
         scratch_shapes=list(scratch),
         compiler_params=pltpu.CompilerParams(
@@ -562,7 +731,6 @@
 def make_body(mesh):
     group, replicas = mesh.shape["fsdp"], mesh.shape["replica"]
     local = E // group
-    chunk = 2
 
     def body(
         hidden_in, seq_lengths, routes, norm1_gain, w_query, w_key, w_value, w_output, norm2_gain, w_router,
@@ -589,53 +757,40 @@
             ),
             (hidden_in, seq_lengths, routes, cosines, sines, weights),
         )
-        n2_all = lax.all_gather(n2, "fsdp", axis=0, tiled=True)
-        gt_all = lax.all_gather(gt, "fsdp", axis=0, tiled=False)
-        base = (lax.axis_index("fsdp") * local).astype(jnp.int32).reshape(1)
-        whole = pl.Buffered(1)
-        token_block = pl.BlockSpec((chunk * tokens, D), lambda c: (c, 0))
-        slot_block = pl.BlockSpec((local, chunk * CAP, D), lambda c: (0, c, 0))
-        yp, dxp, xs, dye, dgu, hx = pl.pallas_call(
-            experts,
-            grid=(group // chunk,),
-            in_specs=[
-                pl.BlockSpec(memory_space=pltpu.SMEM), token_block, token_block,
-                pl.BlockSpec((chunk, E, tokens), lambda c: (c, 0, 0)),
-                pl.BlockSpec((local, 3 * FF, D), lambda c: (0, 0, 0), pipeline_mode=whole),
+        chips = group // 2
+        dma = pltpu.SemaphoreType.DMA
+        anywhere = pl.BlockSpec(memory_space=pl.ANY)
+        inside = pl.BlockSpec(memory_space=pltpu.VMEM)
+        wide = D + LANE
+        dx, yp, grad_experts = pl.pallas_call(
+            functools.partial(middle, chips),
+            in_specs=[inside, inside, anywhere, anywhere],
+            out_specs=[inside, anywhere, inside],
+            out_shape=[
+                shape((tokens, wide), F32), shape((chips, 2, tokens, D), BF), shape((local, 3 * FF, D), BF),
             ],
-            out_specs=[
-                token_block, pl.BlockSpec((chunk * tokens, D + LANE), lambda c: (c, 0)),
-                slot_block, slot_block, slot_block,
-                pl.BlockSpec((local, chunk * CAP, FF), lambda c: (0, c, 0)),
-            ],
-            out_shape=[
-                shape((group * tokens, D), BF), shape((group * tokens, D + LANE), BF),
-                shape((local, group * CAP, D), BF), shape((local, group * CAP, D), BF),
-                shape((local, group * CAP, D), BF), shape((local, group * CAP, FF), BF),
-            ],
-            compiler_params=pltpu.CompilerParams(vmem_limit_bytes=VMEM_LIMIT),
-        )(base, n2_all, dout_all, gt_all, expert_weights)
-        dx = lax.psum_scatter(dxp, "fsdp", scatter_dimension=0, tiled=True)
-        wide = pl.BlockSpec((1, group * CAP, D), lambda i: (i, 0, 0))
-        grad_experts = pl.pallas_call(
-            expert_weights_back,
-            grid=(local,),
-            in_specs=[wide, wide, wide, pl.BlockSpec((1, group * CAP, FF), lambda i: (i, 0, 0))],
-            out_specs=pl.BlockSpec((1, 3 * FF, D), lambda i: (i, 0, 0)),
-            out_shape=shape((local, 3 * FF, D), BF),
-            compiler_params=pltpu.CompilerParams(vmem_limit_bytes=VMEM_LIMIT),
-        )(xs, dye, dgu, hx)
-        moe = lax.psum_scatter(yp, "fsdp", scatter_dimension=0, tiled=True)
+            scratch_shapes=[
+                pltpu.VMEM((chips, 2, tokens, D), BF), pltpu.VMEM((chips, 2, E, tokens), F32),
+                pltpu.VMEM((2, 2, tokens, D), BF), pltpu.VMEM((local, 3 * FF, D), BF),
+                pltpu.VMEM((local, group * CAP, D), BF), pltpu.VMEM((local, group * CAP, D), BF),
+                pltpu.VMEM((local, group * CAP, D), BF), pltpu.VMEM((local, group * CAP, FF), BF),
+                pltpu.VMEM((2, 2, tokens, wide), BF), pltpu.VMEM((2, 2, tokens, D), BF),
+                pltpu.VMEM((chips, tokens, wide), BF), pltpu.VMEM((chips, tokens, wide), BF),
+            ]
+            + ([dma((chips,))] * 3 + [dma((chips, 2))]) * 2 + [dma((chips,))] * 4 + [dma((2,)), dma((2,)), dma((1,))],
+            compiler_params=pltpu.CompilerParams(vmem_limit_bytes=VMEM_LIMIT, has_side_effects=True, collective_id=1),
+        )(n2, gt, dout_all.reshape(chips, 2, tokens, D), expert_weights)
+        moe = lax.psum_scatter(yp.reshape(group * tokens, D), "fsdp", scatter_dimension=0, tiled=True)
         layer_out = (h1 + residual_scale * moe.astype(F32)).astype(BF)
         bits = replicas.bit_length() - 1
         rows = D // group
         size = 3 * FF // bits if bits else 0
-        dma = pltpu.SemaphoreType.DMA
         grad_in, grad_experts, gw = call(
             functools.partial(tail, replicas, group // 2),
             (shape((tokens, D), F32), shape((local, 3 * FF, D), BF), shape((rows, QKVO + LANE), F32)),
-            (hidden_in, out_cotangent, cosines, sines, weights, q, kd, vd, p, o, h1, n2, gd, dx, grad_experts),
+            (hidden_in, out_cotangent, cosines, sines, weights, q, kd, vd, o, h1, n2, gd, dx, grad_experts, p),
             [
+                pltpu.VMEM((2, 2 * tokens, tokens), F32), dma((2,)),
                 pltpu.VMEM((tokens, D), BF), pltpu.VMEM((tokens, QKVO - D), BF),
                 pltpu.VMEM((group // 2, 2, rows, QKVO + LANE), BF), pltpu.VMEM((group // 2, rows, QKVO + LANE), BF),
                 pltpu.VMEM((group // 2, rows, QKVO + LANE), BF), pltpu.VMEM((group // 2, rows, QKVO + LANE), BF),
@@ -646,6 +801,7 @@
             + [pltpu.VMEM((local * bits, size >> (k + 1), D), BF) for k in range(bits - 1)]
             + [dma((max(local * bits, 1), max(2 * bits, 1)))] * 2 + [dma((1,))] * 2 + [dma((group // 2,))] * 4
             + [dma((replicas,))] * 6,
+            outside=1,
             collective_id=0,
         )
         a, b, c = H * HD, H * HD + KVH * HD, H * HD + 2 * KVH * HD

time: 487 us -> 420 us (0.86)
  waiting for transfers between devices: 219 us -> 99.5 us
  Pallas kernels: 208 us -> 282 us
  blocking collectives: 15.8 us -> 0 us
    reduce_scatter x2 -> x1, waiting for transfers between devices: 86.4 us -> 0.01 us  [body(): lax.psum_scatter(yp.reshape(group * tokens, D), 'fsdp', scatter_dimension...]
    all_gather x1 -> x0, waiting for transfers between devices: 47.4 us -> none  [body(): n2_all = lax.all_gather(n2, 'fsdp', axis=0, tiled=True)]
    pallas_call x2 -> x1, Pallas kernels: 46.6 us -> 88.6 us  [body(): pl.pallas_call(functools.partial(middle, chips), in_specs=[inside, inside...]
    pallas_call x2, Pallas kernels: 161 us -> 193 us  [call(): pl.pallas_call(kernel, out_shape=out_shape, in_specs=[pl.BlockSpec(memory...]
    all_gather x1 -> x0, blocking collectives: 15.8 us -> none  [body(): gt_all = lax.all_gather(gt, 'fsdp', axis=0, tiled=False)]
    all_gather x1, waiting for transfers between devices: 22.5 us -> 37.3 us  [body(): dout_all = lax.all_gather(out_cotangent, 'fsdp', axis=0, tiled=True)]
  transfers between devices with their start and end apart: 5 -> 3, of which waited for: 5 -> 2; matrix products, arithmetic and copies ran while one was open for 1% -> 4% of each run, Pallas kernels for 5% -> 46%
where the time goes in v3:
time: 420 us
  Pallas kernels  282 us (67%)
  waiting for transfers between devices  99.5 us (24%)
  between operations  13.8 us (3%)
  other arithmetic  13.5 us (3%)
  local copies, waits for them, and re-layouts  11.1 us (3%)
    pallas_call x2, Pallas kernels, call(): pl.pallas_call(kernel, out_shape=out_shape, in_specs=[pl.BlockSpec(memory...  193 us
    pallas_call x1, Pallas kernels, body(): pl.pallas_call(functools.partial(middle, chips), in_specs=[inside, inside...  88.6 us
    all_gather x1, waiting for transfers between devices, body(): weights = lax.all_gather(packed, 'fsdp', axis=0, tiled=True)  61.4 us
    all_gather x1, waiting for transfers between devices, body(): dout_all = lax.all_gather(out_cotangent, 'fsdp', axis=0, tiled=True)  37.3 us
    convert_element_type x1, other arithmetic, body(): grad_experts.astype(F32)  9.26 us
  transfers between devices with their start and end apart: 3, of which 2 were waited for; matrix products, arithmetic and copies ran while one was open for 4% of the time, Pallas kernels for 46%

profile of v3, /device:TPU:10, one launch (start us, length us, event | category | flops | bytes accessed | tf_op | source)
XLA Modules:
  0.0 419.5 jit_solution(1813246129573477503)
XLA Ops:
  7.2 0.0 all-gather.3.cloned.1.call-start
  7.2 0.8 copy.33
  8.0 0.8 copy.34
  8.8 0.8 copy.35
  9.6 2.1 concatenate.7
  11.7 0.0 all-gather.3.cloned.1.call-update
  11.7 0.0 all-gather.5.cloned.1.call-start
  11.8 0.7 all-gather.5.cloned.1.call-update
  12.5 0.0 reduce-scatter.2.cloned.1.call-start
  12.5 1.5 copy.36.routes_ref
  14.0 0.1 compare_select_fusion
  14.1 0.8 select_reduce_fusion.1
  14.9 0.1 select_reduce_fusion
  15.0 1.2 fusion
  16.2 61.4 %all-gather.3.cloned.1.call-done.w_ref = bf16[1024,3200]{1,0:T(8,128)(2,1)} async-done(((bf16[128,3200]{1,0:T(8,128)(2,1)}), bf16[1024,3200]{1,0:T(8,128)(2,1)}) %all-gather.3.cloned.1.call-update) | async-done | bytes 6553616 | tf_op jit(solution)/shard_map/all_gather | solution.py:748
  77.6 10.8 %shard_map.204 = (bf16[256,1024]{1,0:T(8,128)(2,1)}, bf16[256,1024]{1,0:T(8,128)(2,1)}, bf16[256,1024]{1,0:T(8,128)(2,1)}, f32[8,512,256]{2,1,0:T(8,128)}, bf16[...) custom-call(bf16[256,1024]{1,0:T(8,128)(2,1)} %x_ref.3, ...), custom_call_target="tpu_custom_call" | custom-call | tf_op jit(solution)/shard_map/pallas_call | solution.py:703
  88.5 37.3 %all-gather.5.cloned.1.call-done = bf16[2048,1024]{1,0:T(8,128)(2,1)} async-done(((bf16[256,1024]{1,0:T(8,128)(2,1)}), bf16[2048,1024]{1,0:T(8,128)(2,1)}) %all-gather.5.cloned.1.call-update) | async-done | bytes 4194320 | tf_op jit(solution)/shard_map/all_gather | solution.py:749
  125.8 88.6 %shard_map.205 = (f32[256,1152]{1,0:T(8,128)}, bf16[4,2,256,1024]{3,2,1,0:T(8,128)(2,1)}, bf16[2,1536,1024]{2,1,0:T(8,128)(2,1)}) custom-call(bf16[256,1024]{1,0:T(8,128)(2,1)} %get-tuple-element.26.n2_ref, f32[16,256]{1,0:T(8,128)} %get-tuple-element.27.gt_ref, bf16[4,2,256,1024]{3,2,1,0:T(8,128)(2,1)} %bitcast.5, bf16[2,1536,1024]{2,1,0:T(8,128)(2,1)} %w_hbm.1), custom_call_target="tpu_custom_call" | custom-call | tf_op jit(solution)/shard_map/pallas_call | solution.py:765
  214.4 0.0 reduce-scatter.2.cloned.1.call-update
  214.4 182.2 %shard_map.206 = (f32[256,1024]{1,0:T(8,128)}, bf16[2,1536,1024]{2,1,0:T(8,128)(2,1)}, f32[128,3200]{1,0:T(8,128)}) custom-call(bf16[256,1024]{1,0:T(8,128)(2,1)} %x_ref.3, bf16[256,1024]{1,0:T(8,128)(2,1)} %dout_ref.1, f32[256,128]{1,0:T(8,128)} %get-tuple-element.77.cos_ref, f32[256,128]{1,0:T(8,128)} %get-tuple-element.76.sin_ref, ...), custom_call_target="tpu_custom_call" | custom-call | tf_op jit(solution)/shard_map/pallas_call | solution.py:703
  396.6 0.8 slice.27
  397.4 0.7 copy.37
  398.1 0.0 copy-start.1
  398.1 9.3 %convert_element_type.19 = f32[2,1536,1024]{2,1,0:T(8,128)} convert(bf16[2,1536,1024]{2,1,0:T(8,128)(2,1)} %get-tuple-element.39) | non-fusion elementwise | flops 3145728 | bytes 18874368 | tf_op jit(solution)/shard_map/convert_element_type | solution.py:810
  407.4 0.0 copy-done.1
  407.4 0.7 slice_reduce_fusion
  408.1 0.9 fusion.2
  408.9 1.1 fusion.1
  410.0 0.0 copy-done
  410.0 2.0 add_convert_fusion
  412.0 0.0 copy-done.2
  412.0 1.0 copy.39
  (6 shorter events, 0.0 us)
Async XLA Ops:
  7.2 70.5 %all-gather.3.cloned.1.call-start = ((), (), s32[]{:S(2)}) async-start(), calls=%async_computation.1 | async-start | bytes 7372800 | tf_op jit(solution)/shard_map/all_gather | solution.py:748
  11.7 114.1 %all-gather.5.cloned.1.call-start = ((), (), s32[]{:S(2)}) async-start(), calls=%async_computation.2 | async-start | bytes 4718592 | tf_op jit(solution)/shard_map/all_gather | solution.py:749
  12.5 397.6 %reduce-scatter.2.cloned.1.call-start = ((), (), s32[]{:S(2)}) async-start(), calls=%async_computation.3 | async-start | bytes 4718592 | tf_op jit(solution)/shard_map/reduce_scatter | solution.py:783
  398.1 9.3 %copy-start.1 = (f32[128,3200]{1,0:T(8,128)S(1)}, f32[128,3200]{1,0:T(8,128)}, u32[]{:S(2)}) copy-start(f32[128,3200]{1,0:T(8,128)} %get-tuple-element.38) | copy-start | bytes 4915204
  398.1 11.9 %copy-start = (f32[256,1024]{1,0:T(8,128)S(1)}, f32[256,1024]{1,0:T(8,128)}, u32[]{:S(2)}) copy-start(f32[256,1024]{1,0:T(8,128)} %get-tuple-element.25.h1_ref) | copy-start | bytes 3145732
  407.4 4.7 %copy-start.2 = (f32[256,1024]{1,0:T(8,128)S(1)}, f32[256,1024]{1,0:T(8,128)}, u32[]{:S(2)}) copy-start(f32[256,1024]{1,0:T(8,128)} %get-tuple-element.91) | copy-start | bytes 3145732
Sparse Core Ops, SparseCore 0:
  11.8 65.7 all-gather.2
  79.2 46.5 all-gather.4
  214.5 62.5 reduce-scatter.1

commit v4 on v3

--- a/solution.py
+++ b/solution.py
@@ -17,7 +17,9 @@
 E = 16
 CAP = 144
 LANE = 128
-QKVO = H * HD + 2 * KVH * HD + D
+QKV = H * HD + 2 * KVH * HD
+QKVO = QKV + D
+W_O = QKV + LANE
 
 norm_eps = 1e-06
 score_scale = 0.015625
@@ -55,75 +57,274 @@
     return jnp.concatenate([jnp.where(low, block, zero), jnp.where(low, zero, block)], axis=0)
 
 
-def attention_forward(
-    x_ref, len_ref, routes_ref, cos_ref, sin_ref, w_ref,
-    q_ref, kd_ref, vd_ref, p_ref, o_ref, h1_ref, n2_ref, gd_ref, gt_ref,
+def rope_table(tokens):
+    frequency = np.float32(rope_base) ** (-np.arange(0, HD, 2, dtype=np.float32) / np.float32(HD))
+    frequency = np.tile(frequency.astype(np.float32), LANE // (HD // 2))
+    angles = (np.arange(tokens, dtype=np.float32)[:, None] * frequency[None, :]).astype(np.float64)
+    sign = np.where(np.arange(LANE) % HD < HD // 2, -1.0, 1.0)
+    pieces = []
+    for values in (np.cos(angles), np.sin(angles) * sign[None, :]):
+        rest = values.astype(np.float32)
+        for _ in range(3):
+            piece = rest.astype(BF)
+            pieces.append(piece)
+            rest = rest - piece.astype(np.float32)
+    return np.concatenate(pieces, axis=1)
+
+
+class Copies:
+    def make(self, src, dst, send, recv, device):
+        return pltpu.make_async_remote_copy(
+            src_ref=src, dst_ref=dst, send_sem=send, recv_sem=recv, device_id=device, device_id_type=pl.DeviceIdType.MESH
+        )
+
+
+def meet(devices, expected):
+    barrier = pltpu.get_barrier_semaphore()
+    for condition, device in devices:
+
+        def signal(device=device):
+            pl.semaphore_signal(barrier, inc=1, device_id=device, device_id_type=pl.DeviceIdType.MESH)
+
+        if condition is True:
+            signal()
+        else:
+            pl.when(condition)(signal)
+    pl.semaphore_wait(barrier, expected)
+
+
+def front(
+    replicas, chips,
+    x_ref, len_ref, routes_ref, table_ref, wq_ref, wk_ref, wv_ref, wo_ref, wr_ref, g1_ref, g2_ref, dout_ref,
+    w_all, q_ref, kd_ref, vd_ref, o_ref, h1_ref, n2_ref, gd_ref, gt_ref, cos_ref, sin_ref, p_hbm, do_all,
+    p_ref, p_sem, own_sem, z_up, z_down, z_recv, xy_send, xy_recv, mate_send, mate_recv, do_send, do_recv,
 ):
     tokens = x_ref.shape[0]
-    lane = lanes_of(tokens)
-    low = lane < HD
-    small = w_ref[:, QKVO:].astype(F32).T
-    gain_one, gain_two = small[E : E + 1], small[E + 1 : E + 2]
+    r, f = lax.axis_index("replica"), lax.axis_index("fsdp")
+    z, c = f // 2, f % 2
+    mate, above, below = (r, z * 2 + 1 - c), (r, f + 2), (r, f - 2)
+    make = Copies().make
+    peers = [(True, mate), (z > 0, below), (z < chips - 1, above)]
+    peers += [(True, ((r + d) % replicas, f)) for d in range(1, replicas)]
+
+    own_dout = pltpu.make_async_copy(dout_ref, do_all.at[z, c], own_sem.at[0])
+    own_dout.start()
+    rows = wq_ref.shape[0]
+    packed = [wr_ref[...].astype(F32), g1_ref[...].astype(F32), g2_ref[...].astype(F32)]
+    packed = jnp.concatenate(packed + [jnp.zeros((LANE - E - 2, rows), F32)], axis=0)
+    own = w_all.at[z, c]
+    own[:, : H * HD] = wq_ref[...]
+    own[:, H * HD : H * HD + KVH * HD] = wk_ref[...]
+    own[:, H * HD + KVH * HD : QKV] = wv_ref[...]
+    own[:, QKV:W_O] = packed.T.astype(BF)
+    own[:, W_O:] = wo_ref[...]
+    meet(peers, 1 + (replicas - 1) + jnp.where(z > 0, 1, 0) + jnp.where(z < chips - 1, 1, 0))
+
+    def part(kind):
+        if kind == 0:
+            return pl.ds(pl.multiple_of(r * (QKV // replicas), LANE), QKV // replicas)
+        if kind == 1:
+            return pl.ds(QKV, LANE)
+        return pl.ds(pl.multiple_of(W_O + r * (D // replicas), LANE), D // replicas)
+
+    def along(zb, kind, up):
+        ref = w_all.at[zb, c, :, part(kind)]
+        return make(ref, ref, (z_up if up else z_down).at[kind, zb], z_recv.at[kind, zb], above if up else below)
+
+    def across(zb, kind, d):
+        ref = w_all.at[zb, c, :, part(kind)]
+        return make(ref, ref, xy_send.at[kind, zb, d], xy_recv.at[kind, zb, r], ((r + d) % replicas, f))
+
+    def wait_across(zb, kind):
+        for d in range(1, replicas):
+            peer = (r + d) % replicas
+            ref = w_all.at[zb, c, :, part(kind)]
+            make(ref, ref, xy_send.at[kind, zb, d], xy_recv.at[kind, zb, peer], (peer, f)).wait_recv()
+
+    def to_mate(zb, core, late):
+        ref = w_all.at[zb, core, :, pl.ds(W_O, D) if late else pl.ds(0, W_O)]
+        return make(ref, ref, mate_send.at[late, zb], mate_recv.at[late, zb], mate)
+
+    def dout_copy(zb, core, way):
+        source = do_all.at[zb, core]
+        return make(source, do_all.at[zb, core], do_send.at[way, zb], do_recv.at[zb, core], (above, below, mate)[way])
+
+    def both_sides(k, act):
+        @pl.when(z >= k)
+        def _():
+            act(z - k, True)
+
+        @pl.when(z < chips - k)
+        def _():
+            act(z + k, False)
+
+    def onward(up):
+        return z < chips - 1 if up else z > 0
+
+    for kind in range(3):
+        both_sides(1, lambda zb, low: along(z, kind, not low).start())
+    for late in range(2):
+        to_mate(z, c, late).start()
+
     source = x_ref[...].astype(F32)
     factor = lax.rsqrt(jnp.mean(source * source, axis=1, keepdims=True) + norm_eps)
-    normed = (source * factor * gain_one).astype(BF)
-    cosines, sines = cos_ref[...], sin_ref[...]
-    q_all = dot(normed, w_ref[:, : H * HD])
-    for g in range(H // 2):
-        at = slice(g * LANE, (g + 1) * LANE)
-        block = q_all[:, at]
-        q_ref[:, at] = (block * cosines + turned(block, lane) * sines).astype(BF)
-    kv = dot(normed, w_ref[:, H * HD : H * HD + 2 * KVH * HD])
-    for m in range(KVH // 2):
-        block = kv[:, m * LANE : (m + 1) * LANE]
-        block = block * cosines + turned(block, lane) * sines
-        other = pltpu.roll(block, HD, 1)
-        kd_ref[:, 2 * m * LANE : (2 * m + 1) * LANE] = jnp.where(low, block, other).astype(BF)
-        kd_ref[:, (2 * m + 1) * LANE : (2 * m + 2) * LANE] = jnp.where(low, other, block).astype(BF)
-        block = kv[:, KVH * HD + m * LANE : KVH * HD + (m + 1) * LANE]
-        other = pltpu.roll(block, HD, 1)
-        vd_ref[:, 2 * m * LANE : (2 * m + 1) * LANE] = jnp.where(low, block, other).astype(BF)
-        vd_ref[:, (2 * m + 1) * LANE : (2 * m + 2) * LANE] = jnp.where(low, other, block).astype(BF)
-
+    lane = lanes_of(tokens)
+    low_lane = lane < HD
     row = lax.broadcasted_iota(jnp.int32, (tokens, tokens), 0)
     column = lax.broadcasted_iota(jnp.int32, (tokens, tokens), 1)
     row_at = lax.broadcasted_iota(jnp.int32, (tokens, 1), 0)
     column_at = lax.broadcasted_iota(jnp.int32, (1, tokens), 1)
     row_segment = jnp.zeros((tokens, 1), jnp.int32)
+    row_start = jnp.zeros((tokens, 1), jnp.int32)
     column_segment = jnp.zeros((1, tokens), jnp.int32)
     end = jnp.int32(0)
     for j in range(len_ref.shape[1]):
         end = end + len_ref[0, j]
         row_segment += (row_at >= end).astype(jnp.int32)
+        row_start = jnp.maximum(row_start, jnp.where(row_at >= end, end, 0))
         column_segment += (column_at >= end).astype(jnp.int32)
+    place = (column == row - row_start).astype(F32).astype(BF)
+    found = dot(place, table_ref[...])
+    found = [found[:, i * LANE : (i + 1) * LANE] for i in range(6)]
+    cosines, sines = found[0] + found[1] + found[2], found[3] + found[4] + found[5]
+    cos_ref[...] = cosines
+    sin_ref[...] = sines
+
+    own_dout.wait()
+    for k in range(1, chips):
+        for kind in range(3):
+
+            def arrive(zb, low, kind=kind):
+                along(zb, kind, low).wait_recv()
+
+                @pl.when(onward(low))
+                def _():
+                    along(zb, kind, low).start()
+
+                if kind != 1:
+                    for d in range(1, replicas):
+                        across(zb, kind, d).start()
+
+            both_sides(k, arrive)
+        if k == 1:
+            both_sides(1, lambda zb, low: dout_copy(z, c, 1 if low else 0).start())
+            dout_copy(z, c, 2).start()
+
+    def share(k, late):
+        def act(zb, low):
+            wait_across(zb, 2 if late else 0)
+            to_mate(zb, c, late).start()
+
+        both_sides(k, act)
+
+    for k in range(1, chips):
+        share(k, 0)
+    for k in range(chips):
+        to_mate(k, 1 - c, 0).wait_recv()
+
+    def columns(start, size):
+        return w_all[:, :, :, start : start + size].reshape(D, size)
+
+    small = columns(QKV, LANE)
+    gains = small.astype(F32).T
+    gain_one, gain_two = gains[E : E + 1], gains[E + 1 : E + 2]
+    normed = (source * factor * gain_one).astype(BF)
+    q_all = dot(normed, columns(0, H * HD))
+    for g in range(H // 2):
+        at = slice(g * LANE, (g + 1) * LANE)
+        block = q_all[:, at]
+        q_ref[:, at] = (block * cosines + turned(block, lane) * sines).astype(BF)
+    kv = dot(normed, columns(H * HD, 2 * KVH * HD))
+    for m in range(KVH // 2):
+        block = kv[:, m * LANE : (m + 1) * LANE]
+        block = block * cosines + turned(block, lane) * sines
+        other = pltpu.roll(block, HD, 1)
+        kd_ref[:, 2 * m * LANE : (2 * m + 1) * LANE] = jnp.where(low_lane, block, other).astype(BF)
+        kd_ref[:, (2 * m + 1) * LANE : (2 * m + 2) * LANE] = jnp.where(low_lane, other, block).astype(BF)
+        block = kv[:, KVH * HD + m * LANE : KVH * HD + (m + 1) * LANE]
+        other = pltpu.roll(block, HD, 1)
+        vd_ref[:, 2 * m * LANE : (2 * m + 1) * LANE] = jnp.where(low_lane, block, other).astype(BF)
+        vd_ref[:, (2 * m + 1) * LANE : (2 * m + 2) * LANE] = jnp.where(low_lane, other, block).astype(BF)
     bias = jnp.where((row_segment == column_segment) & (column <= row), 0.0, masked_score)
     bias = jnp.concatenate([bias, bias], axis=0)
 
+    def p_copy(g):
+        return pltpu.make_async_copy(p_ref.at[g % 2], p_hbm.at[g], p_sem.at[g % 2])
+
     for g in range(KVH):
         at = slice(g * LANE, (g + 1) * LANE)
-        queries = halves(q_ref[:, at].astype(F32), low).astype(BF)
+        queries = halves(q_ref[:, at].astype(F32), low_lane).astype(BF)
         scores = dot_nt(queries, kd_ref[:, at]) * score_scale + bias
         shifted = jnp.exp(scores - jnp.max(scores, axis=1, keepdims=True))
         weights = shifted * (1.0 / jnp.sum(shifted, axis=1, keepdims=True))
-        p_ref[g] = weights
+        if g >= 2:
+            p_copy(g - 2).wait()
+        p_ref[g % 2] = weights
+        p_copy(g).start()
         mixed = dot(weights.astype(BF), vd_ref[:, at])
-        o_ref[:, at] = jnp.where(low, mixed[:tokens], mixed[tokens:]).astype(BF)
-
-    after = source + residual_scale * dot(o_ref[...], w_ref[:, QKVO - D : QKVO])
+        o_ref[:, at] = jnp.where(low_lane, mixed[:tokens], mixed[tokens:]).astype(BF)
+
+    for k in range(1, chips):
+        share(k, 1)
+
+    def dout_arrive(zb, low):
+        dout_copy(zb, c, 0 if low else 1).wait_recv()
+
+        @pl.when(onward(low))
+        def _():
+            dout_copy(zb, c, 0 if low else 1).start()
+
+        dout_copy(zb, c, 2).start()
+
+    if chips > 1:
+        both_sides(1, dout_arrive)
+    for k in range(chips):
+        to_mate(k, 1 - c, 1).wait_recv()
+    after = source + residual_scale * dot(o_ref[...], columns(W_O, D))
     h1_ref[...] = after
     factor = lax.rsqrt(jnp.mean(after * after, axis=1, keepdims=True) + norm_eps)
     normed = (after * factor * gain_two).astype(BF)
     n2_ref[...] = normed
-    logits = dot(normed, w_ref[:, QKVO:])
-    routed = jnp.zeros((tokens, LANE), jnp.bool_)
-    for j in range(TOPK):
-        routed |= routes_ref[:, j : j + 1] == lane
-    top = jnp.max(jnp.where(routed, logits, masked_score), axis=1, keepdims=True)
+    logits = dot(normed, small).T[:E]
+    expert = lax.broadcasted_iota(jnp.int32, (E, tokens), 0)
+    routed = routes_ref[0:1] == expert
+    for j in range(1, TOPK):
+        routed |= routes_ref[j : j + 1] == expert
+    top = jnp.max(jnp.where(routed, logits, masked_score), axis=0, keepdims=True)
     powers = jnp.where(routed, jnp.exp(logits - top), 0.0)
-    gates = powers / jnp.sum(powers, axis=1, keepdims=True)
+    gates = powers / jnp.sum(powers, axis=0, keepdims=True)
     gates = jnp.where(routed, gates, -1.0)
-    gd_ref[...] = gates
-    gt_ref[...] = gates.T[:E]
+    gt_ref[...] = gates
+    gd_ref[...] = jnp.concatenate([gates, jnp.full((LANE - E, tokens), -1.0, F32)], axis=0).T
+
+    for k in range(2, chips):
+        both_sides(k, dout_arrive)
+    for k in range(chips):
+        dout_copy(k, 1 - c, 2).wait_recv()
+    for g in (KVH - 2, KVH - 1):
+        p_copy(g).wait()
+    for k in range(chips):
+        for late in range(2):
+            to_mate(k, c, late).wait_send()
+        dout_copy(k, c, 2).wait_send()
+
+        @pl.when((z >= k) & (z < chips - 1))
+        def _():
+            dout_copy(k, c, 0).wait_send()
+            for kind in range(3):
+                along(k, kind, True).wait_send()
+
+        @pl.when((z <= k) & (z > 0))
+        def _():
+            dout_copy(k, c, 1).wait_send()
+            for kind in range(3):
+                along(k, kind, False).wait_send()
+
+        @pl.when(z != k)
+        def _():
+            for d in range(1, replicas):
+                for kind in (0, 2):
+                    across(k, kind, d).wait_send()
 
 
 def middle(
@@ -369,7 +570,7 @@
     def put(at, value):
         gw_ref[:, :, :, at] = value.astype(BF).reshape(*gw_ref.shape[:3], value.shape[1])
 
-    small = w_ref[:, QKVO:].astype(F32).T
+    small = w_ref[:, QKV:W_O].astype(F32).T
     gain_one, gain_two = small[E : E + 1], small[E + 1 : E + 2]
     after = h1_ref[...]
     factor_two = lax.rsqrt(jnp.mean(after * after, axis=1, keepdims=True) + norm_eps)
@@ -378,7 +579,7 @@
     grad_gates = jnp.where(lane < E, tail + pltpu.roll(tail, LANE - E, 1), 0.0)
     chosen = gates * (grad_gates - jnp.sum(gates * grad_gates, axis=1, keepdims=True))
     grad_logits = chosen.astype(BF)
-    grad_normed = dx_ref[:, :D].astype(F32) + dot_nt(grad_logits, w_ref[:, QKVO:])
+    grad_normed = dx_ref[:, :D].astype(F32) + dot_nt(grad_logits, w_ref[:, QKV:W_O])
     scaled = grad_normed * gain_two
     grad_after = dout_ref[...].astype(F32) + (
         factor_two * scaled - after * factor_two**3 * jnp.mean(scaled * after, axis=1, keepdims=True)
@@ -386,7 +587,7 @@
     grad_gain_two = jnp.sum(grad_normed * after * factor_two, axis=0, keepdims=True)
     grad_branch = (residual_scale * grad_after).astype(BF)
     put(slice(QKVO - D, QKVO), dot_tn(o_ref[...], grad_branch))
-    do_ref[...] = dot_nt(grad_branch, w_ref[:, QKVO - D : QKVO]).astype(BF)
+    do_ref[...] = dot_nt(grad_branch, w_ref[:, W_O:]).astype(BF)
     grad_router = dot_tn(n2_ref[...], grad_logits)
 
     cosines, sines = cos_ref[...], sin_ref[...]
@@ -420,7 +621,7 @@
     factor_one = lax.rsqrt(jnp.mean(source * source, axis=1, keepdims=True) + norm_eps)
     normed = (source * factor_one * gain_one).astype(BF)
     put(slice(0, QKVO - D), dot_tn(normed, dqkv_ref[...]))
-    grad_normed = dot_nt(dqkv_ref[...], w_ref[:, : QKVO - D])
+    grad_normed = dot_nt(dqkv_ref[...], w_ref[:, :QKV])
     scaled = grad_normed * gain_one
     grad_vector = factor_one * scaled - source * factor_one**3 * jnp.mean(scaled * source, axis=1, keepdims=True)
     gin_ref[...] = grad_after + grad_vector
@@ -438,16 +639,6 @@
         return carry
 
     lax.fori_loop(0, rows // step, some, 0)
-
-
-class Copies:
-    def __init__(self):
-        self.sent = []
-
-    def make(self, src, dst, send, recv, device):
-        return pltpu.make_async_remote_copy(
-            src_ref=src, dst_ref=dst, send_sem=send, recv_sem=recv, device_id=device, device_id_type=pl.DeviceIdType.MESH
-        )
 
 
 def tail(
@@ -697,14 +888,17 @@
             next(process, None)
 
 
-def call(kernel, out_shape, args, scratch=(), outside=0, **params):
+def call(kernel, out_shape, args, scratch=(), outside=0, out_outside=0, **params):
     spaces = [pltpu.SMEM if a.dtype == jnp.int32 and a.size <= 16 else pltpu.VMEM for a in args]
     spaces[len(args) - outside :] = [pl.ANY] * outside
     return pl.pallas_call(
         kernel,
         out_shape=out_shape,
         in_specs=[pl.BlockSpec(memory_space=space) for space in spaces],
-        out_specs=jax.tree.map(lambda _: pl.BlockSpec(memory_space=pltpu.VMEM), out_shape),
+        out_specs=[
+            pl.BlockSpec(memory_space=pltpu.VMEM if i < len(out_shape) - out_outside else pl.ANY)
+            for i in range(len(out_shape))
+        ],
         scratch_shapes=list(scratch),
         compiler_params=pltpu.CompilerParams(
             vmem_limit_bytes=VMEM_LIMIT, has_side_effects="collective_id" in params, **params
@@ -714,18 +908,6 @@
 
 def shape(dims, dtype):
     return jax.ShapeDtypeStruct(dims, dtype)
-
-
-def rope_tables(seq_lengths, tokens):
-    ends = jnp.sum(jnp.where(np.tri(seq_lengths.shape[1], dtype=bool), seq_lengths[0][None, :], 0), axis=1)
-    token = jnp.arange(tokens, dtype=jnp.int32)
-    start = jnp.max(jnp.where(token[:, None] >= ends[None, :], ends[None, :], 0), axis=1)
-    position = (token - start).astype(F32)
-    frequency = rope_base ** (-jnp.arange(0, HD, 2, dtype=F32) / HD)
-    frequency = jnp.concatenate([frequency] * (LANE // (HD // 2)))
-    sign = jnp.where(jnp.arange(LANE) % HD < HD // 2, -1.0, 1.0)
-    angles = position[:, None] * frequency[None, :]
-    return jnp.cos(angles), jnp.sin(angles) * sign[None, :]
 
 
 def make_body(mesh):
@@ -738,27 +920,29 @@
     ):
         tokens = hidden_in.shape[0]
         rows = w_query.shape[0]
-        packed = jnp.concatenate(
-            [
-                w_query, w_key, w_value, w_output, w_router, norm1_gain[:, None], norm2_gain[:, None],
-                jnp.zeros((rows, LANE - E - 2), BF),
-            ],
-            axis=1,
-        )
-        weights = lax.all_gather(packed, "fsdp", axis=0, tiled=True)
-        dout_all = lax.all_gather(out_cotangent, "fsdp", axis=0, tiled=True)
-        cosines, sines = rope_tables(seq_lengths, tokens)
-        q, kd, vd, p, o, h1, n2, gd, gt = call(
-            attention_forward,
-            (
-                shape((tokens, D), BF), shape((tokens, D), BF), shape((tokens, D), BF),
-                shape((KVH, 2 * tokens, tokens), F32), shape((tokens, D), BF), shape((tokens, D), F32),
-                shape((tokens, D), BF), shape((tokens, LANE), F32), shape((E, tokens), F32),
-            ),
-            (hidden_in, seq_lengths, routes, cosines, sines, weights),
-        )
         chips = group // 2
         dma = pltpu.SemaphoreType.DMA
+        weights, q, kd, vd, o, h1, n2, gd, gt, cosines, sines, p, dout_all = call(
+            functools.partial(front, replicas, chips),
+            (
+                shape((chips, 2, rows, W_O + D), BF), shape((tokens, D), BF), shape((tokens, D), BF),
+                shape((tokens, D), BF), shape((tokens, D), BF), shape((tokens, D), F32), shape((tokens, D), BF),
+                shape((tokens, LANE), F32), shape((E, tokens), F32), shape((tokens, LANE), F32),
+                shape((tokens, LANE), F32), shape((KVH, 2 * tokens, tokens), F32), shape((chips, 2, tokens, D), BF),
+            ),
+            (
+                hidden_in, seq_lengths, routes.T, rope_table(tokens), w_query, w_key, w_value, w_output, w_router.T,
+                norm1_gain[None], norm2_gain[None], out_cotangent,
+            ),
+            [
+                pltpu.VMEM((2, 2 * tokens, tokens), F32), dma((2,)), dma((1,)), dma((3, chips)), dma((3, chips)),
+                dma((3, chips)), dma((3, chips, replicas)), dma((3, chips, replicas)), dma((2, chips)),
+                dma((2, chips)), dma((3, chips)), dma((chips, 2)),
+            ],
+            out_outside=2,
+            collective_id=2,
+        )
+        weights = weights.reshape(D, W_O + D)
         anywhere = pl.BlockSpec(memory_space=pl.ANY)
         inside = pl.BlockSpec(memory_space=pltpu.VMEM)
         wide = D + LANE
@@ -779,11 +963,10 @@
             ]
             + ([dma((chips,))] * 3 + [dma((chips, 2))]) * 2 + [dma((chips,))] * 4 + [dma((2,)), dma((2,)), dma((1,))],
             compiler_params=pltpu.CompilerParams(vmem_limit_bytes=VMEM_LIMIT, has_side_effects=True, collective_id=1),
-        )(n2, gt, dout_all.reshape(chips, 2, tokens, D), expert_weights)
+        )(n2, gt, dout_all, expert_weights)
         moe = lax.psum_scatter(yp.reshape(group * tokens, D), "fsdp", scatter_dimension=0, tiled=True)
         layer_out = (h1 + residual_scale * moe.astype(F32)).astype(BF)
         bits = replicas.bit_length() - 1
-        rows = D // group
         size = 3 * FF // bits if bits else 0
         grad_in, grad_experts, gw = call(
             functools.partial(tail, replicas, group // 2),

time: 420 us -> 373 us (0.89)
  waiting for transfers between devices: 99.5 us -> 0.02 us
  Pallas kernels: 282 us -> 343 us
  local copies, waits for them, and re-layouts: 11.1 us -> 5.14 us
    all_gather x2 -> x0, waiting for transfers between devices: 98.8 us -> none  [the longest x1 61.4 us: body(): weights = lax.all_gather(packed, 'fsdp', axis=0, tiled=True)]
    pallas_call x2, Pallas kernels: 193 us -> 251 us  [call(): pl.pallas_call(kernel, out_shape=out_shape, in_specs=[pl.BlockSpec(memory...]
  transfers between devices with their start and end apart: 3 -> 1, of which waited for: 2 -> 0; matrix products, arithmetic and copies ran while one was open for 4% -> 4% of each run, Pallas kernels for 46% -> 49%
where the time goes in v4:
time: 373 us
  Pallas kernels  343 us (92%)
  between operations  14.1 us (4%)
  other arithmetic  11.3 us (3%)
  local copies, waits for them, and re-layouts  5.14 us (1%)
    pallas_call x2, Pallas kernels, call(): pl.pallas_call(kernel, out_shape=out_shape, in_specs=[pl.BlockSpec(memory...  251 us
    pallas_call x1, Pallas kernels, body(): pl.pallas_call(functools.partial(middle, chips), in_specs=[inside, inside...  91.3 us
    convert_element_type x1, other arithmetic, body(): grad_experts.astype(F32)  9.26 us
  transfers between devices with their start and end apart: 1, of which 0 were waited for; matrix products, arithmetic and copies ran while one was open for 4% of the time, Pallas kernels for 49%

profile of v4, /device:TPU:10, one launch (start us, length us, event | category | flops | bytes accessed | tf_op | source)
XLA Modules:
  0.0 373.1 jit_solution(7800371640188434489)
XLA Ops:
  7.2 0.0 reduce-scatter.2.cloned.1.call-start
  7.2 69.3 %shard_map.204 = (bf16[4,2,128,3200]{3,2,1,0:T(8,128)(2,1)}, bf16[256,1024]{1,0:T(8,128)(2,1)}, bf16[256,1024]{1,0:T(8,128)(2,1)}, bf16[256,1024]{1,0:T(8,128)(2...) custom-call(bf16[256,1024]{1,0:T(8,128)(2,1)} %x_ref.3, ...), custom_call_target="tpu_custom_call" | custom-call | tf_op jit(solution)/shard_map/pallas_call | solution.py:894
  76.6 91.3 %shard_map.205 = (f32[256,1152]{1,0:T(8,128)}, bf16[4,2,256,1024]{3,2,1,0:T(8,128)(2,1)}, bf16[2,1536,1024]{2,1,0:T(8,128)(2,1)}) custom-call(bf16[256,1024]{1,0:T(8,128)(2,1)} %get-tuple-element.30.n2_ref, f32[16,256]{1,0:T(8,128)} %get-tuple-element.31.gt_ref, bf16[4,2,256,1024]{3,2,1,0:T(8,128)(2,1)} %get-tuple-element.32.do_hbm, bf16[2,1536,1024]{2,1,0:T(8,128)(2,1)} %w_hbm.1), custom_call_target="tpu_custom_call" | custom-call | tf_op jit(solution)/shard_map/pallas_call | solution.py:949
  167.9 0.0 reduce-scatter.2.cloned.1.call-update
  167.9 181.9 %shard_map.206 = (f32[256,1024]{1,0:T(8,128)}, bf16[2,1536,1024]{2,1,0:T(8,128)(2,1)}, f32[128,3200]{1,0:T(8,128)}) custom-call(bf16[256,1024]{1,0:T(8,128)(2,1)} %x_ref.3, bf16[256,1024]{1,0:T(8,128)(2,1)} %dout_ref.3, f32[256,128]{1,0:T(8,128)} %get-tuple-element.34.cos_ref, f32[256,128]{1,0:T(8,128)} %get-tuple-element.35.sin_ref, ...), custom_call_target="tpu_custom_call" | custom-call | tf_op jit(solution)/shard_map/pallas_call | solution.py:894
  349.8 0.8 slice.27
  350.7 0.7 copy.24
  351.3 0.0 copy-start.1
  351.3 0.0 copy-start
  351.3 9.3 %convert_element_type.11 = f32[2,1536,1024]{2,1,0:T(8,128)} convert(bf16[2,1536,1024]{2,1,0:T(8,128)(2,1)} %get-tuple-element.47) | non-fusion elementwise | flops 3145728 | bytes 18874368 | tf_op jit(solution)/shard_map/convert_element_type | solution.py:993
  360.6 0.0 copy-done.1
  360.6 0.0 copy-start.2
  360.6 0.7 slice_reduce_fusion
  361.3 0.9 fusion.1
  362.2 1.1 fusion
  363.3 0.0 reduce-scatter.2.cloned.1.call-done
  363.3 0.0 copy-done
  363.3 2.0 add_convert_fusion
  365.3 0.0 copy-done.2
  365.3 1.0 copy.26
Async XLA Ops:
  7.2 356.1 %reduce-scatter.2.cloned.1.call-start = ((), (), s32[]{:S(2)}) async-start(), calls=%async_computation.1 | async-start | bytes 4718592 | tf_op jit(solution)/shard_map/reduce_scatter | solution.py:967
  351.3 9.3 %copy-start.1 = (f32[128,3200]{1,0:T(8,128)S(1)}, f32[128,3200]{1,0:T(8,128)}, u32[]{:S(2)}) copy-start(f32[128,3200]{1,0:T(8,128)} %get-tuple-element.46) | copy-start | bytes 4915204
  351.3 11.9 %copy-start = (f32[256,1024]{1,0:T(8,128)S(1)}, f32[256,1024]{1,0:T(8,128)}, u32[]{:S(2)}) copy-start(f32[256,1024]{1,0:T(8,128)} %get-tuple-element.29.h1_ref) | copy-start | bytes 3145732
  360.6 4.7 %copy-start.2 = (f32[256,1024]{1,0:T(8,128)S(1)}, f32[256,1024]{1,0:T(8,128)}, u32[]{:S(2)}) copy-start(f32[256,1024]{1,0:T(8,128)} %get-tuple-element.85) | copy-start | bytes 3145732
Sparse Core Ops, SparseCore 0:
  168.0 62.3 reduce-scatter.1

commit v5 on v4

--- a/solution.py
+++ b/solution.py
@@ -589,6 +589,7 @@
     put(slice(QKVO - D, QKVO), dot_tn(o_ref[...], grad_branch))
     do_ref[...] = dot_nt(grad_branch, w_ref[:, W_O:]).astype(BF)
     grad_router = dot_tn(n2_ref[...], grad_logits)
+    yield
 
     cosines, sines = cos_ref[...], sin_ref[...]
     key_back, value_back = [], []
@@ -616,6 +617,7 @@
         dqkv_ref[:, at] = (block * cosines - turned(block, lane) * sines).astype(BF)
         at = slice(H * HD + KVH * HD + m * LANE, H * HD + KVH * HD + (m + 1) * LANE)
         dqkv_ref[:, at] = jnp.where(low, value_back[2 * m], value_back[2 * m + 1]).astype(BF)
+    yield
 
     source = x_ref[...].astype(F32)
     factor_one = lax.rsqrt(jnp.mean(source * source, axis=1, keepdims=True) + norm_eps)
@@ -635,7 +637,7 @@
 def add_rows(target, first, second, rows, step):
     def some(i, carry):
         at = pl.ds(pl.multiple_of(i * step, step), step)
-        target(at, first(at).astype(F32) + second(at).astype(F32))
+        target[at] = (first[at].astype(F32) + second[at].astype(F32)).astype(target.dtype)
         return carry
 
     lax.fori_loop(0, rows // step, some, 0)
@@ -643,39 +645,30 @@
 
 def tail(
     replicas, chips,
-    x_ref, dout_ref, cos_ref, sin_ref, w_ref, q_ref, kd_ref, vd_ref, o_ref, h1_ref, n2_ref, gd_ref, dx_ref, ge_ref, p_hbm,
-    gin_ref, gexp_ref, gproj_ref,
-    p_ref, p_sem, do_ref, dqkv_ref, gw_ref, core_ref, up_ref, down_ref, parts_ref, smalls_ref, result_ref, *rest,
+    x_ref, dout_ref, cos_ref, sin_ref, q_ref, kd_ref, vd_ref, o_ref, h1_ref, n2_ref, gd_ref, dx_ref,
+    w_hbm, ge_hbm, yp_hbm, p_hbm,
+    gin_ref, out_ref, gexp_ref, gproj_ref,
+    w_ref, p_ref, do_ref, dqkv_ref, gw_ref, gw_core, gw_up, gw_down, y_ref, y_core, y_up, y_down,
+    parts_ref, smalls_ref, result_ref, *rest,
 ):
     bits = replicas.bit_length() - 1
-    jobs = ge_ref.shape[0] * bits
-    arrived = rest[:bits]
-    kept = rest[bits : 2 * bits - 1] if bits else ()
-    rest = rest[2 * bits - 1 if bits else 0 :]
-    (ar_send, ar_recv, core_send, core_recv, up_send, up_recv, down_send, down_recv,
+    arrived, rest = rest[:bits], rest[bits:]
+    kept, rest = rest[: max(bits - 1, 1)], rest[max(bits - 1, 1) :]
+    (load_sem, p_sem, y_load, ge_load, ar_send, ar_recv, y_core_sem, y_up_send, y_up_recv, y_down_send, y_down_recv,
+     gw_core_sem, gw_up_send, gw_up_recv, gw_down_send, gw_down_recv,
      part_send, part_recv, small_send, small_recv, result_send, result_recv) = rest
     r, f = lax.axis_index("replica"), lax.axis_index("fsdp")
     z, c = f // 2, f % 2
-    mate = (r, z * 2 + 1 - c)
-    above, below = (r, f + 2), (r, f - 2)
-    rows = gw_ref.shape[2]
+    mate, above, below = (r, z * 2 + 1 - c), (r, f + 2), (r, f - 2)
+    rows, tokens = gw_ref.shape[2], x_ref.shape[0]
+    local = ge_hbm.shape[0]
     make = Copies().make
 
-    barrier = pltpu.get_barrier_semaphore()
-    expected = 1 + (replicas - 1) + jnp.where(z > 0, 1, 0) + jnp.where(z < chips - 1, 1, 0)
-    pl.semaphore_signal(barrier, inc=1, device_id=mate, device_id_type=pl.DeviceIdType.MESH)
-    for d in range(1, replicas):
-        pl.semaphore_signal(barrier, inc=1, device_id=((r + d) % replicas, f), device_id_type=pl.DeviceIdType.MESH)
-
-    @pl.when(z > 0)
-    def _():
-        pl.semaphore_signal(barrier, inc=1, device_id=below, device_id_type=pl.DeviceIdType.MESH)
-
-    @pl.when(z < chips - 1)
-    def _():
-        pl.semaphore_signal(barrier, inc=1, device_id=above, device_id_type=pl.DeviceIdType.MESH)
-
-    pl.semaphore_wait(barrier, expected)
+    load_w = pltpu.make_async_copy(w_hbm, w_ref, load_sem.at[0])
+    load_y = [pltpu.make_async_copy(yp_hbm.at[k, c], y_ref.at[k], y_load.at[k]) for k in range(chips)]
+    peers = [(True, mate), (z > 0, below), (z < chips - 1, above)]
+    peers += [(True, ((r + d) % replicas, f)) for d in range(1, replicas)]
+    meet(peers, 1 + (replicas - 1) + jnp.where(z > 0, 1, 0) + jnp.where(z < chips - 1, 1, 0))
 
     def bit_of(b):
         return (r // (1 << b)) % 2
@@ -684,7 +677,7 @@
         return (r + (1 - 2 * bit_of(b)) * (1 << b), f)
 
     def halving(e):
-        size = ge_ref.shape[1] // bits
+        size = ge_hbm.shape[1] // bits
         orders = [[(g + k) % bits for k in range(bits)] for g in range(bits)]
         starts = [[] for _ in range(bits)]
         for g in range(bits):
@@ -693,48 +686,52 @@
                 starts[g].append(at)
                 at = at + bit_of(orders[g][k]) * (size >> (k + 1))
             starts[g].append(at)
-        copies = {}
-
-        def source(g, k, at, length):
-            return ge_ref.at[e, pl.ds(g * size + at, length)] if k == 0 else kept[k - 1].at[e * bits + g, pl.ds(at, length)]
+        copies, loads = {}, {}
+
+        def region(g, k):
+            half = size >> (k + 1)
+            return pl.ds(pl.multiple_of(starts[g][k + 1], half), half)
 
         def exchange(g, k):
             half = size >> (k + 1)
-            give = pl.multiple_of((1 - bit_of(orders[g][k])) * half, half)
+            give = (1 - bit_of(orders[g][k])) * half
+            if k:
+                source = kept[k - 1].at[e * bits + g, pl.ds(pl.multiple_of(give, half), half)]
+            else:
+                source = ge_hbm.at[e, pl.ds(pl.multiple_of(g * size + give, half), half)]
             copies[g, k] = make(
-                source(g, k, give, half), arrived[k].at[e * bits + g], ar_send.at[e * bits + g, k],
-                ar_recv.at[e * bits + g, k], partner(orders[g][k]),
+                source, arrived[k].at[e * bits + g],
+                ar_send.at[e * bits + g, k], ar_recv.at[e * bits + g, k], partner(orders[g][k]),
             )
             copies[g, k].start()
 
         def spread(g, k):
-            half = size >> (k + 1)
-            at = pl.ds(pl.multiple_of(starts[g][k + 1], half), half)
+            ref = gexp_ref.at[e, region(g, k)]
             copies[g, bits + k] = make(
-                gexp_ref.at[e, at], gexp_ref.at[e, at], ar_send.at[e * bits + g, bits + k],
-                ar_recv.at[e * bits + g, bits + k], partner(orders[g][k]),
+                ref, ref, ar_send.at[e * bits + g, bits + k], ar_recv.at[e * bits + g, bits + k], partner(orders[g][k])
             )
             copies[g, bits + k].start()
 
         for g in range(bits):
             exchange(g, 0)
+        for g in range(bits):
+            loads[g] = pltpu.make_async_copy(
+                ge_hbm.at[e, region(g, 0)], kept[0].at[e * bits + g], ge_load.at[e * bits + g]
+            )
+            loads[g].start()
         yield
         for k in range(bits):
             half = size >> (k + 1)
             for g in range(bits):
+                if k == 0:
+                    loads[g].wait()
                 copies[g, k].wait_recv()
-                keep = pl.multiple_of(bit_of(orders[g][k]) * half, half)
-                own = source(g, k, keep, half)
-                there = arrived[k].at[e * bits + g]
-                if k < bits - 1:
-                    into = kept[k].at[e * bits + g]
-                else:
-                    into = gexp_ref.at[e, pl.ds(pl.multiple_of(starts[g][bits], half), half)]
-
-                def write(at, value, into=into):
-                    into[at] = value.astype(BF)
-
-                add_rows(write, lambda at: own[at], lambda at: there[at], half, min(half, 64))
+                job = e * bits + g
+                own = kept[max(k - 1, 0)].at[job]
+                if k:
+                    own = own.at[pl.ds(pl.multiple_of(bit_of(orders[g][k]) * half, half), half)]
+                into = kept[k].at[job] if k < bits - 1 else gexp_ref.at[e, region(g, k)]
+                add_rows(into, own, arrived[k].at[job], half, min(half, 64))
                 if k < bits - 1:
                     exchange(g, k + 1)
                 else:
@@ -749,34 +746,30 @@
         for copy in copies.values():
             copy.wait_send()
 
-    def line():
-        crossing = make(gw_ref.at[:, 1 - c], core_ref, core_send.at[0], core_recv.at[0], mate)
+    def line(for_mate, core_ref, own, ready, up_ref, down_ref, core_sem, up_send, up_recv, down_send, down_recv, step):
+        size = core_ref.shape[1]
+        crossing = make(for_mate, core_ref, core_sem.at[0], core_sem.at[1], mate)
         crossing.start()
         yield
         crossing.wait_recv()
 
         def add_block(block, other):
-            def write(at, value):
-                gw_ref[block, c, at] = value.astype(BF)
-
-            add_rows(write, lambda at: gw_ref[block, c, at], lambda at: other[block, at], rows, 16)
+            add_rows(own(block), own(block), other.at[block], size, step)
 
         def send(block, up):
             there, send_sem, recv_sem = (up_ref, up_send, up_recv) if up else (down_ref, down_send, down_recv)
-            return make(
-                gw_ref.at[block, c], there.at[block], send_sem.at[block], recv_sem.at[block], above if up else below
-            )
-
-        for k in range(chips):
+            return make(own(block), there.at[block], send_sem.at[block], recv_sem.at[block], above if up else below)
+
+        ready()
+        nearby = [k for pair in zip(range(chips - 1, -1, -1), range(chips)) for k in pair][:chips]
+        for k in nearby:
             add_block(k, core_ref)
-        for k in range(chips - 1):
-            owner = chips - 1 - k
-
-            @pl.when(z == 0)
+
+            @pl.when((z == 0) & (k > 0))
             def _():
-                send(owner, True).start()
-
-            @pl.when(z == chips - 1)
+                send(k, True).start()
+
+            @pl.when((z == chips - 1) & (k < chips - 1))
             def _():
                 send(k, False).start()
 
@@ -808,6 +801,29 @@
             send(z, False).wait_recv()
             add_block(z, down_ref)
 
+        crossing.wait_send()
+        for k in range(chips):
+
+            @pl.when(z < k)
+            def _():
+                send(k, True).wait_send()
+
+            @pl.when(z > k)
+            def _():
+                send(k, False).wait_send()
+
+    def mixture():
+        yield from line(
+            yp_hbm.at[:, 1 - c], y_core, lambda k: y_ref.at[k], lambda: [copy.wait() for copy in load_y], y_up, y_down,
+            y_core_sem, y_up_send, y_up_recv, y_down_send, y_down_recv, 32,
+        )
+        out_ref[...] = (h1_ref[...] + residual_scale * y_ref[z].astype(F32)).astype(BF)
+
+    def projection():
+        yield from line(
+            gw_ref.at[:, 1 - c], gw_core, lambda k: gw_ref.at[k, c], lambda: None, gw_up, gw_down,
+            gw_core_sem, gw_up_send, gw_up_recv, gw_down_send, gw_down_recv, 16,
+        )
         wide = QKVO // replicas
 
         def columns(part):
@@ -853,39 +869,57 @@
             make(result_ref.at[peer], result_ref.at[peer], result_send.at[d], result_recv.at[peer], (peer, f)).wait_recv()
         for k in range(replicas):
             gproj_ref[:, k * wide : (k + 1) * wide] = result_ref[k].astype(F32)
-        crossing.wait_send()
-        for k in range(chips):
-
-            @pl.when(z < k)
-            def _():
-                send(k, True).wait_send()
-
-            @pl.when(z > k)
-            def _():
-                send(k, False).wait_send()
-
         for d in range(1, replicas):
             part_copy(d).wait_send()
             small_copy(d).wait_send()
             result_copy(d).wait_send()
 
-    experts_sums = [halving(e) for e in range(ge_ref.shape[0])] if bits else []
-    for e, sums in enumerate(experts_sums):
-        next(sums)
+    sums = [halving(e) for e in range(local)] if bits else []
+    first, last = sums[:1], sums[1:]
+    moe, grads = [mixture()], [projection()]
+
+    def go(*turns):
+        for turn in turns:
+            for process in turn:
+                next(process, None)
+
+    go(sums, moe)
+    load_w.start()
+    for copy in load_y:
+        copy.start()
     if not bits:
-        gexp_ref[...] = ge_ref[...]
-    attention_backward(
+        pltpu.sync_copy(ge_hbm, gexp_ref)
+    load_w.wait()
+    backward = attention_backward(
         x_ref, dout_ref, cos_ref, sin_ref, w_ref, q_ref, kd_ref, vd_ref, p_hbm, o_ref, h1_ref, n2_ref, gd_ref, dx_ref,
         gin_ref, gw_ref, do_ref, dqkv_ref, p_ref, p_sem,
     )
-    projections = line()
-    first, last = experts_sums[:1], experts_sums[1:]
-    order = [[projections], first, [projections], last, [projections], first, last, [projections], first, last]
-    order += [[projections], first, [projections], last, [projections]]
-    order += [[projections] + experts_sums] * (chips + 2 * bits)
-    for turn in order:
-        for process in turn:
-            next(process, None)
+    next(backward)
+    go(moe)
+    next(backward)
+    go(first, moe)
+    next(backward, None)
+    go(grads, moe, grads, last, first, moe, last, first, grads, last, grads, first, grads, last, grads, grads)
+    go(*[moe + grads + sums] * (2 * chips + 2 * bits + 4))
+
+
+def finish(gexp_ref, gproj_ref, gin_ref, out_ref, *outs):
+    layer, grad_in, gains_one, query, key, value, output, gains_two, router, expert = outs
+    expert[...] = gexp_ref[...].astype(F32)
+
+    @pl.when(pl.program_id(0) == 0)
+    def _():
+        layer[...] = out_ref[...]
+        grad_in[...] = gin_ref[...]
+        a, b, c = H * HD, H * HD + KVH * HD, QKV
+        query[...] = gproj_ref[:, :a]
+        key[...] = gproj_ref[:, a:b]
+        value[...] = gproj_ref[:, b:c]
+        output[...] = gproj_ref[:, c:QKVO]
+        small = gproj_ref[:, QKVO:].T
+        router[...] = small[:E]
+        gains_one[...] = small[E : E + 1]
+        gains_two[...] = small[E + 1 : E + 2]
 
 
 def call(kernel, out_shape, args, scratch=(), outside=0, out_outside=0, **params):
@@ -964,33 +998,55 @@
             + ([dma((chips,))] * 3 + [dma((chips, 2))]) * 2 + [dma((chips,))] * 4 + [dma((2,)), dma((2,)), dma((1,))],
             compiler_params=pltpu.CompilerParams(vmem_limit_bytes=VMEM_LIMIT, has_side_effects=True, collective_id=1),
         )(n2, gt, dout_all, expert_weights)
-        moe = lax.psum_scatter(yp.reshape(group * tokens, D), "fsdp", scatter_dimension=0, tiled=True)
-        layer_out = (h1 + residual_scale * moe.astype(F32)).astype(BF)
         bits = replicas.bit_length() - 1
         size = 3 * FF // bits if bits else 0
-        grad_in, grad_experts, gw = call(
-            functools.partial(tail, replicas, group // 2),
-            (shape((tokens, D), F32), shape((local, 3 * FF, D), BF), shape((rows, QKVO + LANE), F32)),
-            (hidden_in, out_cotangent, cosines, sines, weights, q, kd, vd, o, h1, n2, gd, dx, grad_experts, p),
+        width = QKVO + LANE
+        grad_in, layer_out, grad_experts, gw = call(
+            functools.partial(tail, replicas, chips),
+            (
+                shape((tokens, D), F32), shape((tokens, D), BF), shape((local, 3 * FF, D), BF), shape((rows, width), F32),
+            ),
+            (hidden_in, out_cotangent, cosines, sines, q, kd, vd, o, h1, n2, gd, dx, weights, grad_experts, yp, p),
             [
-                pltpu.VMEM((2, 2 * tokens, tokens), F32), dma((2,)),
-                pltpu.VMEM((tokens, D), BF), pltpu.VMEM((tokens, QKVO - D), BF),
-                pltpu.VMEM((group // 2, 2, rows, QKVO + LANE), BF), pltpu.VMEM((group // 2, rows, QKVO + LANE), BF),
-                pltpu.VMEM((group // 2, rows, QKVO + LANE), BF), pltpu.VMEM((group // 2, rows, QKVO + LANE), BF),
+                pltpu.VMEM((D, W_O + D), BF), pltpu.VMEM((2, 2 * tokens, tokens), F32), pltpu.VMEM((tokens, D), BF),
+                pltpu.VMEM((tokens, QKV), BF), pltpu.VMEM((chips, 2, rows, width), BF),
+            ]
+            + [pltpu.VMEM((chips, rows, width), BF)] * 3 + [pltpu.VMEM((chips, tokens, D), BF)] * 4
+            + [
                 pltpu.VMEM((replicas, rows, QKVO // replicas), BF), pltpu.VMEM((replicas, rows, LANE), BF),
                 pltpu.VMEM((replicas, rows, QKVO // replicas), BF),
             ]
             + [pltpu.VMEM((local * bits, size >> (k + 1), D), BF) for k in range(bits)]
-            + [pltpu.VMEM((local * bits, size >> (k + 1), D), BF) for k in range(bits - 1)]
-            + [dma((max(local * bits, 1), max(2 * bits, 1)))] * 2 + [dma((1,))] * 2 + [dma((group // 2,))] * 4
-            + [dma((replicas,))] * 6,
-            outside=1,
+            + [pltpu.VMEM((max(local * bits, 1), max(size >> (k + 1), 16), D), BF) for k in range(max(bits - 1, 1))]
+            + [dma((1,)), dma((2,)), dma((chips,)), dma((max(local * bits, 1),))]
+            + [dma((max(local * bits, 1), max(2 * bits, 1)))] * 2
+            + ([dma((2,))] + [dma((chips,))] * 4) * 2 + [dma((replicas,))] * 6,
+            outside=4,
             collective_id=0,
         )
-        a, b, c = H * HD, H * HD + KVH * HD, H * HD + 2 * KVH * HD
+        steps = 8
+        block = local * 3 * FF // steps
+        fixed = [
+            shape((tokens, D), BF), shape((tokens, D), F32), shape((1, rows), F32), shape((rows, H * HD), F32),
+            shape((rows, KVH * HD), F32), shape((rows, KVH * HD), F32), shape((rows, D), F32), shape((1, rows), F32),
+            shape((E, rows), F32),
+        ]
+
+        def still(a):
+            return pl.BlockSpec(a.shape, lambda i: (0, 0))
+
+        expert_block = pl.BlockSpec((block, D), lambda i: (i, 0))
+        outs = pl.pallas_call(
+            finish,
+            grid=(steps,),
+            in_specs=[expert_block, still(gw), still(grad_in), still(layer_out)],
+            out_specs=[still(a) for a in fixed] + [expert_block],
+            out_shape=fixed + [shape((local * 3 * FF, D), F32)],
+            compiler_params=pltpu.CompilerParams(vmem_limit_bytes=32 * 2**20),
+        )(grad_experts.reshape(local * 3 * FF, D), gw, grad_in, layer_out)
         return (
-            layer_out, grad_in, gw[:, QKVO + E], gw[:, :a], gw[:, a:b], gw[:, b:c], gw[:, c:QKVO], gw[:, QKVO + E + 1],
-            gw[:, QKVO : QKVO + E], grad_experts.astype(F32),
+            outs[0], outs[1], outs[2][0], outs[3], outs[4], outs[5], outs[6], outs[7][0], outs[8].T,
+            outs[9].reshape(local, 3 * FF, D),
         )
 
     return body

time: 373 us -> 327 us (0.88)
  Pallas kernels: 343 us -> 317 us
  between operations: 14.1 us -> 0.68 us
  other arithmetic: 11.3 us -> 0 us
    pallas_call x2, Pallas kernels: 251 us -> 219 us  [call(): pl.pallas_call(kernel, out_shape=out_shape, in_specs=[pl.BlockSpec(memory...]
    convert_element_type x2 -> x0, other arithmetic: 11.3 us -> none  [the longest x1 9.26 us: body(): grad_experts.astype(F32)]
    pallas_call x0 -> x1, Pallas kernels: none -> 6.73 us  [body(): pl.pallas_call(finish, grid=(steps,), in_specs=[expert_block, still(gw),...]
    unnamed x8, local copies, waits for them, and re-layouts: 1.65 us -> 6.47 us
  transfers between devices with their start and end apart: 1 -> 0, of which waited for: 0 -> 0; matrix products, arithmetic and copies ran while one was open for 4% -> 0% of each run, Pallas kernels for 49% -> 0%
where the time goes in v5:
time: 327 us; the launch traced here: 324 us
  Pallas kernels  317 us (97%)
  local copies, waits for them, and re-layouts  6.47 us (2%)
    pallas_call x2, Pallas kernels, call(): pl.pallas_call(kernel, out_shape=out_shape, in_specs=[pl.BlockSpec(memory...  219 us
    pallas_call x1, Pallas kernels, body(): pl.pallas_call(functools.partial(middle, chips), in_specs=[inside, inside...  91.5 us
    pallas_call x1, Pallas kernels, body(): pl.pallas_call(finish, grid=(steps,), in_specs=[expert_block, still(gw),...  6.73 us

profile of v5, /device:TPU:10, one launch (start us, length us, event | category | flops | bytes accessed | tf_op | source)
XLA Modules:
  0.0 324.2 jit_solution(11162140964464299656)
XLA Ops:
  0.6 69.2 %shard_map.204 = (bf16[4,2,128,3200]{3,2,1,0:T(8,128)(2,1)}, bf16[256,1024]{1,0:T(8,128)(2,1)}, bf16[256,1024]{1,0:T(8,128)(2,1)}, bf16[256,1024]{1,0:T(8,128)(2...) custom-call(bf16[256,1024]{1,0:T(8,128)(2,1)} %x_ref.3, ...), custom_call_target="tpu_custom_call" | custom-call | tf_op jit(solution)/shard_map/pallas_call | solution.py:928
  69.9 91.5 %shard_map.205 = (f32[256,1152]{1,0:T(8,128)}, bf16[4,2,256,1024]{3,2,1,0:T(8,128)(2,1)}, bf16[2,1536,1024]{2,1,0:T(8,128)(2,1)}) custom-call(bf16[256,1024]{1,0:T(8,128)(2,1)} %get-tuple-element.47.n2_ref, f32[16,256]{1,0:T(8,128)} %get-tuple-element.49.gt_ref, bf16[4,2,256,1024]{3,2,1,0:T(8,128)(2,1)} %get-tuple-element.50.do_hbm, bf16[2,1536,1024]{2,1,0:T(8,128)(2,1)} %w_hbm.1), custom_call_target="tpu_custom_call" | custom-call | tf_op jit(solution)/shard_map/pallas_call | solution.py:983
  161.3 149.6 %shard_map.206 = (f32[256,1024]{1,0:T(8,128)}, bf16[256,1024]{1,0:T(8,128)(2,1)}, bf16[2,1536,1024]{2,1,0:T(8,128)(2,1)}, f32[128,3200]{1,0:T(8,128)}) custom-call(bf16[256,1024]{1,0:T(8,128)(2,1)} %x_ref.3, bf16[256,1024]{1,0:T(8,128)(2,1)} %dout_ref.3, f32[256,128]{1,0:T(8,128)} %get-tuple-element.40.cos_ref, f32[256,128]{1,0:T(8,128)} %get-tuple-element.41.sin_ref, ...), custom_call_target="tpu_custom_call" | custom-call | tf_op jit(solution)/shard_map/pallas_call | solution.py:928
  311.0 0.0 copy-start
  311.0 2.8 copy-done
  313.8 0.0 copy-start.1
  313.8 1.4 copy-done.1
  315.2 0.0 copy-start.2
  315.2 1.2 copy-done.2
  316.4 0.0 copy-start.3
  316.4 1.0 copy-done.3
  317.5 6.7 %shard_map.207 = (bf16[256,1024]{1,0:T(8,128)(2,1)}, f32[256,1024]{1,0:T(8,128)}, f32[1,128]{1,0:T(1,128)}, f32[128,1024]{1,0:T(8,128)}, f32[128,512]{1,0:T(8,12...) custom-call(bf16[3072,1024]{1,0:T(8,128)(2,1)S(1)} %bitcast.10, ...), custom_call_target="tpu_custom_call" | custom-call | tf_op jit(solution)/shard_map/pallas_call | solution.py:1039
Async XLA Ops:
  311.0 2.8 copy-start
  313.8 1.4 copy-start.1
  315.2 1.2 copy-start.2
  316.4 1.0 copy-start.3

commit v6 on v5

v6 whole, which is shorter than its diff:
```python
import functools

import jax
import jax.numpy as jnp
import numpy as np
from jax import lax
from jax.experimental import pallas as pl
from jax.experimental.pallas import tpu as pltpu
from jax.sharding import PartitionSpec as P

D = 1024
H = 16
KVH = 8
HD = 64
FF = 512
TOPK = 8
E = 16
CAP = 144
LANE = 128
QKV = H * HD + 2 * KVH * HD
QKVO = QKV + D
W_O = QKV + LANE

norm_eps = 1e-06
score_scale = 0.015625
residual_scale = 0.22
rope_base = 10000.0
masked_score = -1e30

BF = jnp.bfloat16
F32 = jnp.float32
VMEM_LIMIT = 63 * 2**20


def dot(a, b):
    return lax.dot_general(a, b, (((1,), (0,)), ((), ())), preferred_element_type=F32)


def dot_nt(a, b):
    return lax.dot_general(a, b, (((1,), (1,)), ((), ())), preferred_element_type=F32)


def dot_tn(a, b):
    return lax.dot_general(a, b, (((0,), (0,)), ((), ())), preferred_element_type=F32)


def lanes_of(rows):
    return lax.broadcasted_iota(jnp.int32, (rows, LANE), 1)


def turned(block, lane):
    return jnp.where(lane % HD < HD // 2, pltpu.roll(block, LANE - HD // 2, 1), pltpu.roll(block, HD // 2, 1))


def halves(block, low):
    zero = jnp.zeros_like(block)
    return jnp.concatenate([jnp.where(low, block, zero), jnp.where(low, zero, block)], axis=0)


def rope_table(tokens):
    frequency = np.float32(rope_base) ** (-np.arange(0, HD, 2, dtype=np.float32) / np.float32(HD))
    frequency = np.tile(frequency.astype(np.float32), LANE // (HD // 2))
    angles = (np.arange(tokens, dtype=np.float32)[:, None] * frequency[None, :]).astype(np.float64)
    sign = np.where(np.arange(LANE) % HD < HD // 2, -1.0, 1.0)
    pieces = []
    for values in (np.cos(angles), np.sin(angles) * sign[None, :]):
        rest = values.astype(np.float32)
        for _ in range(3):
            piece = rest.astype(BF)
            pieces.append(piece)
            rest = rest - piece.astype(np.float32)
    return np.concatenate(pieces, axis=1)


class Copies:
    def make(self, src, dst, send, recv, device):
        return pltpu.make_async_remote_copy(
            src_ref=src, dst_ref=dst, send_sem=send, recv_sem=recv, device_id=device, device_id_type=pl.DeviceIdType.MESH
        )


def meet(devices, expected):
    barrier = pltpu.get_barrier_semaphore()
    for condition, device in devices:

        def signal(device=device):
            pl.semaphore_signal(barrier, inc=1, device_id=device, device_id_type=pl.DeviceIdType.MESH)

        if condition is True:
            signal()
        else:
            pl.when(condition)(signal)
    pl.semaphore_wait(barrier, expected)


def front(
    replicas, chips,
    x_ref, len_ref, routes_ref, table_ref, wq_ref, wk_ref, wv_ref, wo_ref, wr_ref, g1_ref, g2_ref, dout_ref,
    w_all, q_ref, kd_ref, vd_ref, o_ref, h1_ref, n2_ref, gd_ref, gt_ref, cos_ref, sin_ref, p_hbm, do_all,
    p_ref, p_sem, own_sem, z_up, z_down, z_recv, xy_send, xy_recv, mate_send, mate_recv, do_send, do_recv,
):
    tokens = x_ref.shape[0]
    r, f = lax.axis_index("replica"), lax.axis_index("fsdp")
    z, c = f // 2, f % 2
    mate, above, below = (r, z * 2 + 1 - c), (r, f + 2), (r, f - 2)
    make = Copies().make
    peers = [(True, mate), (z > 0, below), (z < chips - 1, above)]
    peers += [(True, ((r + d) % replicas, f)) for d in range(1, replicas)]

    own_dout = pltpu.make_async_copy(dout_ref, do_all.at[z, c], own_sem.at[0])
    own_dout.start()
    rows = wq_ref.shape[0]
    packed = [wr_ref[...].astype(F32), g1_ref[...].astype(F32), g2_ref[...].astype(F32)]
    packed = jnp.concatenate(packed + [jnp.zeros((LANE - E - 2, rows), F32)], axis=0)
    own = w_all.at[z, c]
    own[:, : H * HD] = wq_ref[...]
    own[:, H * HD : H * HD + KVH * HD] = wk_ref[...]
    own[:, H * HD + KVH * HD : QKV] = wv_ref[...]
    own[:, QKV:W_O] = packed.T.astype(BF)
    own[:, W_O:] = wo_ref[...]
    meet(peers, 1 + (replicas - 1) + jnp.where(z > 0, 1, 0) + jnp.where(z < chips - 1, 1, 0))

    def part(kind):
        if kind == 0:
            return pl.ds(pl.multiple_of(r * (QKV // replicas), LANE), QKV // replicas)
        if kind == 1:
            return pl.ds(QKV, LANE)
        return pl.ds(pl.multiple_of(W_O + r * (D // replicas), LANE), D // replicas)

    def along(zb, kind, up):
        ref = w_all.at[zb, c, :, part(kind)]
        return make(ref, ref, (z_up if up else z_down).at[kind, zb], z_recv.at[kind, zb], above if up else below)

    def across(zb, kind, d):
        ref = w_all.at[zb, c, :, part(kind)]
        return make(ref, ref, xy_send.at[kind, zb, d], xy_recv.at[kind, zb, r], ((r + d) % replicas, f))

    def wait_across(zb, kind):
        for d in range(1, replicas):
            peer = (r + d) % replicas
            ref = w_all.at[zb, c, :, part(kind)]
            make(ref, ref, xy_send.at[kind, zb, d], xy_recv.at[kind, zb, peer], (peer, f)).wait_recv()

    def to_mate(zb, core, late):
        ref = w_all.at[zb, core, :, pl.ds(W_O, D) if late else pl.ds(0, W_O)]
        return make(ref, ref, mate_send.at[late, zb], mate_recv.at[late, zb], mate)

    def dout_copy(zb, core, way):
        source = do_all.at[zb, core]
        return make(source, do_all.at[zb, core], do_send.at[way, zb], do_recv.at[zb, core], (above, below, mate)[way])

    def both_sides(k, act):
        @pl.when(z >= k)
        def _():
            act(z - k, True)

        @pl.when(z < chips - k)
        def _():
            act(z + k, False)

    def onward(up):
        return z < chips - 1 if up else z > 0

    for kind in range(3):
        both_sides(1, lambda zb, low: along(z, kind, not low).start())
    for late in range(2):
        to_mate(z, c, late).start()

    source = x_ref[...].astype(F32)
    factor = lax.rsqrt(jnp.mean(source * source, axis=1, keepdims=True) + norm_eps)
    lane = lanes_of(tokens)
    low_lane = lane < HD
    row = lax.broadcasted_iota(jnp.int32, (tokens, tokens), 0)
    column = lax.broadcasted_iota(jnp.int32, (tokens, tokens), 1)
    row_at = lax.broadcasted_iota(jnp.int32, (tokens, 1), 0)
    column_at = lax.broadcasted_iota(jnp.int32, (1, tokens), 1)
    row_segment = jnp.zeros((tokens, 1), jnp.int32)
    row_start = jnp.zeros((tokens, 1), jnp.int32)
    column_segment = jnp.zeros((1, tokens), jnp.int32)
    end = jnp.int32(0)
    for j in range(len_ref.shape[1]):
        end = end + len_ref[0, j]
        row_segment += (row_at >= end).astype(jnp.int32)
        row_start = jnp.maximum(row_start, jnp.where(row_at >= end, end, 0))
        column_segment += (column_at >= end).astype(jnp.int32)
    place = (column == row - row_start).astype(F32).astype(BF)
    found = dot(place, table_ref[...])
    found = [found[:, i * LANE : (i + 1) * LANE] for i in range(6)]
    cosines, sines = found[0] + found[1] + found[2], found[3] + found[4] + found[5]
    cos_ref[...] = cosines
    sin_ref[...] = sines

    own_dout.wait()
    for k in range(1, chips):
        for kind in range(3):

            def arrive(zb, low, kind=kind):
                along(zb, kind, low).wait_recv()

                @pl.when(onward(low))
                def _():
                    along(zb, kind, low).start()

                if kind != 1:
                    for d in range(1, replicas):
                        across(zb, kind, d).start()

            both_sides(k, arrive)
        if k == 1:
            both_sides(1, lambda zb, low: dout_copy(z, c, 1 if low else 0).start())
            dout_copy(z, c, 2).start()

    def share(k, late):
        def act(zb, low):
            wait_across(zb, 2 if late else 0)
            to_mate(zb, c, late).start()

        both_sides(k, act)

    def dout_arrive(zb, low):
        dout_copy(zb, c, 0 if low else 1).wait_recv()

        @pl.when(onward(low))
        def _():
            dout_copy(zb, c, 0 if low else 1).start()

        dout_copy(zb, c, 2).start()

    for k in range(1, chips):
        share(k, 0)
    if chips > 1:
        both_sides(1, dout_arrive)
    for k in range(chips):
        to_mate(k, 1 - c, 0).wait_recv()

    def columns(start, size):
        return w_all[:, :, :, start : start + size].reshape(D, size)

    small = columns(QKV, LANE)
    gains = small.astype(F32).T
    gain_one, gain_two = gains[E : E + 1], gains[E + 1 : E + 2]
    normed = (source * factor * gain_one).astype(BF)
    q_all = dot(normed, columns(0, H * HD))
    for g in range(H // 2):
        at = slice(g * LANE, (g + 1) * LANE)
        block = q_all[:, at]
        q_ref[:, at] = (block * cosines + turned(block, lane) * sines).astype(BF)
    kv = dot(normed, columns(H * HD, 2 * KVH * HD))
    for m in range(KVH // 2):
        block = kv[:, m * LANE : (m + 1) * LANE]
        block = block * cosines + turned(block, lane) * sines
        other = pltpu.roll(block, HD, 1)
        kd_ref[:, 2 * m * LANE : (2 * m + 1) * LANE] = jnp.where(low_lane, block, other).astype(BF)
        kd_ref[:, (2 * m + 1) * LANE : (2 * m + 2) * LANE] = jnp.where(low_lane, other, block).astype(BF)
        block = kv[:, KVH * HD + m * LANE : KVH * HD + (m + 1) * LANE]
        other = pltpu.roll(block, HD, 1)
        vd_ref[:, 2 * m * LANE : (2 * m + 1) * LANE] = jnp.where(low_lane, block, other).astype(BF)
        vd_ref[:, (2 * m + 1) * LANE : (2 * m + 2) * LANE] = jnp.where(low_lane, other, block).astype(BF)
    bias = jnp.where((row_segment == column_segment) & (column <= row), 0.0, masked_score)
    bias = jnp.concatenate([bias, bias], axis=0)

    def p_copy(g):
        return pltpu.make_async_copy(p_ref.at[g % 2], p_hbm.at[g], p_sem.at[g % 2])

    for g in range(KVH):
        at = slice(g * LANE, (g + 1) * LANE)
        queries = halves(q_ref[:, at].astype(F32), low_lane).astype(BF)
        scores = dot_nt(queries, kd_ref[:, at]) * score_scale + bias
        shifted = jnp.exp(scores - jnp.max(scores, axis=1, keepdims=True))
        weights = shifted * (1.0 / jnp.sum(shifted, axis=1, keepdims=True))
        if g >= 2:
            p_copy(g - 2).wait()
        p_ref[g % 2] = weights
        p_copy(g).start()
        mixed = dot(weights.astype(BF), vd_ref[:, at])
        o_ref[:, at] = jnp.where(low_lane, mixed[:tokens], mixed[tokens:]).astype(BF)

    if chips > 2:
        both_sides(2, dout_arrive)
    for k in range(1, chips):
        share(k, 1)

    for k in range(chips):
        to_mate(k, 1 - c, 1).wait_recv()
    after = source + residual_scale * dot(o_ref[...], columns(W_O, D))
    h1_ref[...] = after
    factor = lax.rsqrt(jnp.mean(after * after, axis=1, keepdims=True) + norm_eps)
    normed = (after * factor * gain_two).astype(BF)
    n2_ref[...] = normed
    logits = dot(normed, small).T[:E]
    expert = lax.broadcasted_iota(jnp.int32, (E, tokens), 0)
    routed = routes_ref[0:1] == expert
    for j in range(1, TOPK):
        routed |= routes_ref[j : j + 1] == expert
    top = jnp.max(jnp.where(routed, logits, masked_score), axis=0, keepdims=True)
    powers = jnp.where(routed, jnp.exp(logits - top), 0.0)
    gates = powers / jnp.sum(powers, axis=0, keepdims=True)
    gates = jnp.where(routed, gates, -1.0)
    gt_ref[...] = gates
    gd_ref[...] = jnp.concatenate([gates, jnp.full((LANE - E, tokens), -1.0, F32)], axis=0).T

    for k in range(3, chips):
        both_sides(k, dout_arrive)
    for k in range(chips):
        dout_copy(k, 1 - c, 2).wait_recv()
    for g in (KVH - 2, KVH - 1):
        p_copy(g).wait()
    for k in range(chips):
        for late in range(2):
            to_mate(k, c, late).wait_send()
        dout_copy(k, c, 2).wait_send()

        @pl.when((z >= k) & (z < chips - 1))
        def _():
            dout_copy(k, c, 0).wait_send()
            for kind in range(3):
                along(k, kind, True).wait_send()

        @pl.when((z <= k) & (z > 0))
        def _():
            dout_copy(k, c, 1).wait_send()
            for kind in range(3):
                along(k, kind, False).wait_send()

        @pl.when(z != k)
        def _():
            for d in range(1, replicas):
                for kind in (0, 2):
                    across(k, kind, d).wait_send()


def attention_backward(
    x_ref, dout_ref, cos_ref, sin_ref, w_ref, q_ref, kd_ref, vd_ref, p_hbm, o_ref, h1_ref, n2_ref, gd_ref, dx_ref, dgate,
    gin_ref, gw_ref, do_ref, dqkv_ref, p_ref, p_sem,
):
    tokens = x_ref.shape[0]
    lane = lanes_of(tokens)
    low = lane < HD

    def p_copy(g):
        return pltpu.make_async_copy(p_hbm.at[g], p_ref.at[g % 2], p_sem.at[g % 2])

    p_copy(0).start()

    def put(at, value):
        gw_ref[:, :, :, at] = value.astype(BF).reshape(*gw_ref.shape[:3], value.shape[1])

    small = w_ref[:, QKV:W_O].astype(F32).T
    gain_one, gain_two = small[E : E + 1], small[E + 1 : E + 2]
    after = h1_ref[...]
    factor_two = lax.rsqrt(jnp.mean(after * after, axis=1, keepdims=True) + norm_eps)
    gates = jnp.maximum(gd_ref[...], 0.0)
    grad_gates = dgate()
    chosen = gates * (grad_gates - jnp.sum(gates * grad_gates, axis=1, keepdims=True))
    grad_logits = chosen.astype(BF)
    grad_normed = dx_ref[...] + dot_nt(grad_logits, w_ref[:, QKV:W_O])
    scaled = grad_normed * gain_two
    grad_after = dout_ref[...].astype(F32) + (
        factor_two * scaled - after * factor_two**3 * jnp.mean(scaled * after, axis=1, keepdims=True)
    )
    grad_gain_two = jnp.sum(grad_normed * after * factor_two, axis=0, keepdims=True)
    grad_branch = (residual_scale * grad_after).astype(BF)
    put(slice(QKVO - D, QKVO), dot_tn(o_ref[...], grad_branch))
    do_ref[...] = dot_nt(grad_branch, w_ref[:, W_O:]).astype(BF)
    grad_router = dot_tn(n2_ref[...], grad_logits)
    yield

    cosines, sines = cos_ref[...], sin_ref[...]
    key_back, value_back = [], []
    for g in range(KVH):
        at = slice(g * LANE, (g + 1) * LANE)
        queries = halves(q_ref[:, at].astype(F32), low).astype(BF)
        outs = halves(do_ref[:, at].astype(F32), low).astype(BF)
        if g + 1 < KVH:
            p_copy(g + 1).start()
        p_copy(g).wait()
        weights = p_ref[g % 2]
        grad_weights = dot_nt(outs, vd_ref[:, at])
        total = jnp.sum(weights * grad_weights, axis=1, keepdims=True)
        grad_scores = (weights * (grad_weights - total)).astype(BF)
        block = dot(grad_scores, kd_ref[:, at])
        block = jnp.where(low, block[:tokens], block[tokens:]) * score_scale
        dqkv_ref[:, at] = (block * cosines - turned(block, lane) * sines).astype(BF)
        block = dot_tn(grad_scores, queries) * score_scale
        key_back.append(block + pltpu.roll(block, HD, 1))
        block = dot_tn(weights.astype(BF), outs)
        value_back.append(block + pltpu.roll(block, HD, 1))
    for m in range(KVH // 2):
        block = jnp.where(low, key_back[2 * m], key_back[2 * m + 1])
        at = slice(H * HD + m * LANE, H * HD + (m + 1) * LANE)
        dqkv_ref[:, at] = (block * cosines - turned(block, lane) * sines).astype(BF)
        at = slice(H * HD + KVH * HD + m * LANE, H * HD + KVH * HD + (m + 1) * LANE)
        dqkv_ref[:, at] = jnp.where(low, value_back[2 * m], value_back[2 * m + 1]).astype(BF)
    yield

    source = x_ref[...].astype(F32)
    factor_one = lax.rsqrt(jnp.mean(source * source, axis=1, keepdims=True) + norm_eps)
    normed = (source * factor_one * gain_one).astype(BF)
    put(slice(0, QKVO - D), dot_tn(normed, dqkv_ref[...]))
    grad_normed = dot_nt(dqkv_ref[...], w_ref[:, :QKV])
    scaled = grad_normed * gain_one
    grad_vector = factor_one * scaled - source * factor_one**3 * jnp.mean(scaled * source, axis=1, keepdims=True)
    gin_ref[...] = grad_after + grad_vector
    grad_gain_one = jnp.sum(grad_normed * source * factor_one, axis=0, keepdims=True)
    gains = jnp.concatenate([grad_gain_one, grad_gain_two, jnp.zeros((6, D), F32)], axis=0).T
    at = lanes_of(D)
    extra = jnp.where(at == E, gains[:, 0:1], jnp.where(at == E + 1, gains[:, 1:2], grad_router))
    put(slice(QKVO, QKVO + LANE), extra)


def add_rows(target, first, second, rows, step):
    def some(i, carry):
        at = pl.ds(pl.multiple_of(i * step, step), step)
        target[at] = (first[at].astype(F32) + second[at].astype(F32)).astype(target.dtype)
        return carry

    lax.fori_loop(0, rows // step, some, 0)


def back(
    replicas, chips,
    x_ref, dout_ref, cos_ref, sin_ref, h1_ref, n2_ref, gd_ref, gt_ref,
    do_hbm, we_hbm, w_hbm, q_hbm, kd_hbm, vd_hbm, o_hbm, p_hbm,
    gin_ref, out_ref, result_ref, total_ref, ge_hbm, y_core, y_up, y_down, gw_up, gw_down, *rest,
):
    bits = replicas.bit_length() - 1
    roomy = chips <= 4
    arrived, rest = rest[:bits], rest[bits:]
    if not roomy:
        core_ref, from_ref, rest = rest[0], rest[1], rest[2:]
    (ge_ref, n2_all, gt_all, via_ref, pair_ref, dx_ref, dgt_ref, dgt_all, y_ref, gw_core, parts_ref, smalls_ref), rest = rest[:12], rest[12:]
    if roomy:
        core_ref, from_ref, rest = rest[0], rest[1], rest[2:]
    (n2_up, n2_down, n2_mate, n2_recv, gt_up, gt_down, gt_mate, gt_recv,
     core_send, core_recv, far_send, far_recv, pair_send, via_recv, dgt_send, dgt_recv, yc_send, yc_recv,
     do_sem, we_sem, load_sem, stage_sem, ge_sem, p_sem, ar_send, ar_recv, ar_free,
     y_up_send, y_up_recv, y_down_send, y_down_recv, gw_core_sem, gw_up_send, gw_up_recv, gw_down_send, gw_down_recv,
     part_send, part_recv, small_send, small_recv, result_send, result_recv) = rest
    local, tokens, rows = ge_ref.shape[0], x_ref.shape[0], gw_core.shape[1]
    r, f = lax.axis_index("replica"), lax.axis_index("fsdp")
    z, c = f // 2, f % 2
    mate, above, below = (r, z * 2 + 1 - c), (r, f + 2), (r, f - 2)
    make = Copies().make

    load_experts = pltpu.make_async_copy(we_hbm, ge_ref, we_sem.at[0])
    load_experts.start()
    n2_all[z, c] = n2_ref[...]
    gt_all[z, c] = gt_ref[...]
    peers = [(True, mate)]
    for k in range(1, chips):
        to = (z + k) % chips
        peers += [(True, (r, to * 2 + c)), (True, (r, to * 2 + 1 - c))]
    peers += [(True, ((r + d) % replicas, f)) for d in range(1, replicas)]
    meet(peers, len(peers))

    def bit_of(b):
        return (r // (1 << b)) % 2

    def partner(b):
        return (r + (1 - 2 * bit_of(b)) * (1 << b), f)

    stages = {}

    def landed(ref, name):
        stage, sem = stages[name]
        if ref.shape != stage.shape:
            stage = stage.at[pl.ds(0, ref.shape[0])]
        copy = pltpu.make_async_copy(ref, stage, sem)
        copy.start()
        copy.wait()
        return stage

    def halving(e):
        size = ge_ref.shape[1] // bits
        orders = [[(g + k) % bits for k in range(bits)] for g in range(bits)]
        starts = [[] for _ in range(bits)]
        for g in range(bits):
            at = g * size
            for k in range(bits):
                starts[g].append(at)
                at = at + bit_of(orders[g][k]) * (size >> (k + 1))
            starts[g].append(at)

        def region(g, k):
            half = size >> (k + 1)
            return ge_ref.at[e, pl.ds(pl.multiple_of(starts[g][k + 1], half), half)]

        def exchange(g, k):
            half, job = size >> (k + 1), e * bits + g
            give = pl.multiple_of(starts[g][k] + (1 - bit_of(orders[g][k])) * half, half)
            return make(
                ge_ref.at[e, pl.ds(give, half)], arrived[k].at[job], ar_send.at[job, k], ar_recv.at[job, k],
                partner(orders[g][k]),
            )

        def spread(g, k):
            job, ref = e * bits + g, region(g, k)
            return make(ref, ref, ar_send.at[job, bits + k], ar_recv.at[job, bits + k], partner(orders[g][k]))

        def spread_once_free(g, k):
            pl.semaphore_wait(ar_free.at[e * bits + g, k], 1)
            spread(g, k).start()

        yield
        for g in range(bits):
            exchange(g, 0).start()
        yield
        for k in range(bits):
            half = size >> (k + 1)
            for g in range(bits):
                job = e * bits + g
                exchange(g, k).wait_recv()
                own = region(g, k)
                add_rows(own, own, landed(arrived[k].at[job], "halves"), half, min(half, 64))
                if k < bits - 1:
                    exchange(g, k + 1).start()
                exchange(g, k).wait_send()
                pl.semaphore_signal(
                    ar_free.at[job, k], inc=1, device_id=partner(orders[g][k]), device_id_type=pl.DeviceIdType.MESH
                )
                if k == bits - 1:
                    spread_once_free(g, k)
            yield
        for k in range(bits - 1, -1, -1):
            for g in range(bits):
                spread(g, k).wait_recv()
                if k > 0:
                    spread_once_free(g, k - 1)
            yield
        for g in range(bits):
            for k in range(bits):
                spread(g, k).wait_send()
        pltpu.make_async_copy(ge_ref.at[e], ge_hbm.at[e], ge_sem.at[e]).start()

    sums = [halving(e) for e in range(local)] if bits else []
    first, last = sums[:1], sums[1:]
    for process in sums:
        next(process)

    def pass_on(zb, how):
        to = {"up": above, "down": below, "mate": mate}[how]
        sems = {"up": (n2_up, gt_up), "down": (n2_down, gt_down), "mate": (n2_mate, gt_mate)}[how]
        return [
            make(ref.at[zb, c], ref.at[zb, c], sem.at[zb], recv.at[zb, c], to)
            for ref, sem, recv in ((gt_all, sems[1], gt_recv), (n2_all, sems[0], n2_recv))
        ]

    def got(zb, core):
        for ref, sem, recv in ((gt_all, gt_mate, gt_recv), (n2_all, n2_mate, n2_recv)):
            make(ref.at[zb, core], ref.at[zb, core], sem.at[zb], recv.at[zb, core], mate).wait_recv()

    def start(copies):
        for copy in copies:
            copy.start()

    @pl.when(z < chips - 1)
    def _():
        start(pass_on(z, "up"))

    @pl.when(z > 0)
    def _():
        start(pass_on(z, "down"))

    start(pass_on(z, "mate"))
    inner = jnp.minimum(z, chips - 1 - z)

    def place(t):
        k = (t + 1) // 2
        near = jnp.where(t % 2 == 1, z - k, z + k)
        return jnp.where(t <= 2 * inner, near, jnp.where(2 * z < chips - 1, t, chips - 1 - t))

    def far(zc):
        return jnp.where(zc > z, zc - z, z - zc)

    def side_of(zc):
        return jnp.where(zc > z, 1, 0)

    def relay(k, low, high):
        @pl.when(low)
        def _():
            got(z - k, c)

            @pl.when(z < chips - 1)
            def _():
                start(pass_on(z - k, "up"))

            start(pass_on(z - k, "mate"))

        @pl.when(high)
        def _():
            got(z + k, c)

            @pl.when(z > 0)
            def _():
                start(pass_on(z + k, "down"))

            start(pass_on(z + k, "mate"))

    def early(t):
        return (t >= 2) & (t % 2 == 0) & (t <= 2 * inner) & (t < chips - 1)

    def pair_copy(side):
        owner = z + 2 * side - 1
        return make(pair_ref.at[side], from_ref.at[z], pair_send.at[side], far_recv.at[z], (r, owner * 2 + c))

    def experts_and_sums(do_buf, xs_ref, dye_ref, dgu_ref, hx_ref, dxp_ref, yps_ref, core_stage):
        stages["core"] = (core_stage, stage_sem.at[0])
        before = lax.broadcasted_iota(jnp.int32, (tokens, tokens), 0) < lax.broadcasted_iota(jnp.int32, (tokens, tokens), 1)
        before = before.astype(F32).astype(BF)
        slot_index = lax.broadcasted_iota(jnp.int32, (CAP, tokens), 0).astype(F32)
        pair = 2 * CAP

        def do_copy(zc, slot):
            return pltpu.make_async_copy(do_hbm.at[zc], do_buf.at[slot], do_sem.at[slot])

        def core_copy(zc, slot, t):
            return make(dxp_ref.at[slot, 1 - c], core_ref.at[zc], core_send.at[t], core_recv.at[zc], mate)

        def y_copy(zc, slot, t):
            return make(yps_ref.at[slot], y_core.at[zc], yc_send.at[t], yc_recv.at[zc], mate)

        def via_copy(zc, slot, t):
            side = side_of(zc)
            return make(
                dxp_ref.at[slot, c], via_ref.at[side], far_send.at[t], via_recv.at[side], (r, (z + 2 * side - 1) * 2 + c)
            )

        def far_copy(zc, slot, t):
            return make(dxp_ref.at[slot, c], from_ref.at[z], far_send.at[t], far_recv.at[z], (r, zc * 2 + c))

        def dgt_copy(zc, core, t):
            return make(dgt_ref.at[t, core], dgt_all.at[f], dgt_send.at[t, core], dgt_recv.at[f], (r, zc * 2 + core))

        def free_slot(t, slot):
            core_copy(z, slot, t).wait_send()
            y_copy(z, slot, t).wait_send()

            @pl.when(far(place(t)) >= 2)
            def _():
                far_copy(z, slot, t).wait_send()

        do_copy(z, 0).start()

        def chunk(t, carry):
            zc = place(t)
            slot = t % 2
            k = far(zc)
            both = (t % 2 == 1) & (t <= 2 * inner)
            single = (t > 2 * inner) & jnp.logical_not(early(t - 1))
            relay(k, both | (single & (zc < z)), both | (single & (zc > z)))
            got(zc, 1 - c)

            @pl.when(t < chips - 1)
            def _():
                do_copy(place(t + 1), 1 - slot).start()

            do_copy(zc, slot).wait()

            @pl.when(t == 0)
            def _():
                load_experts.wait()

            @pl.when(t >= 2)
            def _():
                free_slot(t - 2, slot)

            picks, gates, dms = [], [], []
            at_chip = pl.multiple_of(zc * pair, 16)
            for core in range(2):
                mine = [gt_all[zc, core, pl.ds(f * local + i, 1), :] for i in range(local)]
                mine = jnp.concatenate(mine, axis=0) if local > 1 else mine[0]
                rank = jnp.where(mine >= 0.0, dot((mine >= 0.0).astype(F32).astype(BF), before), -1.0)
                chosen = [slot_index == rank[i : i + 1] for i in range(local)]
                gates.append([jnp.sum(jnp.where(chosen[i], mine[i : i + 1], 0.0), axis=1, keepdims=True) for i in range(local)])
                picks.append([one.astype(F32) for one in chosen])
                pick = jnp.concatenate([one.astype(BF) for one in picks[core]], axis=0)
                taken = dot(pick, n2_all[zc, core]).astype(BF)
                grads = dot(pick, do_buf[slot, core]) * residual_scale
                dms.append(grads)
                at = pl.ds(pl.multiple_of(at_chip + core * CAP, 16), CAP)
                for i in range(local):
                    part = slice(i * CAP, (i + 1) * CAP)
                    xs_ref[i, at] = taken[part]
                    dye_ref[i, at] = (gates[core][i] * grads[part]).astype(BF)
            at = pl.ds(at_chip, pair)
            mades, backs, values = [], [], []
            for i in range(local):
                slots = xs_ref[i, at]
                gate_pre = dot_nt(slots, ge_ref[i, :FF])
                up_pre = dot_nt(slots, ge_ref[i, FF : 2 * FF])
                grad_act = dot_nt(dye_ref[i, at], ge_ref[i, 2 * FF :])
                sigmoid = 1.0 / (1.0 + jnp.exp(-gate_pre))
                silu = gate_pre * sigmoid
                act = (silu * up_pre).astype(BF)
                hx_ref[i, at] = act
                grad_gate = (grad_act * up_pre * (sigmoid * (1.0 + gate_pre * (1.0 - sigmoid)))).astype(BF)
                grad_up = (grad_act * silu).astype(BF)
                dgu_ref[i, at, :FF] = grad_gate
                dgu_ref[i, at, FF:] = grad_up
                backs.append((dot(grad_gate, ge_ref[i, :FF]) + dot(grad_up, ge_ref[i, FF : 2 * FF])).astype(BF))
                made = dot(act, ge_ref[i, 2 * FF :]).astype(BF).astype(F32)
                mades.append(made)
                for core in range(2):
                    part = slice(core * CAP, (core + 1) * CAP)
                    value = jnp.sum(dms[core][i * CAP : (i + 1) * CAP] * made[part], axis=1, keepdims=True)
                    values.append(jnp.sum(picks[core][i] * value, axis=0, keepdims=True))
            for core in range(2):
                pick = jnp.concatenate([one.astype(BF) for one in picks[core]], axis=0)
                part = slice(core * CAP, (core + 1) * CAP)
                sent = jnp.concatenate([backs[i][part] for i in range(local)], axis=0)
                dxp_ref[slot, core] = dot_tn(pick, sent).astype(BF)
                for i in range(local):
                    dgt_ref[t, core, i : i + 1] = values[2 * i + core]
            core_copy(zc, slot, t).start()
            for core in range(2):

                @pl.when((t > 0) | (c != core))
                def _():
                    dgt_copy(zc, core, t).start()

            @pl.when(early(t))
            def _():
                k_next = t // 2 + 1
                relay(k_next, z >= k_next, z + k_next < chips)

            for core in range(2):
                pick = jnp.concatenate([one.astype(BF) for one in picks[core]], axis=0)
                part = slice(core * CAP, (core + 1) * CAP)
                sent = jnp.concatenate([(gates[core][i] * mades[i][part]).astype(BF) for i in range(local)], axis=0)
                mixed = dot_tn(pick, sent).astype(BF)

                @pl.when(c == core)
                def _():
                    y_ref[zc] = mixed

                @pl.when(c != core)
                def _():
                    yps_ref[slot] = mixed

            y_copy(zc, slot, t).start()
            core_copy(zc, slot, t).wait_recv()
            there = core_ref.at[zc] if roomy else landed(core_ref.at[zc], "core")
            own = dxp_ref.at[slot, c]

            @pl.when(k == 0)
            def _():
                dx_ref[...] = own[...].astype(F32) + there[...].astype(F32)

            @pl.when(k == 1)
            def _():
                side = side_of(zc)
                add_rows(pair_ref.at[side], own, there, tokens, 64)

                @pl.when((z == 0) | (z == chips - 1))
                def _():
                    pair_copy(side).start()

            @pl.when(k >= 2)
            def _():
                add_rows(own, own, there, tokens, 64)

                @pl.when(k == 2)
                def _():
                    via_copy(zc, slot, t).start()

                @pl.when(k > 2)
                def _():
                    far_copy(zc, slot, t).start()

            return carry

        lax.fori_loop(0, chips, chunk, 0)

        @pl.when((z > 0) & (z < chips - 1))
        def _():
            for side in range(2):
                make(via_ref.at[side], via_ref.at[side], far_send.at[0], via_recv.at[side], mate).wait_recv()
                add_rows(pair_ref.at[side], pair_ref.at[side], via_ref.at[side], tokens, 64)
                pair_copy(side).start()

        for i in range(local):
            ge_ref[i, : 2 * FF] = dot_tn(dgu_ref[i], xs_ref[i]).astype(BF)
            ge_ref[i, 2 * FF :] = dot_tn(hx_ref[i], dye_ref[i]).astype(BF)
            if bits:
                next(sums[i])
        for t in range(max(chips - 2, 0), chips):
            free_slot(t, t % 2)
        for t in range(chips):
            for core in range(2):

                @pl.when((t > 0) | (c != core))
                def _():
                    dgt_copy(z, core, t).wait_send()

    slots = chips * 2 * CAP
    pl.run_scoped(
        experts_and_sums,
        pltpu.VMEM((2, 2, tokens, D), BF), pltpu.VMEM((local, slots, D), BF), pltpu.VMEM((local, slots, D), BF),
        pltpu.VMEM((local, slots, 2 * FF), BF), pltpu.VMEM((local, slots, FF), BF), pltpu.VMEM((2, 2, tokens, D), BF),
        pltpu.VMEM((2, tokens, D), BF), pltpu.VMEM((16 if roomy else tokens, D), BF),
    )

    def line(own, size, step, core_add, name, up_ref, down_ref, up_send, up_recv, down_send, down_recv):
        def add_block(block, other):
            add_rows(own(block), own(block), landed(other.at[block], name), size, step)

        def send(block, up):
            there, send_sem, recv_sem = (up_ref, up_send, up_recv) if up else (down_ref, down_send, down_recv)
            return make(own(block), there.at[block], send_sem.at[block], recv_sem.at[block], above if up else below)

        nearby = [k for both in zip(range(chips - 1, -1, -1), range(chips)) for k in both][:chips]
        for k in nearby:
            core_add(k)

            @pl.when((z == 0) & (k > 0))
            def _():
                send(k, True).start()

            @pl.when((z == chips - 1) & (k < chips - 1))
            def _():
                send(k, False).start()

        yield
        for k in range(chips - 2):
            owner = chips - 1 - k

            @pl.when((z > 0) & (z < owner))
            def _():
                send(owner, True).wait_recv()
                add_block(owner, up_ref)
                send(owner, True).start()

            @pl.when((z < chips - 1) & (z > k))
            def _():
                send(k, False).wait_recv()
                add_block(k, down_ref)
                send(k, False).start()

            yield

        @pl.when(z > 0)
        def _():
            send(z, True).wait_recv()
            add_block(z, up_ref)

        @pl.when(z < chips - 1)
        def _():
            send(z, False).wait_recv()
            add_block(z, down_ref)

        for k in range(chips):

            @pl.when(z < k)
            def _():
                send(k, True).wait_send()

            @pl.when(z > k)
            def _():
                send(k, False).wait_send()

    def mixture():
        def core_add(k):
            make(y_core.at[k], y_core.at[k], yc_send.at[k], yc_recv.at[k], mate).wait_recv()
            add_rows(y_ref.at[k], y_ref.at[k], landed(y_core.at[k], "tokens"), tokens, 32)

        yield from line(
            lambda k: y_ref.at[k], tokens, 32, core_add, "tokens", y_up, y_down, y_up_send, y_up_recv, y_down_send,
            y_down_recv,
        )
        out_ref[...] = (h1_ref[...] + residual_scale * y_ref[z].astype(F32)).astype(BF)

    def attention(w_ref, q_ref, kd_ref, vd_ref, o_ref, p_ref, do_ref, dqkv_ref, gw_ref, halves_stage, tokens_stage, rows_stage):
        stages["halves"] = (halves_stage, stage_sem.at[1])
        stages["tokens"] = (tokens_stage, stage_sem.at[2])
        stages["rows"] = (rows_stage, stage_sem.at[3])
        loads = [
            pltpu.make_async_copy(source, target, load_sem.at[i])
            for i, (source, target) in enumerate(
                ((w_hbm, w_ref), (o_hbm, o_ref), (q_hbm, q_ref), (kd_hbm, kd_ref), (vd_hbm, vd_ref))
            )
        ]
        start(loads)

        def projection():
            crossing = make(gw_ref.at[:, 1 - c], gw_core, gw_core_sem.at[0], gw_core_sem.at[1], mate)
            crossing.start()
            yield
            crossing.wait_recv()

            def own(k):
                return gw_ref.at[k, c]

            yield from line(
                own, rows, 16, lambda k: add_rows(own(k), own(k), gw_core.at[k], rows, 16), "rows", gw_up, gw_down,
                gw_up_send, gw_up_recv, gw_down_send, gw_down_recv,
            )
            crossing.wait_send()
            wide = QKVO // replicas

            def columns(part):
                return pl.ds(pl.multiple_of(part * wide, LANE), wide)

            mine = gw_ref.at[z, c]

            def part_copy(d):
                to = (r + d) % replicas
                return make(mine.at[:, columns(to)], parts_ref.at[r], part_send.at[d], part_recv.at[r], (to, f))

            def small_copy(d):
                to = (r + d) % replicas
                return make(mine.at[:, pl.ds(QKVO, LANE)], smalls_ref.at[r], small_send.at[d], small_recv.at[r], (to, f))

            for d in range(1, replicas):
                part_copy(d).start()
                small_copy(d).start()
            parts_ref[r] = mine[:, columns(r)]
            smalls_ref[r] = mine[:, pl.ds(QKVO, LANE)]
            yield
            for d in range(1, replicas):
                peer = (r + d) % replicas
                make(parts_ref.at[peer], parts_ref.at[peer], part_send.at[d], part_recv.at[peer], (peer, f)).wait_recv()
                make(smalls_ref.at[peer], smalls_ref.at[peer], small_send.at[d], small_recv.at[peer], (peer, f)).wait_recv()
            total = parts_ref[0].astype(F32)
            small = smalls_ref[0].astype(F32)
            for k in range(1, replicas):
                total = total + parts_ref[k].astype(F32)
                small = small + smalls_ref[k].astype(F32)
            result_ref[r] = total.astype(BF)
            total_ref[...] = small

            def result_copy(d):
                to = (r + d) % replicas
                return make(result_ref.at[r], result_ref.at[r], result_send.at[d], result_recv.at[r], (to, f))

            for d in range(1, replicas):
                result_copy(d).start()
            yield
            for d in range(1, replicas):
                peer = (r + d) % replicas
                make(
                    result_ref.at[peer], result_ref.at[peer], result_send.at[d], result_recv.at[peer], (peer, f)
                ).wait_recv()
            for d in range(1, replicas):
                part_copy(d).wait_send()
                small_copy(d).wait_send()
                result_copy(d).wait_send()

        moe, grads = [mixture()], [projection()]

        def go(*turns):
            for turn in turns:
                for process in turn:
                    next(process, None)

        def dgate():
            found = [dgt_all[k, :local] for k in range(2 * chips)]
            return jnp.concatenate(found + [jnp.zeros((LANE - E, tokens), F32)], axis=0).T

        for k in range(chips):

            @pl.when((z == k + 1) | (z + 1 == k) | (z > k + 2) | (z + 2 < k))
            def _():
                make(from_ref.at[k], from_ref.at[k], far_send.at[0], far_recv.at[k], mate).wait_recv()
                there = from_ref.at[k] if roomy else landed(from_ref.at[k], "tokens")
                add_rows(dx_ref, dx_ref, there, tokens, 64)

        for k in range(2 * chips):

            @pl.when(f == k)
            def _():
                for core in range(2):

                    @pl.when(c == core)
                    def _():
                        dgt_all[k] = dgt_ref[0, core]

            @pl.when(f != k)
            def _():
                make(dgt_all.at[k], dgt_all.at[k], dgt_send.at[0, 0], dgt_recv.at[k], mate).wait_recv()

        go(moe)
        for load in loads:
            load.wait()
        backward = attention_backward(
            x_ref, dout_ref, cos_ref, sin_ref, w_ref, q_ref, kd_ref, vd_ref, p_hbm, o_ref, h1_ref, n2_ref, gd_ref, dx_ref,
            dgate, gin_ref, gw_ref, do_ref, dqkv_ref, p_ref, p_sem,
        )
        next(backward)
        go(first)
        next(backward)
        go(moe)
        next(backward, None)
        go(grads, last, moe, grads, first, moe, last, first, grads, last, grads, first, grads, last, grads, grads)
        go(*[moe + grads + sums] * (2 * chips + 2 * bits + 4))

    size = ge_ref.shape[1] // max(bits, 1)
    pl.run_scoped(
        attention,
        pltpu.VMEM((D, W_O + D), BF), pltpu.VMEM((tokens, D), BF), pltpu.VMEM((tokens, D), BF), pltpu.VMEM((tokens, D), BF),
        pltpu.VMEM((tokens, D), BF), pltpu.VMEM((2, 2 * tokens, tokens), F32), pltpu.VMEM((tokens, D), BF),
        pltpu.VMEM((tokens, QKV), BF), pltpu.VMEM((chips, 2, rows, QKVO + LANE), BF), pltpu.VMEM((size // 2, D), BF),
        pltpu.VMEM((tokens, D), BF), pltpu.VMEM((rows, QKVO + LANE), BF),
    )

    for e in range(local):
        copy = pltpu.make_async_copy(ge_ref.at[e], ge_hbm.at[e], ge_sem.at[e])
        if not bits:
            copy.start()
        copy.wait()
    for side in range(2):

        @pl.when(z > 0 if side == 0 else z < chips - 1)
        def _():
            pair_copy(side).wait_send()

    for k in range(chips):

        @pl.when((z >= k) & (z < chips - 1))
        def _():
            for copy in pass_on(k, "up"):
                copy.wait_send()

        @pl.when((z <= k) & (z > 0))
        def _():
            for copy in pass_on(k, "down"):
                copy.wait_send()

        for copy in pass_on(k, "mate"):
            copy.wait_send()


def finish(gexp_ref, result_ref, total_ref, gin_ref, out_ref, *outs):
    layer, grad_in, gains_one, query, key, value, output, gains_two, router, expert = outs
    expert[...] = gexp_ref[...].astype(F32)

    @pl.when(pl.program_id(0) == 0)
    def _():
        layer[...] = out_ref[...]
        grad_in[...] = gin_ref[...]
        wide = result_ref.shape[2]
        start = 0
        for ref in (query, key, value, output):
            for at in range(0, ref.shape[1], LANE):
                part, column = divmod(start + at, wide)
                ref[:, at : at + LANE] = result_ref[part, :, column : column + LANE].astype(F32)
            start += ref.shape[1]
        small = total_ref[...].T
        router[...] = small[:E]
        gains_one[...] = small[E : E + 1]
        gains_two[...] = small[E + 1 : E + 2]


def call(kernel, out_shape, args, scratch=(), outside=0, out_outside=0, **params):
    spaces = [pltpu.SMEM if a.dtype == jnp.int32 and a.size <= 16 else pltpu.VMEM for a in args]
    spaces[len(args) - outside :] = [pl.ANY] * outside
    return pl.pallas_call(
        kernel,
        out_shape=out_shape,
        in_specs=[pl.BlockSpec(memory_space=space) for space in spaces],
        out_specs=[
            pl.BlockSpec(memory_space=pltpu.VMEM if i < len(out_shape) - out_outside else pl.ANY)
            for i in range(len(out_shape))
        ],
        scratch_shapes=list(scratch),
        compiler_params=pltpu.CompilerParams(
            vmem_limit_bytes=VMEM_LIMIT, has_side_effects="collective_id" in params, **params
        ),
    )(*args)


def shape(dims, dtype):
    return jax.ShapeDtypeStruct(dims, dtype)


def make_body(mesh):
    group, replicas = mesh.shape["fsdp"], mesh.shape["replica"]
    local = E // group

    def body(
        hidden_in, seq_lengths, routes, norm1_gain, w_query, w_key, w_value, w_output, norm2_gain, w_router,
        expert_weights, out_cotangent,
    ):
        tokens = hidden_in.shape[0]
        rows = w_query.shape[0]
        chips = group // 2
        dma = pltpu.SemaphoreType.DMA
        weights, q, kd, vd, o, h1, n2, gd, gt, cosines, sines, p, dout_all = call(
            functools.partial(front, replicas, chips),
            (
                shape((chips, 2, rows, W_O + D), BF), shape((tokens, D), BF), shape((tokens, D), BF),
                shape((tokens, D), BF), shape((tokens, D), BF), shape((tokens, D), F32), shape((tokens, D), BF),
                shape((tokens, LANE), F32), shape((E, tokens), F32), shape((tokens, LANE), F32),
                shape((tokens, LANE), F32), shape((KVH, 2 * tokens, tokens), F32), shape((chips, 2, tokens, D), BF),
            ),
            (
                hidden_in, seq_lengths, routes.T, rope_table(tokens), w_query, w_key, w_value, w_output, w_router.T,
                norm1_gain[None], norm2_gain[None], out_cotangent,
            ),
            [
                pltpu.VMEM((2, 2 * tokens, tokens), F32), dma((2,)), dma((1,)), dma((3, chips)), dma((3, chips)),
                dma((3, chips)), dma((3, chips, replicas)), dma((3, chips, replicas)), dma((2, chips)),
                dma((2, chips)), dma((3, chips)), dma((chips, 2)),
            ],
            out_outside=2,
            collective_id=2,
        )
        weights = weights.reshape(D, W_O + D)
        bits = replicas.bit_length() - 1
        size = 3 * FF // bits if bits else 0
        width = QKVO + LANE
        roomy = chips <= 4
        landing = [shape((local * bits, size >> (k + 1), D), BF) for k in range(bits)]
        blocks = [shape((chips, tokens, D), BF)] * 2
        if not roomy:
            landing += blocks
        landing_sems = [dma((chips,))] * 4
        outs = call(
            functools.partial(back, replicas, chips),
            [
                shape((tokens, D), F32), shape((tokens, D), BF), shape((replicas, rows, QKVO // replicas), BF),
                shape((rows, LANE), F32), shape((local, 3 * FF, D), BF),
            ]
            + [shape((chips, tokens, D), BF)] * 3 + [shape((chips, rows, width), BF)] * 2 + landing,
            (
                hidden_in, out_cotangent, cosines, sines, h1, n2, gd, gt,
                dout_all, expert_weights, weights, q, kd, vd, o, p,
            ),
            [
                pltpu.VMEM((local, 3 * FF, D), BF), pltpu.VMEM((chips, 2, tokens, D), BF),
                pltpu.VMEM((chips, 2, E, tokens), F32), pltpu.VMEM((2, tokens, D), BF), pltpu.VMEM((2, tokens, D), BF),
                pltpu.VMEM((tokens, D), F32), pltpu.VMEM((chips, 2, 8, tokens), F32), pltpu.VMEM((group, 8, tokens), F32),
                pltpu.VMEM((chips, tokens, D), BF), pltpu.VMEM((chips, rows, width), BF),
                pltpu.VMEM((replicas, rows, QKVO // replicas), BF), pltpu.VMEM((replicas, rows, LANE), BF),
            ]
            + ([pltpu.VMEM(b.shape, b.dtype) for b in blocks] if roomy else [])
            + ([dma((chips,))] * 3 + [dma((chips, 2))]) * 2 + [dma((chips,))] * 4 + [dma((2,))] * 2
            + [dma((chips, 2)), dma((group,)), dma((chips,)), dma((chips,))]
            + [dma((2,)), dma((1,)), dma((5,)), dma((4,)), dma((local,)), dma((2,))]
            + [dma((max(local * bits, 1), max(2 * bits, 1)))] * 2
            + [pltpu.SemaphoreType.REGULAR((max(local * bits, 1), max(bits, 1)))]
            + landing_sems + [dma((2,))] + landing_sems + [dma((replicas,))] * 6,
            outside=8,
            out_outside=6 + len(landing),
            collective_id=0,
        )
        grad_in, layer_out, result, total, grad_experts = outs[:5]
        steps = 8
        block = local * 3 * FF // steps
        fixed = [
            shape((tokens, D), BF), shape((tokens, D), F32), shape((1, rows), F32), shape((rows, H * HD), F32),
            shape((rows, KVH * HD), F32), shape((rows, KVH * HD), F32), shape((rows, D), F32), shape((1, rows), F32),
            shape((E, rows), F32),
        ]

        def still(a):
            return pl.BlockSpec(a.shape, lambda i: (0, 0))

        expert_block = pl.BlockSpec((block, D), lambda i: (i, 0))
        outs = pl.pallas_call(
            finish,
            grid=(steps,),
            in_specs=[
                expert_block, pl.BlockSpec(result.shape, lambda i: (0, 0, 0)), still(total), still(grad_in), still(layer_out)
            ],
            out_specs=[still(a) for a in fixed] + [expert_block],
            out_shape=fixed + [shape((local * 3 * FF, D), F32)],
            compiler_params=pltpu.CompilerParams(vmem_limit_bytes=VMEM_LIMIT),
        )(grad_experts.reshape(local * 3 * FF, D), result, total, grad_in, layer_out)
        return (
            outs[0], outs[1], outs[2][0], outs[3], outs[4], outs[5], outs[6], outs[7][0], outs[8].T,
            outs[9].reshape(local, 3 * FF, D),
        )

    return body


def solution(mesh):
    tokens, weights = P(("replica", "fsdp"), None), P("fsdp", None)
    return jax.shard_map(
        make_body(mesh),
        mesh=mesh,
        in_specs=(
            tokens, tokens, tokens, P("fsdp"), weights, weights, weights, weights, P("fsdp"), weights,
            P("fsdp", None, None), tokens,
        ),
        out_specs=(
            tokens, tokens, P("fsdp"), weights, weights, weights, weights, P("fsdp"), weights, P("fsdp", None, None),
        ),
        check_vma=False,
    )
```

time: 327 us -> 319 us (0.976)
  local copies, waits for them, and re-layouts: 6.47 us -> 0 us
  Pallas kernels: 317 us -> 313 us
    pallas_call x2 -> x1, Pallas kernels: 98.2 us -> 10.7 us  [body(): pl.pallas_call(finish, grid=(steps,), in_specs=[expert_block, pl.BlockSpe...]
    pallas_call x2, Pallas kernels: 219 us -> 302 us  [call(): pl.pallas_call(kernel, out_shape=out_shape, in_specs=[pl.BlockSpec(memory...]
    unnamed x8 -> x0, local copies, waits for them, and re-layouts: 6.47 us -> none
where the time goes in v6:
time: 319 us; the launch traced here: 314 us
  Pallas kernels  313 us (98%)
    pallas_call x2, Pallas kernels, call(): pl.pallas_call(kernel, out_shape=out_shape, in_specs=[pl.BlockSpec(memory...  302 us
    pallas_call x1, Pallas kernels, body(): pl.pallas_call(finish, grid=(steps,), in_specs=[expert_block, pl.BlockSpe...  10.7 us

profile of v6, /device:TPU:10, one launch (start us, length us, event | category | flops | bytes accessed | tf_op | source)
XLA Modules:
  0.0 313.8 jit_solution(10857049134283334951)
XLA Ops:
  0.6 58.2 %shard_map.204 = (bf16[4,2,128,3200]{3,2,1,0:T(8,128)(2,1)}, bf16[256,1024]{1,0:T(8,128)(2,1)}, bf16[256,1024]{1,0:T(8,128)(2,1)}, bf16[256,1024]{1,0:T(8,128)(2...) custom-call(bf16[256,1024]{1,0:T(8,128)(2,1)} %x_ref.3, ...), custom_call_target="tpu_custom_call" | custom-call | tf_op jit(solution)/shard_map/pallas_call | solution.py:1056
  58.9 244.2 %shard_map.205 = (f32[256,1024]{1,0:T(8,128)}, bf16[256,1024]{1,0:T(8,128)(2,1)}, bf16[4,128,768]{2,1,0:T(8,128)(2,1)}, f32[128,128]{1,0:T(8,128)}, bf16[2,1536,...) custom-call(bf16[256,1024]{1,0:T(8,128)(2,1)} %x_ref.3, ...), custom_call_target="tpu_custom_call" | custom-call | tf_op jit(solution)/shard_map/pallas_call | solution.py:1056
  303.1 10.7 %shard_map.206 = (bf16[256,1024]{1,0:T(8,128)(2,1)}, f32[256,1024]{1,0:T(8,128)}, f32[1,128]{1,0:T(1,128)}, f32[128,1024]{1,0:T(8,128)}, f32[128,512]{1,0:T(8,12...) custom-call(bf16[3072,1024]{1,0:T(8,128)(2,1)} %bitcast.11, ...), custom_call_target="tpu_custom_call" | custom-call | tf_op jit(solution)/shard_map/pallas_call | solution.py:1159

commit v7 on v6

--- a/solution.py
+++ b/solution.py
@@ -331,7 +331,7 @@
 
 def attention_backward(
     x_ref, dout_ref, cos_ref, sin_ref, w_ref, q_ref, kd_ref, vd_ref, p_hbm, o_ref, h1_ref, n2_ref, gd_ref, dx_ref, dgate,
-    gin_ref, gw_ref, do_ref, dqkv_ref, p_ref, p_sem,
+    gin_ref, gq_ref, go_ref, do_ref, dqkv_ref, p_ref, p_sem,
 ):
     tokens = x_ref.shape[0]
     lane = lanes_of(tokens)
@@ -342,8 +342,8 @@
 
     p_copy(0).start()
 
-    def put(at, value):
-        gw_ref[:, :, :, at] = value.astype(BF).reshape(*gw_ref.shape[:3], value.shape[1])
+    def put(ref, at, value):
+        ref[:, :, :, at] = value.astype(BF).reshape(*ref.shape[:3], value.shape[1])
 
     small = w_ref[:, QKV:W_O].astype(F32).T
     gain_one, gain_two = small[E : E + 1], small[E + 1 : E + 2]
@@ -360,7 +360,7 @@
     )
     grad_gain_two = jnp.sum(grad_normed * after * factor_two, axis=0, keepdims=True)
     grad_branch = (residual_scale * grad_after).astype(BF)
-    put(slice(QKVO - D, QKVO), dot_tn(o_ref[...], grad_branch))
+    put(go_ref, slice(0, D), dot_tn(o_ref[...], grad_branch))
     do_ref[...] = dot_nt(grad_branch, w_ref[:, W_O:]).astype(BF)
     grad_router = dot_tn(n2_ref[...], grad_logits)
     yield
@@ -396,7 +396,7 @@
     source = x_ref[...].astype(F32)
     factor_one = lax.rsqrt(jnp.mean(source * source, axis=1, keepdims=True) + norm_eps)
     normed = (source * factor_one * gain_one).astype(BF)
-    put(slice(0, QKVO - D), dot_tn(normed, dqkv_ref[...]))
+    put(gq_ref, slice(0, QKV), dot_tn(normed, dqkv_ref[...]))
     grad_normed = dot_nt(dqkv_ref[...], w_ref[:, :QKV])
     scaled = grad_normed * gain_one
     grad_vector = factor_one * scaled - source * factor_one**3 * jnp.mean(scaled * source, axis=1, keepdims=True)
@@ -405,7 +405,7 @@
     gains = jnp.concatenate([grad_gain_one, grad_gain_two, jnp.zeros((6, D), F32)], axis=0).T
     at = lanes_of(D)
     extra = jnp.where(at == E, gains[:, 0:1], jnp.where(at == E + 1, gains[:, 1:2], grad_router))
-    put(slice(QKVO, QKVO + LANE), extra)
+    put(gq_ref, slice(QKV, W_O), extra)
 
 
 def add_rows(target, first, second, rows, step):
@@ -421,22 +421,24 @@
     replicas, chips,
     x_ref, dout_ref, cos_ref, sin_ref, h1_ref, n2_ref, gd_ref, gt_ref,
     do_hbm, we_hbm, w_hbm, q_hbm, kd_hbm, vd_hbm, o_hbm, p_hbm,
-    gin_ref, out_ref, result_ref, total_ref, ge_hbm, y_core, y_up, y_down, gw_up, gw_down, *rest,
+    gin_ref, out_ref, rq_ref, ro_ref, total_ref, ge_hbm, y_via, y_from, q_via, q_from, o_via, o_from, *rest,
 ):
     bits = replicas.bit_length() - 1
     roomy = chips <= 4
     arrived, rest = rest[:bits], rest[bits:]
     if not roomy:
-        core_ref, from_ref, rest = rest[0], rest[1], rest[2:]
-    (ge_ref, n2_all, gt_all, via_ref, pair_ref, dx_ref, dgt_ref, dgt_all, y_ref, gw_core, parts_ref, smalls_ref), rest = rest[:12], rest[12:]
+        (core_ref, from_ref, y_core), rest = rest[:3], rest[3:]
+    (ge_ref, n2_all, gt_all, via_ref, pair_ref, dx_ref, dgt_ref, dgt_all, y_ref, q_core, o_core, pq_ref, po_ref, smalls_ref), rest = (
+        rest[:14], rest[14:]
+    )
     if roomy:
-        core_ref, from_ref, rest = rest[0], rest[1], rest[2:]
+        (core_ref, from_ref, y_core), rest = rest[:3], rest[3:]
     (n2_up, n2_down, n2_mate, n2_recv, gt_up, gt_down, gt_mate, gt_recv,
      core_send, core_recv, far_send, far_recv, pair_send, via_recv, dgt_send, dgt_recv, yc_send, yc_recv,
      do_sem, we_sem, load_sem, stage_sem, ge_sem, p_sem, ar_send, ar_recv, ar_free,
-     y_up_send, y_up_recv, y_down_send, y_down_recv, gw_core_sem, gw_up_send, gw_up_recv, gw_down_send, gw_down_recv,
-     part_send, part_recv, small_send, small_recv, result_send, result_recv) = rest
-    local, tokens, rows = ge_ref.shape[0], x_ref.shape[0], gw_core.shape[1]
+     *sum_sems, part_send, part_recv, small_send, small_recv, result_send, result_recv) = rest
+    y_sems, q_sems, o_sems = sum_sems[:3], sum_sems[3:7], sum_sems[7:]
+    local, tokens, rows = ge_ref.shape[0], x_ref.shape[0], q_core.shape[1]
     r, f = lax.axis_index("replica"), lax.axis_index("fsdp")
     z, c = f // 2, f % 2
     mate, above, below = (r, z * 2 + 1 - c), (r, f + 2), (r, f - 2)
@@ -639,11 +641,21 @@
             def _():
                 far_copy(z, slot, t).wait_send()
 
+        def add_ye(zc):
+            make(y_core.at[zc], y_core.at[zc], yc_send.at[0], yc_recv.at[zc], mate).wait_recv()
+            there = y_core.at[zc] if roomy else landed(y_core.at[zc], "core")
+            add_rows(y_ref.at[zc], y_ref.at[zc], there, tokens, 64)
+
         do_copy(z, 0).start()
 
         def chunk(t, carry):
             zc = place(t)
             slot = t % 2
+
+            @pl.when(t > 0)
+            def _():
+                add_ye(place(t - 1))
+
             k = far(zc)
             both = (t % 2 == 1) & (t <= 2 * inner)
             single = (t > 2 * inner) & jnp.logical_not(early(t - 1))
@@ -783,6 +795,7 @@
             ge_ref[i, 2 * FF :] = dot_tn(hx_ref[i], dye_ref[i]).astype(BF)
             if bits:
                 next(sums[i])
+        add_ye(place(chips - 1))
         for t in range(max(chips - 2, 0), chips):
             free_slot(t, t % 2)
         for t in range(chips):
@@ -800,79 +813,61 @@
         pltpu.VMEM((2, tokens, D), BF), pltpu.VMEM((16 if roomy else tokens, D), BF),
     )
 
-    def line(own, size, step, core_add, name, up_ref, down_ref, up_send, up_recv, down_send, down_recv):
-        def add_block(block, other):
-            add_rows(own(block), own(block), landed(other.at[block], name), size, step)
-
-        def send(block, up):
-            there, send_sem, recv_sem = (up_ref, up_send, up_recv) if up else (down_ref, down_send, down_recv)
-            return make(own(block), there.at[block], send_sem.at[block], recv_sem.at[block], above if up else below)
-
-        nearby = [k for both in zip(range(chips - 1, -1, -1), range(chips)) for k in both][:chips]
-        for k in nearby:
-            core_add(k)
-
-            @pl.when((z == 0) & (k > 0))
-            def _():
-                send(k, True).start()
-
-            @pl.when((z == chips - 1) & (k < chips - 1))
-            def _():
-                send(k, False).start()
-
+    def line(own, size, step, core_add, name, via, arrive, send_sem, via_recv, from_recv):
+        def direct(k):
+            return make(own(k), arrive.at[z], send_sem.at[k], from_recv.at[z], (r, k * 2 + c))
+
+        def passing(k, side):
+            return make(own(k), via.at[side], send_sem.at[k], via_recv.at[side], (r, (z + 2 * side - 1) * 2 + c))
+
+        for d in range(chips - 1, 0, -1):
+            for side in range(2):
+                owner = z + (d if side else -d)
+
+                @pl.when((owner >= 0) & (owner < chips))
+                def _():
+                    core_add(owner)
+                    if d > 2:
+                        direct(owner).start()
+                    elif d == 2:
+                        passing(owner, side).start()
+                    else:
+                        pl.when((z == 0) | (z == chips - 1))(lambda: direct(owner).start())
+
+        core_add(z)
         yield
-        for k in range(chips - 2):
-            owner = chips - 1 - k
-
-            @pl.when((z > 0) & (z < owner))
-            def _():
-                send(owner, True).wait_recv()
-                add_block(owner, up_ref)
-                send(owner, True).start()
-
-            @pl.when((z < chips - 1) & (z > k))
-            def _():
-                send(k, False).wait_recv()
-                add_block(k, down_ref)
-                send(k, False).start()
-
-            yield
-
-        @pl.when(z > 0)
+
+        @pl.when((z > 0) & (z < chips - 1))
         def _():
-            send(z, True).wait_recv()
-            add_block(z, up_ref)
-
-        @pl.when(z < chips - 1)
-        def _():
-            send(z, False).wait_recv()
-            add_block(z, down_ref)
-
+            for side in range(2):
+                owner = z + 2 * side - 1
+                make(via.at[side], via.at[side], send_sem.at[0], via_recv.at[side], mate).wait_recv()
+                add_rows(own(owner), own(owner), landed(via.at[side], name), size, step)
+                direct(owner).start()
+
+        yield
         for k in range(chips):
 
-            @pl.when(z < k)
-            def _():
-                send(k, True).wait_send()
-
-            @pl.when(z > k)
-            def _():
-                send(k, False).wait_send()
+            @pl.when((z == k + 1) | (z + 1 == k) | (z > k + 2) | (z + 2 < k))
+            def _():
+                make(arrive.at[k], arrive.at[k], send_sem.at[0], from_recv.at[k], mate).wait_recv()
+                add_rows(own(z), own(z), landed(arrive.at[k], name), size, step)
+
+        for k in range(chips):
+
+            @pl.when(z != k)
+            def _():
+                direct(k).wait_send()
 
     def mixture():
-        def core_add(k):
-            make(y_core.at[k], y_core.at[k], yc_send.at[k], yc_recv.at[k], mate).wait_recv()
-            add_rows(y_ref.at[k], y_ref.at[k], landed(y_core.at[k], "tokens"), tokens, 32)
-
-        yield from line(
-            lambda k: y_ref.at[k], tokens, 32, core_add, "tokens", y_up, y_down, y_up_send, y_up_recv, y_down_send,
-            y_down_recv,
-        )
+        yield from line(lambda k: y_ref.at[k], tokens, 64, lambda k: None, "tokens", y_via, y_from, *y_sems)
         out_ref[...] = (h1_ref[...] + residual_scale * y_ref[z].astype(F32)).astype(BF)
 
-    def attention(w_ref, q_ref, kd_ref, vd_ref, o_ref, p_ref, do_ref, dqkv_ref, gw_ref, halves_stage, tokens_stage, rows_stage):
+    def attention(w_ref, q_ref, kd_ref, vd_ref, o_ref, p_ref, do_ref, dqkv_ref, gq_ref, go_ref, halves_stage, tokens_stage, q_stage, o_stage):
         stages["halves"] = (halves_stage, stage_sem.at[1])
         stages["tokens"] = (tokens_stage, stage_sem.at[2])
-        stages["rows"] = (rows_stage, stage_sem.at[3])
+        stages["q"] = (q_stage, stage_sem.at[3])
+        stages["o"] = (o_stage, stage_sem.at[4])
         loads = [
             pltpu.make_async_copy(source, target, load_sem.at[i])
             for i, (source, target) in enumerate(
@@ -881,71 +876,85 @@
         ]
         start(loads)
 
-        def projection():
-            crossing = make(gw_ref.at[:, 1 - c], gw_core, gw_core_sem.at[0], gw_core_sem.at[1], mate)
+        def projection(index, name, grad_ref, core, via, arrive, sems, parts, results, wide):
+            core_sem, *sems = sems
+            crossing = make(grad_ref.at[:, 1 - c], core, core_sem.at[0], core_sem.at[1], mate)
             crossing.start()
             yield
             crossing.wait_recv()
 
             def own(k):
-                return gw_ref.at[k, c]
+                return grad_ref.at[k, c]
 
             yield from line(
-                own, rows, 16, lambda k: add_rows(own(k), own(k), gw_core.at[k], rows, 16), "rows", gw_up, gw_down,
-                gw_up_send, gw_up_recv, gw_down_send, gw_down_recv,
+                own, rows, 16, lambda k: add_rows(own(k), own(k), core.at[k], rows, 16), name, via, arrive, *sems
             )
             crossing.wait_send()
-            wide = QKVO // replicas
+            mine = grad_ref.at[z, c]
 
             def columns(part):
                 return pl.ds(pl.multiple_of(part * wide, LANE), wide)
 
-            mine = gw_ref.at[z, c]
-
             def part_copy(d):
                 to = (r + d) % replicas
-                return make(mine.at[:, columns(to)], parts_ref.at[r], part_send.at[d], part_recv.at[r], (to, f))
+                return make(
+                    mine.at[:, columns(to)], parts.at[r], part_send.at[index, d], part_recv.at[index, r], (to, f)
+                )
 
             def small_copy(d):
                 to = (r + d) % replicas
-                return make(mine.at[:, pl.ds(QKVO, LANE)], smalls_ref.at[r], small_send.at[d], small_recv.at[r], (to, f))
+                return make(mine.at[:, pl.ds(QKV, LANE)], smalls_ref.at[r], small_send.at[d], small_recv.at[r], (to, f))
 
             for d in range(1, replicas):
                 part_copy(d).start()
-                small_copy(d).start()
-            parts_ref[r] = mine[:, columns(r)]
-            smalls_ref[r] = mine[:, pl.ds(QKVO, LANE)]
-            yield
-            for d in range(1, replicas):
-                peer = (r + d) % replicas
-                make(parts_ref.at[peer], parts_ref.at[peer], part_send.at[d], part_recv.at[peer], (peer, f)).wait_recv()
-                make(smalls_ref.at[peer], smalls_ref.at[peer], small_send.at[d], small_recv.at[peer], (peer, f)).wait_recv()
-            total = parts_ref[0].astype(F32)
-            small = smalls_ref[0].astype(F32)
-            for k in range(1, replicas):
-                total = total + parts_ref[k].astype(F32)
-                small = small + smalls_ref[k].astype(F32)
-            result_ref[r] = total.astype(BF)
-            total_ref[...] = small
-
-            def result_copy(d):
-                to = (r + d) % replicas
-                return make(result_ref.at[r], result_ref.at[r], result_send.at[d], result_recv.at[r], (to, f))
-
-            for d in range(1, replicas):
-                result_copy(d).start()
+                if index == 0:
+                    small_copy(d).start()
+            parts[r] = mine[:, columns(r)]
+            if index == 0:
+                smalls_ref[r] = mine[:, pl.ds(QKV, LANE)]
             yield
             for d in range(1, replicas):
                 peer = (r + d) % replicas
                 make(
-                    result_ref.at[peer], result_ref.at[peer], result_send.at[d], result_recv.at[peer], (peer, f)
+                    parts.at[peer], parts.at[peer], part_send.at[index, d], part_recv.at[index, peer], (peer, f)
+                ).wait_recv()
+                if index == 0:
+                    make(
+                        smalls_ref.at[peer], smalls_ref.at[peer], small_send.at[d], small_recv.at[peer], (peer, f)
+                    ).wait_recv()
+            total = parts[0].astype(F32)
+            for k in range(1, replicas):
+                total = total + parts[k].astype(F32)
+            results[r] = total.astype(BF)
+
+            def result_copy(d):
+                to = (r + d) % replicas
+                return make(
+                    results.at[r], results.at[r], result_send.at[index, d], result_recv.at[index, r], (to, f)
+                )
+
+            for d in range(1, replicas):
+                result_copy(d).start()
+            if index == 0:
+                small = smalls_ref[0].astype(F32)
+                for k in range(1, replicas):
+                    small = small + smalls_ref[k].astype(F32)
+                total_ref[...] = small
+            yield
+            for d in range(1, replicas):
+                peer = (r + d) % replicas
+                make(
+                    results.at[peer], results.at[peer], result_send.at[index, d], result_recv.at[index, peer], (peer, f)
                 ).wait_recv()
             for d in range(1, replicas):
                 part_copy(d).wait_send()
-                small_copy(d).wait_send()
+                if index == 0:
+                    small_copy(d).wait_send()
                 result_copy(d).wait_send()
 
-        moe, grads = [mixture()], [projection()]
+        moe = [mixture()]
+        grads = [projection(0, "q", gq_ref, q_core, q_via, q_from, q_sems, pq_ref, rq_ref, QKV // replicas)]
+        outs = [projection(1, "o", go_ref, o_core, o_via, o_from, o_sems, po_ref, ro_ref, D // replicas)]
 
         def go(*turns):
             for turn in turns:
@@ -983,23 +992,23 @@
             load.wait()
         backward = attention_backward(
             x_ref, dout_ref, cos_ref, sin_ref, w_ref, q_ref, kd_ref, vd_ref, p_hbm, o_ref, h1_ref, n2_ref, gd_ref, dx_ref,
-            dgate, gin_ref, gw_ref, do_ref, dqkv_ref, p_ref, p_sem,
+            dgate, gin_ref, gq_ref, go_ref, do_ref, dqkv_ref, p_ref, p_sem,
         )
         next(backward)
-        go(first)
+        go(outs)
         next(backward)
-        go(moe)
+        go(first, outs)
         next(backward, None)
-        go(grads, last, moe, grads, first, moe, last, first, grads, last, grads, first, grads, last, grads, grads)
-        go(*[moe + grads + sums] * (2 * chips + 2 * bits + 4))
+        go(grads, moe, last, grads, first, outs, last, moe, first, outs, last, grads, outs, outs, first, grads, last, grads, grads)
+        go(*[moe + outs + grads + sums] * (2 * bits + 8))
 
     size = ge_ref.shape[1] // max(bits, 1)
     pl.run_scoped(
         attention,
         pltpu.VMEM((D, W_O + D), BF), pltpu.VMEM((tokens, D), BF), pltpu.VMEM((tokens, D), BF), pltpu.VMEM((tokens, D), BF),
         pltpu.VMEM((tokens, D), BF), pltpu.VMEM((2, 2 * tokens, tokens), F32), pltpu.VMEM((tokens, D), BF),
-        pltpu.VMEM((tokens, QKV), BF), pltpu.VMEM((chips, 2, rows, QKVO + LANE), BF), pltpu.VMEM((size // 2, D), BF),
-        pltpu.VMEM((tokens, D), BF), pltpu.VMEM((rows, QKVO + LANE), BF),
+        pltpu.VMEM((tokens, QKV), BF), pltpu.VMEM((chips, 2, rows, W_O), BF), pltpu.VMEM((chips, 2, rows, D), BF),
+        pltpu.VMEM((size // 2, D), BF), pltpu.VMEM((tokens, D), BF), pltpu.VMEM((rows, W_O), BF), pltpu.VMEM((rows, D), BF),
     )
 
     for e in range(local):
@@ -1029,7 +1038,7 @@
             copy.wait_send()
 
 
-def finish(gexp_ref, result_ref, total_ref, gin_ref, out_ref, *outs):
+def finish(gexp_ref, rq_ref, ro_ref, total_ref, gin_ref, out_ref, *outs):
     layer, grad_in, gains_one, query, key, value, output, gains_two, router, expert = outs
     expert[...] = gexp_ref[...].astype(F32)
 
@@ -1037,13 +1046,13 @@
     def _():
         layer[...] = out_ref[...]
         grad_in[...] = gin_ref[...]
-        wide = result_ref.shape[2]
-        start = 0
-        for ref in (query, key, value, output):
-            for at in range(0, ref.shape[1], LANE):
-                part, column = divmod(start + at, wide)
-                ref[:, at : at + LANE] = result_ref[part, :, column : column + LANE].astype(F32)
-            start += ref.shape[1]
+        for results, targets in ((rq_ref, (query, key, value)), (ro_ref, (output,))):
+            wide, start = results.shape[2], 0
+            for ref in targets:
+                for at in range(0, ref.shape[1], LANE):
+                    part, column = divmod(start + at, wide)
+                    ref[:, at : at + LANE] = results[part, :, column : column + LANE].astype(F32)
+                start += ref.shape[1]
         small = total_ref[...].T
         router[...] = small[:E]
         gains_one[...] = small[E : E + 1]
@@ -1107,20 +1116,20 @@
         weights = weights.reshape(D, W_O + D)
         bits = replicas.bit_length() - 1
         size = 3 * FF // bits if bits else 0
-        width = QKVO + LANE
         roomy = chips <= 4
         landing = [shape((local * bits, size >> (k + 1), D), BF) for k in range(bits)]
-        blocks = [shape((chips, tokens, D), BF)] * 2
+        blocks = [shape((chips, tokens, D), BF)] * 3
         if not roomy:
             landing += blocks
-        landing_sems = [dma((chips,))] * 4
         outs = call(
             functools.partial(back, replicas, chips),
             [
-                shape((tokens, D), F32), shape((tokens, D), BF), shape((replicas, rows, QKVO // replicas), BF),
-                shape((rows, LANE), F32), shape((local, 3 * FF, D), BF),
+                shape((tokens, D), F32), shape((tokens, D), BF), shape((replicas, rows, QKV // replicas), BF),
+                shape((replicas, rows, D // replicas), BF), shape((rows, LANE), F32), shape((local, 3 * FF, D), BF),
+                shape((2, tokens, D), BF), shape((chips, tokens, D), BF), shape((2, rows, W_O), BF),
+                shape((chips, rows, W_O), BF), shape((2, rows, D), BF), shape((chips, rows, D), BF),
             ]
-            + [shape((chips, tokens, D), BF)] * 3 + [shape((chips, rows, width), BF)] * 2 + landing,
+            + landing,
             (
                 hidden_in, out_cotangent, cosines, sines, h1, n2, gd, gt,
                 dout_all, expert_weights, weights, q, kd, vd, o, p,
@@ -1129,21 +1138,23 @@
                 pltpu.VMEM((local, 3 * FF, D), BF), pltpu.VMEM((chips, 2, tokens, D), BF),
                 pltpu.VMEM((chips, 2, E, tokens), F32), pltpu.VMEM((2, tokens, D), BF), pltpu.VMEM((2, tokens, D), BF),
                 pltpu.VMEM((tokens, D), F32), pltpu.VMEM((chips, 2, 8, tokens), F32), pltpu.VMEM((group, 8, tokens), F32),
-                pltpu.VMEM((chips, tokens, D), BF), pltpu.VMEM((chips, rows, width), BF),
-                pltpu.VMEM((replicas, rows, QKVO // replicas), BF), pltpu.VMEM((replicas, rows, LANE), BF),
+                pltpu.VMEM((chips, tokens, D), BF), pltpu.VMEM((chips, rows, W_O), BF), pltpu.VMEM((chips, rows, D), BF),
+                pltpu.VMEM((replicas, rows, QKV // replicas), BF), pltpu.VMEM((replicas, rows, D // replicas), BF),
+                pltpu.VMEM((replicas, rows, LANE), BF),
             ]
             + ([pltpu.VMEM(b.shape, b.dtype) for b in blocks] if roomy else [])
             + ([dma((chips,))] * 3 + [dma((chips, 2))]) * 2 + [dma((chips,))] * 4 + [dma((2,))] * 2
             + [dma((chips, 2)), dma((group,)), dma((chips,)), dma((chips,))]
-            + [dma((2,)), dma((1,)), dma((5,)), dma((4,)), dma((local,)), dma((2,))]
+            + [dma((2,)), dma((1,)), dma((5,)), dma((5,)), dma((local,)), dma((2,))]
             + [dma((max(local * bits, 1), max(2 * bits, 1)))] * 2
             + [pltpu.SemaphoreType.REGULAR((max(local * bits, 1), max(bits, 1)))]
-            + landing_sems + [dma((2,))] + landing_sems + [dma((replicas,))] * 6,
+            + [dma((chips,)), dma((2,)), dma((chips,))] + [dma((2,)), dma((chips,)), dma((2,)), dma((chips,))] * 2
+            + [dma((2, replicas))] * 2 + [dma((replicas,))] * 2 + [dma((2, replicas))] * 2,
             outside=8,
-            out_outside=6 + len(landing),
+            out_outside=7 + len(landing),
             collective_id=0,
         )
-        grad_in, layer_out, result, total, grad_experts = outs[:5]
+        grad_in, layer_out, result_q, result_o, total, grad_experts = outs[:6]
         steps = 8
         block = local * 3 * FF // steps
         fixed = [
@@ -1153,19 +1164,19 @@
         ]
 
         def still(a):
-            return pl.BlockSpec(a.shape, lambda i: (0, 0))
+            return pl.BlockSpec(a.shape, lambda i: (0,) * len(a.shape))
 
         expert_block = pl.BlockSpec((block, D), lambda i: (i, 0))
         outs = pl.pallas_call(
             finish,
             grid=(steps,),
             in_specs=[
-                expert_block, pl.BlockSpec(result.shape, lambda i: (0, 0, 0)), still(total), still(grad_in), still(layer_out)
+                expert_block, still(result_q), still(result_o), still(total), still(grad_in), still(layer_out)
             ],
             out_specs=[still(a) for a in fixed] + [expert_block],
             out_shape=fixed + [shape((local * 3 * FF, D), F32)],
             compiler_params=pltpu.CompilerParams(vmem_limit_bytes=VMEM_LIMIT),
-        )(grad_experts.reshape(local * 3 * FF, D), result, total, grad_in, layer_out)
+        )(grad_experts.reshape(local * 3 * FF, D), result_q, result_o, total, grad_in, layer_out)
         return (
             outs[0], outs[1], outs[2][0], outs[3], outs[4], outs[5], outs[6], outs[7][0], outs[8].T,
             outs[9].reshape(local, 3 * FF, D),

time: 319 us -> 280 us (0.88)
  Pallas kernels: 313 us -> 274 us
    pallas_call x2, Pallas kernels: 302 us -> 263 us  [call(): pl.pallas_call(kernel, out_shape=out_shape, in_specs=[pl.BlockSpec(memory...]
where the time goes in v7:
time: 280 us; the launch traced here: 274 us
  Pallas kernels  274 us (98%)
    pallas_call x2, Pallas kernels, call(): pl.pallas_call(kernel, out_shape=out_shape, in_specs=[pl.BlockSpec(memory...  263 us
    pallas_call x1, Pallas kernels, body(): pl.pallas_call(finish, grid=(steps,), in_specs=[expert_block, still(resul...  10.7 us

profile of v7, /device:TPU:10, one launch (start us, length us, event | category | flops | bytes accessed | tf_op | source)
XLA Modules:
  0.0 274.4 jit_solution(8989611389054548488)
XLA Ops:
  0.6 58.3 %shard_map.204 = (bf16[4,2,128,3200]{3,2,1,0:T(8,128)(2,1)}, bf16[256,1024]{1,0:T(8,128)(2,1)}, bf16[256,1024]{1,0:T(8,128)(2,1)}, bf16[256,1024]{1,0:T(8,128)(2...) custom-call(bf16[256,1024]{1,0:T(8,128)(2,1)} %x_ref.3, ...), custom_call_target="tpu_custom_call" | custom-call | tf_op jit(solution)/shard_map/pallas_call | solution.py:1065
  59.0 204.7 %shard_map.205 = (f32[256,1024]{1,0:T(8,128)}, bf16[256,1024]{1,0:T(8,128)(2,1)}, bf16[4,128,512]{2,1,0:T(8,128)(2,1)}, bf16[4,128,256]{2,1,0:T(8,128)(2,1)}, f3...) custom-call(bf16[256,1024]{1,0:T(8,128)(2,1)} %x_ref.3, ...), custom_call_target="tpu_custom_call" | custom-call | tf_op jit(solution)/shard_map/pallas_call | solution.py:1065
  263.7 10.7 %shard_map.206 = (bf16[256,1024]{1,0:T(8,128)(2,1)}, f32[256,1024]{1,0:T(8,128)}, f32[1,128]{1,0:T(1,128)}, f32[128,1024]{1,0:T(8,128)}, f32[128,512]{1,0:T(8,12...) custom-call(bf16[3072,1024]{1,0:T(8,128)(2,1)} %bitcast.11, ...), custom_call_target="tpu_custom_call" | custom-call | tf_op jit(solution)/shard_map/pallas_call | solution.py:1170

commit v8 on v7

v8 whole, which is shorter than its diff:
```python
import functools

import jax
import jax.numpy as jnp
import numpy as np
from jax import lax
from jax.experimental import pallas as pl
from jax.experimental.pallas import tpu as pltpu
from jax.sharding import PartitionSpec as P

D = 1024
H = 16
KVH = 8
HD = 64
FF = 512
TOPK = 8
E = 16
CAP = 144
LANE = 128
QKV = H * HD + 2 * KVH * HD
QKVO = QKV + D
W_O = QKV + LANE

norm_eps = 1e-06
score_scale = 0.015625
residual_scale = 0.22
rope_base = 10000.0
masked_score = -1e30

BF = jnp.bfloat16
F32 = jnp.float32
VMEM_LIMIT = 63 * 2**20


def dot(a, b):
    return lax.dot_general(a, b, (((1,), (0,)), ((), ())), preferred_element_type=F32)


def dot_nt(a, b):
    return lax.dot_general(a, b, (((1,), (1,)), ((), ())), preferred_element_type=F32)


def dot_tn(a, b):
    return lax.dot_general(a, b, (((0,), (0,)), ((), ())), preferred_element_type=F32)


def lanes_of(rows):
    return lax.broadcasted_iota(jnp.int32, (rows, LANE), 1)


def turned(block, lane):
    return jnp.where(lane % HD < HD // 2, pltpu.roll(block, LANE - HD // 2, 1), pltpu.roll(block, HD // 2, 1))


def halves(block, low):
    zero = jnp.zeros_like(block)
    return jnp.concatenate([jnp.where(low, block, zero), jnp.where(low, zero, block)], axis=0)


def rope_table(tokens):
    frequency = np.float32(rope_base) ** (-np.arange(0, HD, 2, dtype=np.float32) / np.float32(HD))
    frequency = np.tile(frequency.astype(np.float32), LANE // (HD // 2))
    angles = (np.arange(tokens, dtype=np.float32)[:, None] * frequency[None, :]).astype(np.float64)
    sign = np.where(np.arange(LANE) % HD < HD // 2, -1.0, 1.0)
    pieces = []
    for values in (np.cos(angles), np.sin(angles) * sign[None, :]):
        rest = values.astype(np.float32)
        for _ in range(3):
            piece = rest.astype(BF)
            pieces.append(piece)
            rest = rest - piece.astype(np.float32)
    return np.concatenate(pieces, axis=1)


class Copies:
    def make(self, src, dst, send, recv, device):
        return pltpu.make_async_remote_copy(
            src_ref=src, dst_ref=dst, send_sem=send, recv_sem=recv, device_id=device, device_id_type=pl.DeviceIdType.MESH
        )


def meet(devices, expected):
    barrier = pltpu.get_barrier_semaphore()
    for condition, device in devices:

        def signal(device=device):
            pl.semaphore_signal(barrier, inc=1, device_id=device, device_id_type=pl.DeviceIdType.MESH)

        if condition is True:
            signal()
        else:
            pl.when(condition)(signal)
    pl.semaphore_wait(barrier, expected)


def attention_backward(
    x_ref, dout_ref, cos_ref, sin_ref, columns, q_ref, kd_ref, vd_ref, p_hbm, o_ref, h1_ref, n2_ref, gd_ref, dx_ref, dgate,
    gin_ref, gq_ref, gkv_ref, go_ref, do_ref, dqkv_ref, p_ref, p_sem,
):
    tokens = x_ref.shape[0]
    lane = lanes_of(tokens)
    low = lane < HD

    def p_copy(g):
        return pltpu.make_async_copy(p_hbm.at[g], p_ref.at[g % 2], p_sem.at[g % 2])

    p_copy(0).start()

    def put(ref, at, value):
        ref[:, :, :, at] = value.astype(BF).reshape(*ref.shape[:3], value.shape[1])

    small = columns(QKV, LANE).astype(F32).T
    gain_one, gain_two = small[E : E + 1], small[E + 1 : E + 2]
    after = h1_ref[...]
    factor_two = lax.rsqrt(jnp.mean(after * after, axis=1, keepdims=True) + norm_eps)
    gates = jnp.maximum(gd_ref[...], 0.0)
    grad_gates = dgate()
    chosen = gates * (grad_gates - jnp.sum(gates * grad_gates, axis=1, keepdims=True))
    grad_logits = chosen.astype(BF)
    grad_normed = dx_ref[...] + dot_nt(grad_logits, columns(QKV, LANE))
    scaled = grad_normed * gain_two
    grad_after = dout_ref[...].astype(F32) + (
        factor_two * scaled - after * factor_two**3 * jnp.mean(scaled * after, axis=1, keepdims=True)
    )
    grad_gain_two = jnp.sum(grad_normed * after * factor_two, axis=0, keepdims=True)
    gin_ref[...] = grad_after
    grad_branch = (residual_scale * grad_after).astype(BF)
    for at in range(0, D, FF):
        put(go_ref, slice(at, at + FF), dot_tn(o_ref[...], grad_branch[:, at : at + FF]))
    do_ref[...] = dot_nt(grad_branch, columns(W_O, D)).astype(BF)
    grad_router = dot_tn(n2_ref[...], grad_logits)
    yield

    cosines, sines = cos_ref[...], sin_ref[...]
    key_back, value_back = [], []
    for g in range(KVH):
        at = slice(g * LANE, (g + 1) * LANE)
        queries = halves(q_ref[:, at].astype(F32), low).astype(BF)
        outs = halves(do_ref[:, at].astype(F32), low).astype(BF)
        if g + 1 < KVH:
            p_copy(g + 1).start()
        p_copy(g).wait()
        weights = p_ref[g % 2]
        grad_weights = dot_nt(outs, vd_ref[:, at])
        total = jnp.sum(weights * grad_weights, axis=1, keepdims=True)
        grad_scores = (weights * (grad_weights - total)).astype(BF)
        block = dot(grad_scores, kd_ref[:, at])
        block = jnp.where(low, block[:tokens], block[tokens:]) * score_scale
        dqkv_ref[:, at] = (block * cosines - turned(block, lane) * sines).astype(BF)
        block = dot_tn(grad_scores, queries) * score_scale
        key_back.append(block + pltpu.roll(block, HD, 1))
        block = dot_tn(weights.astype(BF), outs)
        value_back.append(block + pltpu.roll(block, HD, 1))
    for m in range(KVH // 2):
        block = jnp.where(low, key_back[2 * m], key_back[2 * m + 1])
        at = slice(H * HD + m * LANE, H * HD + (m + 1) * LANE)
        dqkv_ref[:, at] = (block * cosines - turned(block, lane) * sines).astype(BF)
        at = slice(H * HD + KVH * HD + m * LANE, H * HD + KVH * HD + (m + 1) * LANE)
        dqkv_ref[:, at] = jnp.where(low, value_back[2 * m], value_back[2 * m + 1]).astype(BF)
    yield

    source = x_ref[...].astype(F32)
    factor_one = lax.rsqrt(jnp.mean(source * source, axis=1, keepdims=True) + norm_eps)
    normed = (source * factor_one * gain_one).astype(BF)
    for at in range(0, H * HD, FF):
        put(gq_ref, slice(at, at + FF), dot_tn(normed, dqkv_ref[:, at : at + FF]))
    yield
    grad_normed = dot_nt(dqkv_ref[...], columns(0, QKV))
    scaled = grad_normed * gain_one
    grad_vector = factor_one * scaled - source * factor_one**3 * jnp.mean(scaled * source, axis=1, keepdims=True)
    gin_ref[...] += grad_vector
    grad_gain_one = jnp.sum(grad_normed * source * factor_one, axis=0, keepdims=True)
    gains = jnp.concatenate([grad_gain_one, grad_gain_two, jnp.zeros((6, D), F32)], axis=0).T
    at = lanes_of(D)
    extra = jnp.where(at == E, gains[:, 0:1], jnp.where(at == E + 1, gains[:, 1:2], grad_router))
    put(gkv_ref, slice(D, D + LANE), extra)
    for at in range(0, QKV - H * HD, FF):
        put(gkv_ref, slice(at, at + FF), dot_tn(normed, dqkv_ref[:, H * HD + at : H * HD + at + FF]))


def add_rows(target, first, second, rows, step):
    def some(i, carry):
        at = pl.ds(pl.multiple_of(i * step, step), step)
        target[at] = (first[at].astype(F32) + second[at].astype(F32)).astype(target.dtype)
        return carry

    lax.fori_loop(0, rows // step, some, 0)


def layer(
    replicas, chips,
    x_ref, len_ref, routes_ref, table_ref, wq_ref, wk_ref, wv_ref, wo_ref, wr_ref, g1_ref, g2_ref, dout_ref, we_hbm,
    gin_ref, out_ref, results_ref, total_ref, ge_hbm, p_hbm, heads_hbm, do_all, y_via, y_from, kv_via, kv_from, q_via, q_from,
    o_via, o_from, *rest,
):
    bits = replicas.bit_length() - 1
    roomy = chips <= 4
    arrived, y_core, rest = rest[:bits], rest[bits], rest[bits + 1 :]
    if not roomy:
        (core_ref, from_ref), rest = rest[:2], rest[2:]
    (w_all, h1_ref, gd_ref, cos_ref, sin_ref), rest = rest[:5], rest[5:]
    (heads_sem, own_sem, z_up, z_down, z_recv, xy_send, xy_recv, mate_send, mate_recv, do_send, do_recv), rest = rest[:11], rest[11:]
    (ge_ref, n2_all, gt_all, via_ref, pair_ref, dgt_ref, dgt_all, y_ref, kv_core, q_core, o_core, parts_ref, smalls_ref), rest = (
        rest[:13], rest[13:]
    )
    dx_ref = gin_ref
    if roomy:
        (core_ref, from_ref), rest = rest[:2], rest[2:]
    (n2_up, n2_down, n2_mate, n2_recv, gt_up, gt_down, gt_mate, gt_recv,
     core_send, core_recv, far_send, far_recv, pair_send, via_recv, dgt_send, dgt_recv, yc_send, yc_recv,
     do_sem, we_sem, stage_sem, ge_sem, p_sem, ar_send, ar_recv, ar_free,
     *sum_sems, part_send, part_recv, small_send, small_recv, result_send, result_recv) = rest
    y_sems, kv_sems, q_sems, o_sems = sum_sems[:3], sum_sems[3:7], sum_sems[7:11], sum_sems[11:]
    local, tokens, rows = ge_ref.shape[0], x_ref.shape[0], q_core.shape[1]
    r, f = lax.axis_index("replica"), lax.axis_index("fsdp")
    z, c = f // 2, f % 2
    mate, above, below = (r, z * 2 + 1 - c), (r, f + 2), (r, f - 2)
    make = Copies().make

    load_experts = pltpu.make_async_copy(we_hbm, ge_ref, we_sem.at[0])
    load_experts.start()
    own_dout = pltpu.make_async_copy(dout_ref, do_all.at[z, c], own_sem.at[0])
    own_dout.start()
    packed = [wr_ref[...].astype(F32), g1_ref[...].astype(F32), g2_ref[...].astype(F32)]
    packed = jnp.concatenate(packed + [jnp.zeros((LANE - E - 2, rows), F32)], axis=0)
    own = w_all.at[z, c]
    own[:, : H * HD] = wq_ref[...]
    own[:, H * HD : H * HD + KVH * HD] = wk_ref[...]
    own[:, H * HD + KVH * HD : QKV] = wv_ref[...]
    own[:, QKV:W_O] = packed.T.astype(BF)
    own[:, W_O:] = wo_ref[...]
    peers = [(True, mate)]
    for k in range(1, chips):
        to = (z + k) % chips
        peers += [(True, (r, to * 2 + c)), (True, (r, to * 2 + 1 - c))]
    peers += [(True, ((r + d) % replicas, f)) for d in range(1, replicas)]
    meet(peers, len(peers))

    def part(kind):
        if kind == 0:
            return pl.ds(pl.multiple_of(r * (QKV // replicas), LANE), QKV // replicas)
        if kind == 1:
            return pl.ds(QKV, LANE)
        return pl.ds(pl.multiple_of(W_O + r * (D // replicas), LANE), D // replicas)

    def along(zb, kind, up):
        ref = w_all.at[zb, c, :, part(kind)]
        return make(ref, ref, (z_up if up else z_down).at[kind, zb], z_recv.at[kind, zb], above if up else below)

    def across(zb, kind, d):
        ref = w_all.at[zb, c, :, part(kind)]
        return make(ref, ref, xy_send.at[kind, zb, d], xy_recv.at[kind, zb, r], ((r + d) % replicas, f))

    def wait_across(zb, kind):
        for d in range(1, replicas):
            peer = (r + d) % replicas
            ref = w_all.at[zb, c, :, part(kind)]
            make(ref, ref, xy_send.at[kind, zb, d], xy_recv.at[kind, zb, peer], (peer, f)).wait_recv()

    def to_mate(zb, core, late):
        ref = w_all.at[zb, core, :, pl.ds(W_O, D) if late else pl.ds(0, W_O)]
        return make(ref, ref, mate_send.at[late, zb], mate_recv.at[late, zb], mate)

    def dout_copy(zb, core, way):
        source = do_all.at[zb, core]
        return make(source, do_all.at[zb, core], do_send.at[way, zb], do_recv.at[zb, core], (above, below, mate)[way])

    def both_sides(k, act):
        @pl.when(z >= k)
        def _():
            act(z - k, True)

        @pl.when(z < chips - k)
        def _():
            act(z + k, False)

    def onward(up):
        return z < chips - 1 if up else z > 0

    def dout_arrive(zb, low):
        dout_copy(zb, c, 0 if low else 1).wait_recv()

        @pl.when(onward(low))
        def _():
            dout_copy(zb, c, 0 if low else 1).start()

        dout_copy(zb, c, 2).start()

    def columns(start, size):
        return w_all.reshape(D, W_O + D)[:, start : start + size]

    def forward(p_ref, q_ref, kd_ref, vd_ref, o_ref):
        for kind in range(3):
            both_sides(1, lambda zb, low: along(z, kind, not low).start())
        for late in range(2):
            to_mate(z, c, late).start()

        source = x_ref[...].astype(F32)
        factor = lax.rsqrt(jnp.mean(source * source, axis=1, keepdims=True) + norm_eps)
        lane = lanes_of(tokens)
        low_lane = lane < HD
        row = lax.broadcasted_iota(jnp.int32, (tokens, tokens), 0)
        column = lax.broadcasted_iota(jnp.int32, (tokens, tokens), 1)
        row_at = lax.broadcasted_iota(jnp.int32, (tokens, 1), 0)
        column_at = lax.broadcasted_iota(jnp.int32, (1, tokens), 1)
        row_segment = jnp.zeros((tokens, 1), jnp.int32)
        row_start = jnp.zeros((tokens, 1), jnp.int32)
        column_segment = jnp.zeros((1, tokens), jnp.int32)
        end = jnp.int32(0)
        for j in range(len_ref.shape[1]):
            end = end + len_ref[0, j]
            row_segment += (row_at >= end).astype(jnp.int32)
            row_start = jnp.maximum(row_start, jnp.where(row_at >= end, end, 0))
            column_segment += (column_at >= end).astype(jnp.int32)
        place = (column == row - row_start).astype(F32).astype(BF)
        found = dot(place, table_ref[...])
        found = [found[:, i * LANE : (i + 1) * LANE] for i in range(6)]
        cosines, sines = found[0] + found[1] + found[2], found[3] + found[4] + found[5]
        cos_ref[...] = cosines
        sin_ref[...] = sines

        own_dout.wait()
        for k in range(1, chips):
            for kind in range(3):

                def arrive(zb, low, kind=kind):
                    along(zb, kind, low).wait_recv()

                    @pl.when(onward(low))
                    def _():
                        along(zb, kind, low).start()

                    if kind != 1:
                        for d in range(1, replicas):
                            across(zb, kind, d).start()

                both_sides(k, arrive)
            if k == 1:
                both_sides(1, lambda zb, low: dout_copy(z, c, 1 if low else 0).start())
                dout_copy(z, c, 2).start()

        def share(k, late):
            def act(zb, low):
                wait_across(zb, 2 if late else 0)
                to_mate(zb, c, late).start()

            both_sides(k, act)

        for k in range(1, chips):
            share(k, 0)
        if chips > 1:
            both_sides(1, dout_arrive)
        for k in range(chips):
            to_mate(k, 1 - c, 0).wait_recv()

        small = columns(QKV, LANE)
        gains = small.astype(F32).T
        gain_one, gain_two = gains[E : E + 1], gains[E + 1 : E + 2]
        normed = (source * factor * gain_one).astype(BF)
        q_all = dot(normed, columns(0, H * HD))
        for g in range(H // 2):
            at = slice(g * LANE, (g + 1) * LANE)
            block = q_all[:, at]
            q_ref[:, at] = (block * cosines + turned(block, lane) * sines).astype(BF)
        kv = dot(normed, columns(H * HD, 2 * KVH * HD))
        for m in range(KVH // 2):
            block = kv[:, m * LANE : (m + 1) * LANE]
            block = block * cosines + turned(block, lane) * sines
            other = pltpu.roll(block, HD, 1)
            kd_ref[:, 2 * m * LANE : (2 * m + 1) * LANE] = jnp.where(low_lane, block, other).astype(BF)
            kd_ref[:, (2 * m + 1) * LANE : (2 * m + 2) * LANE] = jnp.where(low_lane, other, block).astype(BF)
            block = kv[:, KVH * HD + m * LANE : KVH * HD + (m + 1) * LANE]
            other = pltpu.roll(block, HD, 1)
            vd_ref[:, 2 * m * LANE : (2 * m + 1) * LANE] = jnp.where(low_lane, block, other).astype(BF)
            vd_ref[:, (2 * m + 1) * LANE : (2 * m + 2) * LANE] = jnp.where(low_lane, other, block).astype(BF)
        saves = [
            pltpu.make_async_copy(ref, heads_hbm.at[i], heads_sem.at[i]) for i, ref in enumerate((q_ref, kd_ref, vd_ref, o_ref))
        ]
        for save in saves[:3]:
            save.start()
        bias = jnp.where((row_segment == column_segment) & (column <= row), 0.0, masked_score)
        bias = jnp.concatenate([bias, bias], axis=0)

        def p_copy(g):
            return pltpu.make_async_copy(p_ref.at[g % 2], p_hbm.at[g], p_sem.at[g % 2])

        for g in range(KVH):
            at = slice(g * LANE, (g + 1) * LANE)
            queries = halves(q_ref[:, at].astype(F32), low_lane).astype(BF)
            scores = dot_nt(queries, kd_ref[:, at]) * score_scale + bias
            shifted = jnp.exp(scores - jnp.max(scores, axis=1, keepdims=True))
            weights = shifted * (1.0 / jnp.sum(shifted, axis=1, keepdims=True))
            if g >= 2:
                p_copy(g - 2).wait()
            p_ref[g % 2] = weights
            p_copy(g).start()
            mixed = dot(weights.astype(BF), vd_ref[:, at])
            o_ref[:, at] = jnp.where(low_lane, mixed[:tokens], mixed[tokens:]).astype(BF)

        saves[3].start()
        if chips > 2:
            both_sides(2, dout_arrive)
        for k in range(1, chips):
            share(k, 1)

        for k in range(chips):
            to_mate(k, 1 - c, 1).wait_recv()
        after = source + residual_scale * dot(o_ref[...], columns(W_O, D))
        h1_ref[...] = after
        factor = lax.rsqrt(jnp.mean(after * after, axis=1, keepdims=True) + norm_eps)
        normed = (after * factor * gain_two).astype(BF)
        n2_all[z, c] = normed
        logits = dot(normed, small).T[:E]
        expert = lax.broadcasted_iota(jnp.int32, (E, tokens), 0)
        routed = routes_ref[0:1] == expert
        for j in range(1, TOPK):
            routed |= routes_ref[j : j + 1] == expert
        top = jnp.max(jnp.where(routed, logits, masked_score), axis=0, keepdims=True)
        powers = jnp.where(routed, jnp.exp(logits - top), 0.0)
        gates = powers / jnp.sum(powers, axis=0, keepdims=True)
        gates = jnp.where(routed, gates, -1.0)
        gt_all[z, c] = gates
        gd_ref[...] = jnp.concatenate([gates, jnp.full((LANE - E, tokens), -1.0, F32)], axis=0).T
        for g in (KVH - 2, KVH - 1):
            p_copy(g).wait()
        for save in saves:
            save.wait()

    pl.run_scoped(forward, pltpu.VMEM((2, 2 * tokens, tokens), F32), *[pltpu.VMEM((tokens, D), BF)] * 4)

    def bit_of(b):
        return (r // (1 << b)) % 2

    def partner(b):
        return (r + (1 - 2 * bit_of(b)) * (1 << b), f)

    stages = {}

    def landed(ref, name):
        stage, sem = stages[name]
        if ref.shape != stage.shape:
            stage = stage.at[pl.ds(0, ref.shape[0])]
        copy = pltpu.make_async_copy(ref, stage, sem)
        copy.start()
        copy.wait()
        return stage

    def halving(e):
        size = ge_ref.shape[1] // bits
        orders = [[(g + k) % bits for k in range(bits)] for g in range(bits)]
        starts = [[] for _ in range(bits)]
        for g in range(bits):
            at = g * size
            for k in range(bits):
                starts[g].append(at)
                at = at + bit_of(orders[g][k]) * (size >> (k + 1))
            starts[g].append(at)

        def region(g, k):
            half = size >> (k + 1)
            return ge_ref.at[e, pl.ds(pl.multiple_of(starts[g][k + 1], half), half)]

        def exchange(g, k):
            half, job = size >> (k + 1), e * bits + g
            give = pl.multiple_of(starts[g][k] + (1 - bit_of(orders[g][k])) * half, half)
            return make(
                ge_ref.at[e, pl.ds(give, half)], arrived[k].at[job], ar_send.at[job, k], ar_recv.at[job, k],
                partner(orders[g][k]),
            )

        def spread(g, k):
            job, ref = e * bits + g, region(g, k)
            return make(ref, ref, ar_send.at[job, bits + k], ar_recv.at[job, bits + k], partner(orders[g][k]))

        def spread_once_free(g, k):
            pl.semaphore_wait(ar_free.at[e * bits + g, k], 1)
            spread(g, k).start()

        yield
        for g in range(bits):
            exchange(g, 0).start()
        yield
        for k in range(bits):
            half = size >> (k + 1)
            for g in range(bits):
                job = e * bits + g
                exchange(g, k).wait_recv()
                own = region(g, k)
                add_rows(own, own, landed(arrived[k].at[job], "halves"), half, min(half, 64))
                if k < bits - 1:
                    exchange(g, k + 1).start()
                exchange(g, k).wait_send()
                pl.semaphore_signal(
                    ar_free.at[job, k], inc=1, device_id=partner(orders[g][k]), device_id_type=pl.DeviceIdType.MESH
                )
                if k == bits - 1:
                    spread_once_free(g, k)
            yield
        for k in range(bits - 1, -1, -1):
            for g in range(bits):
                spread(g, k).wait_recv()
                if k > 0:
                    spread_once_free(g, k - 1)
            yield
        for g in range(bits):
            for k in range(bits):
                spread(g, k).wait_send()
        pltpu.make_async_copy(ge_ref.at[e], ge_hbm.at[e], ge_sem.at[e]).start()

    sums = [halving(e) for e in range(local)] if bits else []
    first, last = sums[:1], sums[1:]
    for process in sums:
        next(process)

    def pass_on(zb, how):
        to = {"up": above, "down": below, "mate": mate}[how]
        sems = {"up": (n2_up, gt_up), "down": (n2_down, gt_down), "mate": (n2_mate, gt_mate)}[how]
        return [
            make(ref.at[zb, c], ref.at[zb, c], sem.at[zb], recv.at[zb, c], to)
            for ref, sem, recv in ((gt_all, sems[1], gt_recv), (n2_all, sems[0], n2_recv))
        ]

    def got(zb, core):
        for ref, sem, recv in ((gt_all, gt_mate, gt_recv), (n2_all, n2_mate, n2_recv)):
            make(ref.at[zb, core], ref.at[zb, core], sem.at[zb], recv.at[zb, core], mate).wait_recv()

    def start(copies):
        for copy in copies:
            copy.start()

    @pl.when(z < chips - 1)
    def _():
        start(pass_on(z, "up"))

    @pl.when(z > 0)
    def _():
        start(pass_on(z, "down"))

    start(pass_on(z, "mate"))
    inner = jnp.minimum(z, chips - 1 - z)

    def place(t):
        k = (t + 1) // 2
        near = jnp.where(t % 2 == 1, z - k, z + k)
        return jnp.where(t <= 2 * inner, near, jnp.where(2 * z < chips - 1, t, chips - 1 - t))

    def far(zc):
        return jnp.where(zc > z, zc - z, z - zc)

    def side_of(zc):
        return jnp.where(zc > z, 1, 0)

    def relay(k, low, high):
        @pl.when(low)
        def _():
            pl.when(k > 2)(lambda: dout_arrive(z - k, True))
            got(z - k, c)

            @pl.when(z < chips - 1)
            def _():
                start(pass_on(z - k, "up"))

            start(pass_on(z - k, "mate"))

        @pl.when(high)
        def _():
            pl.when(k > 2)(lambda: dout_arrive(z + k, False))
            got(z + k, c)

            @pl.when(z > 0)
            def _():
                start(pass_on(z + k, "down"))

            start(pass_on(z + k, "mate"))

    def early(t):
        return (t >= 2) & (t % 2 == 0) & (t <= 2 * inner) & (t < chips - 1)

    def pair_copy(side):
        owner = z + 2 * side - 1
        return make(pair_ref.at[side], from_ref.at[z], pair_send.at[side], far_recv.at[z], (r, owner * 2 + c))

    def experts_and_sums(do_buf, xs_ref, dye_ref, dgu_ref, hx_ref, dxp_ref, yps_ref, core_stage):
        stages["core"] = (core_stage, stage_sem.at[0])
        before = lax.broadcasted_iota(jnp.int32, (tokens, tokens), 0) < lax.broadcasted_iota(jnp.int32, (tokens, tokens), 1)
        before = before.astype(F32).astype(BF)
        slot_index = lax.broadcasted_iota(jnp.int32, (CAP, tokens), 0).astype(F32)
        pair = 2 * CAP

        def do_copy(zc):
            return pltpu.make_async_copy(do_all.at[zc], do_buf, do_sem.at[0])

        def core_copy(zc, slot, t):
            return make(dxp_ref.at[slot, 1 - c], core_ref.at[zc], core_send.at[t], core_recv.at[zc], mate)

        def y_copy(zc, slot, t):
            return make(yps_ref.at[slot], y_core.at[zc], yc_send.at[t], yc_recv.at[zc], mate)

        def via_copy(zc, slot, t):
            side = side_of(zc)
            return make(
                dxp_ref.at[slot, c], via_ref.at[side], far_send.at[t], via_recv.at[side], (r, (z + 2 * side - 1) * 2 + c)
            )

        def far_copy(zc, slot, t):
            return make(dxp_ref.at[slot, c], from_ref.at[z], far_send.at[t], far_recv.at[z], (r, zc * 2 + c))

        def dgt_copy(zc, core, t):
            return make(dgt_ref.at[t, core], dgt_all.at[f], dgt_send.at[t, core], dgt_recv.at[f], (r, zc * 2 + core))

        def free_slot(t, slot):
            core_copy(z, slot, t).wait_send()
            y_copy(z, slot, t).wait_send()

            @pl.when(far(place(t)) >= 2)
            def _():
                far_copy(z, slot, t).wait_send()

        def add_ye(zc):
            make(y_core.at[zc], y_core.at[zc], yc_send.at[0], yc_recv.at[zc], mate).wait_recv()
            add_rows(y_ref.at[zc], y_ref.at[zc], landed(y_core.at[zc], "core"), tokens, 64)
            send_sem, _, from_recv = y_sems


        def chunk(t, carry):
            zc = place(t)
            slot = t % 2

            @pl.when(t > 0)
            def _():
                add_ye(place(t - 1))

            k = far(zc)
            both = (t % 2 == 1) & (t <= 2 * inner)
            single = (t > 2 * inner) & jnp.logical_not(early(t - 1))
            relay(k, both | (single & (zc < z)), both | (single & (zc > z)))
            dout_copy(zc, 1 - c, 2).wait_recv()
            do_copy(zc).start()
            got(zc, 1 - c)
            do_copy(zc).wait()

            @pl.when(t == 0)
            def _():
                load_experts.wait()

            @pl.when(t >= 2)
            def _():
                free_slot(t - 2, slot)

            picks, gates, dms = [], [], []
            at_chip = pl.multiple_of(zc * pair, 16)
            for core in range(2):
                mine = [gt_all[zc, core, pl.ds(f * local + i, 1), :] for i in range(local)]
                mine = jnp.concatenate(mine, axis=0) if local > 1 else mine[0]
                rank = jnp.where(mine >= 0.0, dot((mine >= 0.0).astype(F32).astype(BF), before), -1.0)
                chosen = [slot_index == rank[i : i + 1] for i in range(local)]
                gates.append([jnp.sum(jnp.where(chosen[i], mine[i : i + 1], 0.0), axis=1, keepdims=True) for i in range(local)])
                picks.append([one.astype(F32) for one in chosen])
                pick = jnp.concatenate([one.astype(BF) for one in picks[core]], axis=0)
                taken = dot(pick, n2_all[zc, core]).astype(BF)
                grads = dot(pick, do_buf[core])
                dms.append(grads.astype(BF))
                grads = grads * residual_scale
                at = pl.ds(pl.multiple_of(at_chip + core * CAP, 16), CAP)
                for i in range(local):
                    part = slice(i * CAP, (i + 1) * CAP)
                    xs_ref[i, at] = taken[part]
                    dye_ref[i, at] = (gates[core][i] * grads[part]).astype(BF)
            at = pl.ds(at_chip, pair)
            mades, backs, values = [], [], []
            for i in range(local):
                slots = xs_ref[i, at]
                gate_pre = dot_nt(slots, ge_ref[i, :FF])
                up_pre = dot_nt(slots, ge_ref[i, FF : 2 * FF])
                grad_act = dot_nt(dye_ref[i, at], ge_ref[i, 2 * FF :])
                sigmoid = 1.0 / (1.0 + jnp.exp(-gate_pre))
                silu = gate_pre * sigmoid
                act = (silu * up_pre).astype(BF)
                hx_ref[i, at] = act
                grad_gate = (grad_act * up_pre * (sigmoid * (1.0 + gate_pre * (1.0 - sigmoid)))).astype(BF)
                grad_up = (grad_act * silu).astype(BF)
                dgu_ref[i, at, :FF] = grad_gate
                dgu_ref[i, at, FF:] = grad_up
                backs.append((dot(grad_gate, ge_ref[i, :FF]) + dot(grad_up, ge_ref[i, FF : 2 * FF])).astype(BF))
                made = dot(act, ge_ref[i, 2 * FF :]).astype(BF)
                mades.append(made)
                for core in range(2):
                    part = slice(core * CAP, (core + 1) * CAP)
                    grads = dms[core][i * CAP : (i + 1) * CAP].astype(F32) * residual_scale
                    value = jnp.sum(grads * made[part].astype(F32), axis=1, keepdims=True)
                    values.append(jnp.sum(picks[core][i] * value, axis=0, keepdims=True))
            for core in range(2):
                pick = jnp.concatenate([one.astype(BF) for one in picks[core]], axis=0)
                part = slice(core * CAP, (core + 1) * CAP)
                sent = jnp.concatenate([backs[i][part] for i in range(local)], axis=0)
                dxp_ref[slot, core] = dot_tn(pick, sent).astype(BF)
                for i in range(local):
                    dgt_ref[t, core, i : i + 1] = values[2 * i + core]
            core_copy(zc, slot, t).start()
            for core in range(2):

                @pl.when((t > 0) | (c != core))
                def _():
                    dgt_copy(zc, core, t).start()

            @pl.when(early(t))
            def _():
                k_next = t // 2 + 1
                relay(k_next, z >= k_next, z + k_next < chips)

            for core in range(2):
                pick = jnp.concatenate([one.astype(BF) for one in picks[core]], axis=0)
                part = slice(core * CAP, (core + 1) * CAP)
                sent = jnp.concatenate([(gates[core][i] * mades[i][part].astype(F32)).astype(BF) for i in range(local)], axis=0)
                mixed = dot_tn(pick, sent).astype(BF)

                @pl.when(c == core)
                def _():
                    y_ref[zc] = mixed

                @pl.when(c != core)
                def _():
                    yps_ref[slot] = mixed

            y_copy(zc, slot, t).start()
            core_copy(zc, slot, t).wait_recv()
            there = core_ref.at[zc] if roomy else landed(core_ref.at[zc], "core")
            own = dxp_ref.at[slot, c]

            @pl.when(k == 0)
            def _():
                dx_ref[...] = own[...].astype(F32) + there[...].astype(F32)

            @pl.when(k == 1)
            def _():
                side = side_of(zc)
                add_rows(pair_ref.at[side], own, there, tokens, 64)

                @pl.when((z == 0) | (z == chips - 1))
                def _():
                    pair_copy(side).start()

            @pl.when(k >= 2)
            def _():
                add_rows(own, own, there, tokens, 64)

                @pl.when(k == 2)
                def _():
                    via_copy(zc, slot, t).start()

                @pl.when(k > 2)
                def _():
                    far_copy(zc, slot, t).start()

            return carry

        lax.fori_loop(0, chips, chunk, 0)

        @pl.when((z > 0) & (z < chips - 1))
        def _():
            for side in range(2):
                make(via_ref.at[side], via_ref.at[side], far_send.at[0], via_recv.at[side], mate).wait_recv()
                add_rows(pair_ref.at[side], pair_ref.at[side], via_ref.at[side], tokens, 64)
                pair_copy(side).start()

        for i in range(local):
            ge_ref[i, :FF] = dot_tn(dgu_ref[i, :, :FF], xs_ref[i]).astype(BF)
            ge_ref[i, FF : 2 * FF] = dot_tn(dgu_ref[i, :, FF:], xs_ref[i]).astype(BF)
            ge_ref[i, 2 * FF :] = dot_tn(hx_ref[i], dye_ref[i]).astype(BF)
            if bits:
                next(sums[i])
        add_ye(place(chips - 1))
        for t in range(max(chips - 2, 0), chips):
            free_slot(t, t % 2)
        for t in range(chips):
            for core in range(2):

                @pl.when((t > 0) | (c != core))
                def _():
                    dgt_copy(z, core, t).wait_send()

    slots = chips * 2 * CAP
    pl.run_scoped(
        experts_and_sums,
        pltpu.VMEM((2, tokens, D), BF), pltpu.VMEM((local, slots, D), BF), pltpu.VMEM((local, slots, D), BF),
        pltpu.VMEM((local, slots, 2 * FF), BF), pltpu.VMEM((local, slots, FF), BF), pltpu.VMEM((2, 2, tokens, D), BF),
        pltpu.VMEM((2, tokens, D), BF), pltpu.VMEM((tokens, D), BF),
    )

    def line(own, size, step, core_add, name, reach, via, arrive, send_sem, via_recv, from_recv):
        def direct(k):
            return make(own(k), arrive.at[z], send_sem.at[k], from_recv.at[z], (r, k * 2 + c))

        def passing(k, side):
            return make(own(k), via.at[side], send_sem.at[k], via_recv.at[side], (r, (z + 2 * side - 1) * 2 + c))

        def within(k):
            return (k >= 0) & (k < chips)

        for d in range(chips - 1, 0, -1):
            for side in range(2):
                way = 1 if side else -1
                owner = z + d * way

                @pl.when(within(owner))
                def _():
                    core_add(owner)
                    if d > reach + 1:
                        direct(owner).start()
                    elif d == reach + 1:
                        passing(owner, side).start()
                    elif d == reach:
                        pl.when(jnp.logical_not(within(z - way)))(lambda: direct(owner).start())

        core_add(z)
        yield
        for side in range(2):
            way = 1 if side else -1
            owner = z + reach * way

            @pl.when(within(owner) & within(z - way))
            def _():
                make(via.at[side], via.at[side], send_sem.at[0], via_recv.at[side], mate).wait_recv()
                add_rows(own(owner), own(owner), landed(via.at[side], name), size, step)
                direct(owner).start()

        yield
        for k in range(chips):

            @pl.when((z != k) & (far(k) != reach + 1))
            def _():
                make(arrive.at[k], arrive.at[k], send_sem.at[0], from_recv.at[k], mate).wait_recv()
                add_rows(own(z), own(z), landed(arrive.at[k], name), size, step)

        for k in range(chips):

            @pl.when(z != k)
            def _():
                direct(k).wait_send()

    def mixture():
        yield from line(lambda k: y_ref.at[k], tokens, 64, lambda k: None, "tokens", 1, y_via, y_from, *y_sems)
        out_ref[...] = (h1_ref[...] + residual_scale * y_ref[z].astype(F32)).astype(BF)

    def attention(q_ref, kd_ref, vd_ref, o_ref, p_ref, do_ref, dqkv_ref, gkv_ref, gq_ref, go_ref, halves_stage, tokens_stage, kv_stage, o_stage):
        loads = [
            pltpu.make_async_copy(heads_hbm.at[i], ref, heads_sem.at[i]) for i, ref in enumerate((q_ref, kd_ref, vd_ref, o_ref))
        ]
        start(loads)
        stages["halves"] = (halves_stage, stage_sem.at[1])
        stages["tokens"] = (tokens_stage, stage_sem.at[2])
        stages["kv"] = (kv_stage, stage_sem.at[3])
        stages["o"] = (o_stage, stage_sem.at[4])
        def projection(index, name, grad_ref, core, via, arrive, sems):
            core_sem, *sems = sems
            parts, results, wide = parts_ref.at[index], results_ref.at[index], D // replicas
            crossing = make(grad_ref.at[:, 1 - c], core, core_sem.at[0], core_sem.at[1], mate)
            crossing.start()
            yield
            crossing.wait_recv()

            def own(k):
                return grad_ref.at[k, c]

            yield from line(
                own, rows, 16, lambda k: add_rows(own(k), own(k), core.at[k], rows, 16), name, 1, via, arrive, *sems
            )
            crossing.wait_send()
            mine = grad_ref.at[z, c]

            def columns(part):
                return pl.ds(pl.multiple_of(part * wide, LANE), wide)

            def part_copy(d):
                to = (r + d) % replicas
                return make(
                    mine.at[:, columns(to)], parts.at[r], part_send.at[index, d], part_recv.at[index, r], (to, f)
                )

            def small_copy(d):
                to = (r + d) % replicas
                return make(mine.at[:, pl.ds(D, LANE)], smalls_ref.at[r], small_send.at[d], small_recv.at[r], (to, f))

            for d in range(1, replicas):
                part_copy(d).start()
                if index == 0:
                    small_copy(d).start()
            parts[r] = mine[:, columns(r)]
            if index == 0:
                smalls_ref[r] = mine[:, pl.ds(D, LANE)]
            yield
            for d in range(1, replicas):
                peer = (r + d) % replicas
                make(
                    parts.at[peer], parts.at[peer], part_send.at[index, d], part_recv.at[index, peer], (peer, f)
                ).wait_recv()
                if index == 0:
                    make(
                        smalls_ref.at[peer], smalls_ref.at[peer], small_send.at[d], small_recv.at[peer], (peer, f)
                    ).wait_recv()
            total = parts[0].astype(F32)
            for k in range(1, replicas):
                total = total + parts[k].astype(F32)
            results[r] = total.astype(BF)

            def result_copy(d):
                to = (r + d) % replicas
                return make(
                    results.at[r], results.at[r], result_send.at[index, d], result_recv.at[index, r], (to, f)
                )

            for d in range(1, replicas):
                result_copy(d).start()
            if index == 0:
                small = smalls_ref[0].astype(F32)
                for k in range(1, replicas):
                    small = small + smalls_ref[k].astype(F32)
                total_ref[...] = small
            yield
            for d in range(1, replicas):
                peer = (r + d) % replicas
                make(
                    results.at[peer], results.at[peer], result_send.at[index, d], result_recv.at[index, peer], (peer, f)
                ).wait_recv()
            for d in range(1, replicas):
                part_copy(d).wait_send()
                if index == 0:
                    small_copy(d).wait_send()
                result_copy(d).wait_send()

        moe = [mixture()]
        kvs = [projection(0, "kv", gkv_ref, kv_core, kv_via, kv_from, kv_sems)]
        outs = [projection(1, "o", go_ref, o_core, o_via, o_from, o_sems)]
        qs = [projection(2, "o", gq_ref, q_core, q_via, q_from, q_sems)]

        def go(*turns):
            for turn in turns:
                for process in turn:
                    next(process, None)

        def dgate():
            found = [dgt_all[k, :local] for k in range(2 * chips)]
            return jnp.concatenate(found + [jnp.zeros((LANE - E, tokens), F32)], axis=0).T

        for k in range(chips):

            @pl.when((z == k + 1) | (z + 1 == k) | (z > k + 2) | (z + 2 < k))
            def _():
                make(from_ref.at[k], from_ref.at[k], far_send.at[0], far_recv.at[k], mate).wait_recv()
                there = from_ref.at[k] if roomy else landed(from_ref.at[k], "tokens")
                add_rows(dx_ref, dx_ref, there, tokens, 64)

        for k in range(2 * chips):

            @pl.when(f == k)
            def _():
                for core in range(2):

                    @pl.when(c == core)
                    def _():
                        dgt_all[k] = dgt_ref[0, core]

            @pl.when(f != k)
            def _():
                make(dgt_all.at[k], dgt_all.at[k], dgt_send.at[0, 0], dgt_recv.at[k], mate).wait_recv()

        for load in loads:
            load.wait()
        backward = attention_backward(
            x_ref, dout_ref, cos_ref, sin_ref, columns, q_ref, kd_ref, vd_ref, p_hbm, o_ref, h1_ref, n2_all.at[z, c], gd_ref,
            dx_ref, dgate, gin_ref, gq_ref, gkv_ref, go_ref, do_ref, dqkv_ref, p_ref, p_sem,
        )
        next(backward)
        go(outs)
        next(backward)
        go(first, outs)
        next(backward)
        go(qs)
        next(backward, None)
        go(kvs, qs, kvs, last, first, moe, outs, last, first, qs, last, outs, kvs, moe, outs, qs, first, qs, outs, kvs, moe, last)
        go(kvs, qs, kvs)
        go(*[moe + outs + qs + kvs + sums] * (2 * bits + 8))

    size = ge_ref.shape[1] // max(bits, 1)
    pl.run_scoped(
        attention, *[pltpu.VMEM((tokens, D), BF)] * 4,
        pltpu.VMEM((2, 2 * tokens, tokens), F32), pltpu.VMEM((tokens, D), BF),
        pltpu.VMEM((tokens, QKV), BF), pltpu.VMEM((chips, 2, rows, D + LANE), BF), pltpu.VMEM((chips, 2, rows, D), BF),
        pltpu.VMEM((chips, 2, rows, D), BF), pltpu.VMEM((size // 2, D), BF), pltpu.VMEM((tokens, D), BF),
        pltpu.VMEM((rows, D + LANE), BF), pltpu.VMEM((rows, D), BF),
    )

    for e in range(local):
        copy = pltpu.make_async_copy(ge_ref.at[e], ge_hbm.at[e], ge_sem.at[e])
        if not bits:
            copy.start()
        copy.wait()
    for side in range(2):

        @pl.when(z > 0 if side == 0 else z < chips - 1)
        def _():
            pair_copy(side).wait_send()

    for k in range(chips):

        @pl.when((z >= k) & (z < chips - 1))
        def _():
            for copy in pass_on(k, "up"):
                copy.wait_send()

        @pl.when((z <= k) & (z > 0))
        def _():
            for copy in pass_on(k, "down"):
                copy.wait_send()

        for copy in pass_on(k, "mate"):
            copy.wait_send()

    for k in range(chips):
        for late in range(2):
            to_mate(k, c, late).wait_send()
        dout_copy(k, c, 2).wait_send()

        @pl.when((z >= k) & (z < chips - 1))
        def _():
            dout_copy(k, c, 0).wait_send()
            for kind in range(3):
                along(k, kind, True).wait_send()

        @pl.when((z <= k) & (z > 0))
        def _():
            dout_copy(k, c, 1).wait_send()
            for kind in range(3):
                along(k, kind, False).wait_send()

        @pl.when(z != k)
        def _():
            for d in range(1, replicas):
                for kind in (0, 2):
                    across(k, kind, d).wait_send()


def finish(gexp_ref, results_ref, total_ref, gin_ref, out_ref, *outs):
    layer_out, grad_in, gains_one, query, key, value, output, gains_two, router, expert = outs
    expert[...] = gexp_ref[...].astype(F32)
    layer_out[...] = out_ref[...]
    grad_in[...] = gin_ref[...]
    for index, targets in ((0, (key, value)), (1, (output,)), (2, (query,))):
        start, wide = 0, results_ref.shape[3]
        for ref in targets:
            for at in range(0, ref.shape[1], LANE):
                part, column = divmod(start + at, wide)
                ref[:, at : at + LANE] = results_ref[index, part, :, column : column + LANE].astype(F32)
            start += ref.shape[1]

    @pl.when(pl.program_id(0) == 0)
    def _():
        small = total_ref[...].T
        router[...] = small[:E]
        gains_one[...] = small[E : E + 1]
        gains_two[...] = small[E + 1 : E + 2]


def call(kernel, out_shape, args, scratch=(), outside=0, out_outside=0, **params):
    spaces = [pltpu.SMEM if a.dtype == jnp.int32 and a.size <= 16 else pltpu.VMEM for a in args]
    spaces[len(args) - outside :] = [pl.ANY] * outside
    return pl.pallas_call(
        kernel,
        out_shape=out_shape,
        in_specs=[pl.BlockSpec(memory_space=space) for space in spaces],
        out_specs=[
            pl.BlockSpec(memory_space=pltpu.VMEM if i < len(out_shape) - out_outside else pl.ANY)
            for i in range(len(out_shape))
        ],
        scratch_shapes=list(scratch),
        compiler_params=pltpu.CompilerParams(
            vmem_limit_bytes=VMEM_LIMIT, has_side_effects="collective_id" in params, **params
        ),
    )(*args)


def shape(dims, dtype):
    return jax.ShapeDtypeStruct(dims, dtype)


def make_body(mesh):
    group, replicas = mesh.shape["fsdp"], mesh.shape["replica"]
    local = E // group

    def body(
        hidden_in, seq_lengths, routes, norm1_gain, w_query, w_key, w_value, w_output, norm2_gain, w_router,
        expert_weights, out_cotangent,
    ):
        tokens = hidden_in.shape[0]
        rows = w_query.shape[0]
        chips = group // 2
        dma = pltpu.SemaphoreType.DMA
        bits = replicas.bit_length() - 1
        size = 3 * FF // bits if bits else 0
        roomy = chips <= 4
        landing = [shape((local * bits, size >> (k + 1), D), BF) for k in range(bits)]
        blocks = [shape((chips, tokens, D), BF)] * 2
        landing += [shape((chips, tokens, D), BF)]
        if not roomy:
            landing += blocks
        outs = call(
            functools.partial(layer, replicas, chips),
            [
                shape((tokens, D), F32), shape((tokens, D), BF), shape((3, replicas, rows, D // replicas), BF),
                shape((rows, LANE), F32), shape((local, 3 * FF, D), BF),
                shape((KVH, 2 * tokens, tokens), F32), shape((4, tokens, D), BF), shape((chips, 2, tokens, D), BF),
                shape((2, tokens, D), BF), shape((chips, tokens, D), BF), shape((2, rows, D + LANE), BF),
                shape((chips, rows, D + LANE), BF), shape((2, rows, D), BF), shape((chips, rows, D), BF),
                shape((2, rows, D), BF), shape((chips, rows, D), BF),
            ]
            + landing,
            (
                hidden_in, seq_lengths, routes.T, rope_table(tokens), w_query, w_key, w_value, w_output, w_router.T,
                norm1_gain[None], norm2_gain[None], out_cotangent, expert_weights,
            ),
            [
                pltpu.VMEM((chips, 2, rows, W_O + D), BF), pltpu.VMEM((tokens, D), F32),
                pltpu.VMEM((tokens, LANE), F32), pltpu.VMEM((tokens, LANE), F32), pltpu.VMEM((tokens, LANE), F32),
                dma((4,)), dma((1,)), dma((3, chips)), dma((3, chips)), dma((3, chips)), dma((3, chips, replicas)),
                dma((3, chips, replicas)), dma((2, chips)), dma((2, chips)), dma((3, chips)), dma((chips, 2)),
                pltpu.VMEM((local, 3 * FF, D), BF), pltpu.VMEM((chips, 2, tokens, D), BF),
                pltpu.VMEM((chips, 2, E, tokens), F32), pltpu.VMEM((2, tokens, D), BF), pltpu.VMEM((2, tokens, D), BF),
                pltpu.VMEM((chips, 2, 8, tokens), F32), pltpu.VMEM((group, 8, tokens), F32),
                pltpu.VMEM((chips, tokens, D), BF), pltpu.VMEM((chips, rows, D + LANE), BF), pltpu.VMEM((chips, rows, D), BF),
                pltpu.VMEM((chips, rows, D), BF), pltpu.VMEM((3, replicas, rows, D // replicas), BF),
                pltpu.VMEM((replicas, rows, LANE), BF),
            ]
            + ([pltpu.VMEM(b.shape, b.dtype) for b in blocks] if roomy else [])
            + ([dma((chips,))] * 3 + [dma((chips, 2))]) * 2 + [dma((chips,))] * 4 + [dma((2,))] * 2
            + [dma((chips, 2)), dma((group,)), dma((chips,)), dma((chips,))]
            + [dma((1,)), dma((1,)), dma((5,)), dma((local,)), dma((2,))]
            + [dma((max(local * bits, 1), max(2 * bits, 1)))] * 2
            + [pltpu.SemaphoreType.REGULAR((max(local * bits, 1), max(bits, 1)))]
            + [dma((chips,)), dma((2,)), dma((chips,))] + [dma((2,)), dma((chips,)), dma((2,)), dma((chips,))] * 3
            + [dma((3, replicas))] * 2 + [dma((replicas,))] * 2 + [dma((3, replicas))] * 2,
            outside=1,
            out_outside=12 + len(landing),
            collective_id=0,
        )
        grad_in, layer_out, results, total, grad_experts = outs[:5]
        steps = 8

        def moving(a, dim=0):
            block = tuple(n // steps if i == dim else n for i, n in enumerate(a.shape))
            return pl.BlockSpec(block, lambda i: tuple(i if at == dim else 0 for at in range(len(block))))

        def still(a):
            return pl.BlockSpec(a.shape, lambda i: (0,) * len(a.shape))

        grad_experts = grad_experts.reshape(local * 3 * FF, D)
        gain, router = shape((1, rows), F32), shape((E, rows), F32)
        wide, narrow = shape((rows, D), F32), shape((rows, KVH * HD), F32)
        out_shapes = [
            shape((tokens, D), BF), shape((tokens, D), F32), gain, wide, narrow, narrow, wide, gain, router,
            shape((local * 3 * FF, D), F32),
        ]
        outs = pl.pallas_call(
            finish,
            grid=(steps,),
            in_specs=[moving(grad_experts), moving(results, 2), still(total), moving(grad_in), moving(layer_out)],
            out_specs=[still(a) if a in (gain, router) else moving(a) for a in out_shapes],
            out_shape=out_shapes,
            compiler_params=pltpu.CompilerParams(vmem_limit_bytes=VMEM_LIMIT),
        )(grad_experts, results, total, grad_in, layer_out)
        return (
            outs[0], outs[1], outs[2][0], outs[3], outs[4], outs[5], outs[6], outs[7][0], outs[8].T,
            outs[9].reshape(local, 3 * FF, D),
        )

    return body


def solution(mesh):
    tokens, weights = P(("replica", "fsdp"), None), P("fsdp", None)
    return jax.shard_map(
        make_body(mesh),
        mesh=mesh,
        in_specs=(
            tokens, tokens, tokens, P("fsdp"), weights, weights, weights, weights, P("fsdp"), weights,
            P("fsdp", None, None), tokens,
        ),
        out_specs=(
            tokens, tokens, P("fsdp"), weights, weights, weights, weights, P("fsdp"), weights, P("fsdp", None, None),
        ),
        check_vma=False,
    )
```

time: 280 us -> 270 us (0.964)
  the two profiles are of different devices: /device:TPU:10 before, /device:TPU:16 now
where the time goes in v8:
time: 270 us; the launch traced here: 268 us
  Pallas kernels  267 us (99%)
    pallas_call x1, Pallas kernels, call(): pl.pallas_call(kernel, out_shape=out_shape, in_specs=[pl.BlockSpec(memory...  257 us
    pallas_call x1, Pallas kernels, body(): pl.pallas_call(finish, grid=(steps,), in_specs=[moving(grad_experts), mov...  9.93 us

profile of v8, /device:TPU:16, one launch (start us, length us, event | category | flops | bytes accessed | tf_op | source)
XLA Modules:
  0.0 267.9 jit_solution(12641227057042683613)
XLA Ops:
  0.6 257.2 %shard_map.204 = (f32[256,1024]{1,0:T(8,128)}, bf16[256,1024]{1,0:T(8,128)(2,1)}, bf16[3,4,128,256]{3,2,1,0:T(8,128)(2,1)}, f32[128,128]{1,0:T(8,128)}, bf16[2,1...) custom-call(bf16[256,1024]{1,0:T(8,128)(2,1)} %x_ref.1, ...), custom_call_target="tpu_custom_call" | custom-call | tf_op jit(solution)/shard_map/pallas_call | solution.py:1067
  257.8 9.9 %shard_map.205 = (bf16[256,1024]{1,0:T(8,128)(2,1)}, f32[256,1024]{1,0:T(8,128)}, f32[1,128]{1,0:T(1,128)}, f32[128,1024]{1,0:T(8,128)}, f32[128,512]{1,0:T(8,12...) custom-call(bf16[3072,1024]{1,0:T(8,128)(2,1)} %bitcast.9, ...), custom_call_target="tpu_custom_call" | custom-call | tf_op jit(solution)/shard_map/pallas_call | solution.py:1162

commit v9 on v8

--- a/solution.py
+++ b/solution.py
@@ -151,6 +151,8 @@
         key_back.append(block + pltpu.roll(block, HD, 1))
         block = dot_tn(weights.astype(BF), outs)
         value_back.append(block + pltpu.roll(block, HD, 1))
+        if g == KVH // 2 - 1:
+            yield
     for m in range(KVH // 2):
         block = jnp.where(low, key_back[2 * m], key_back[2 * m + 1])
         at = slice(H * HD + m * LANE, H * HD + (m + 1) * LANE)
@@ -667,7 +669,7 @@
                     xs_ref[i, at] = taken[part]
                     dye_ref[i, at] = (gates[core][i] * grads[part]).astype(BF)
             at = pl.ds(at_chip, pair)
-            mades, backs, values = [], [], []
+            mades, backs = [], []
             for i in range(local):
                 slots = xs_ref[i, at]
                 gate_pre = dot_nt(slots, ge_ref[i, :FF])
@@ -682,21 +684,20 @@
                 dgu_ref[i, at, :FF] = grad_gate
                 dgu_ref[i, at, FF:] = grad_up
                 backs.append((dot(grad_gate, ge_ref[i, :FF]) + dot(grad_up, ge_ref[i, FF : 2 * FF])).astype(BF))
-                made = dot(act, ge_ref[i, 2 * FF :]).astype(BF)
+            for core in range(2):
+                pick = jnp.concatenate([one.astype(BF) for one in picks[core]], axis=0)
+                part = slice(core * CAP, (core + 1) * CAP)
+                sent = jnp.concatenate([backs[i][part] for i in range(local)], axis=0)
+                dxp_ref[slot, core] = dot_tn(pick, sent).astype(BF)
+            core_copy(zc, slot, t).start()
+            for i in range(local):
+                made = dot(hx_ref[i, at], ge_ref[i, 2 * FF :]).astype(BF)
                 mades.append(made)
                 for core in range(2):
                     part = slice(core * CAP, (core + 1) * CAP)
                     grads = dms[core][i * CAP : (i + 1) * CAP].astype(F32) * residual_scale
                     value = jnp.sum(grads * made[part].astype(F32), axis=1, keepdims=True)
-                    values.append(jnp.sum(picks[core][i] * value, axis=0, keepdims=True))
-            for core in range(2):
-                pick = jnp.concatenate([one.astype(BF) for one in picks[core]], axis=0)
-                part = slice(core * CAP, (core + 1) * CAP)
-                sent = jnp.concatenate([backs[i][part] for i in range(local)], axis=0)
-                dxp_ref[slot, core] = dot_tn(pick, sent).astype(BF)
-                for i in range(local):
-                    dgt_ref[t, core, i : i + 1] = values[2 * i + core]
-            core_copy(zc, slot, t).start()
+                    dgt_ref[t, core, i : i + 1] = jnp.sum(picks[core][i] * value, axis=0, keepdims=True)
             for core in range(2):
 
                 @pl.when((t > 0) | (c != core))
@@ -755,13 +756,6 @@
             return carry
 
         lax.fori_loop(0, chips, chunk, 0)
-
-        @pl.when((z > 0) & (z < chips - 1))
-        def _():
-            for side in range(2):
-                make(via_ref.at[side], via_ref.at[side], far_send.at[0], via_recv.at[side], mate).wait_recv()
-                add_rows(pair_ref.at[side], pair_ref.at[side], via_ref.at[side], tokens, 64)
-                pair_copy(side).start()
 
         for i in range(local):
             ge_ref[i, :FF] = dot_tn(dgu_ref[i, :, :FF], xs_ref[i]).astype(BF)
@@ -769,6 +763,16 @@
             ge_ref[i, 2 * FF :] = dot_tn(hx_ref[i], dye_ref[i]).astype(BF)
             if bits:
                 next(sums[i])
+            if i > 0:
+                continue
+
+            @pl.when((z > 0) & (z < chips - 1))
+            def _():
+                for side in range(2):
+                    make(via_ref.at[side], via_ref.at[side], far_send.at[0], via_recv.at[side], mate).wait_recv()
+                    add_rows(pair_ref.at[side], pair_ref.at[side], via_ref.at[side], tokens, 64)
+                    pair_copy(side).start()
+
         add_ye(place(chips - 1))
         for t in range(max(chips - 2, 0), chips):
             free_slot(t, t % 2)
@@ -973,12 +977,14 @@
         next(backward)
         go(outs)
         next(backward)
-        go(first, outs)
+        go(first)
+        next(backward)
+        go(outs)
         next(backward)
         go(qs)
         next(backward, None)
-        go(kvs, qs, kvs, last, first, moe, outs, last, first, qs, last, outs, kvs, moe, outs, qs, first, qs, outs, kvs, moe, last)
-        go(kvs, qs, kvs)
+        go(kvs, last, qs, first, kvs, last, outs, first, moe, last, qs, outs, kvs, outs, first, qs, outs, moe, qs, kvs, moe, last)
+        go(qs, kvs, kvs)
         go(*[moe + outs + qs + kvs + sums] * (2 * bits + 8))
 
     size = ge_ref.shape[1] // max(bits, 1)
@@ -1143,7 +1149,7 @@
             collective_id=0,
         )
         grad_in, layer_out, results, total, grad_experts = outs[:5]
-        steps = 8
+        steps = 4
 
         def moving(a, dim=0):
             block = tuple(n // steps if i == dim else n for i, n in enumerate(a.shape))

time: 270 us -> 261 us (0.967)
  the two profiles are of different devices: /device:TPU:16 before, /device:TPU:10 now
where the time goes in v9:
time: 261 us; the launch traced here: 260 us
  Pallas kernels  259 us (99%)
    pallas_call x1, Pallas kernels, call(): pl.pallas_call(kernel, out_shape=out_shape, in_specs=[pl.BlockSpec(memory...  249 us
    pallas_call x1, Pallas kernels, body(): pl.pallas_call(finish, grid=(steps,), in_specs=[moving(grad_experts), mov...  9.49 us

profile of v9, /device:TPU:10, one launch (start us, length us, event | category | flops | bytes accessed | tf_op | source)
XLA Modules:
  0.0 259.7 jit_solution(1176575798902102814)
XLA Ops:
  0.6 249.4 %shard_map.204 = (f32[256,1024]{1,0:T(8,128)}, bf16[256,1024]{1,0:T(8,128)(2,1)}, bf16[3,4,128,256]{3,2,1,0:T(8,128)(2,1)}, f32[128,128]{1,0:T(8,128)}, bf16[2,1...) custom-call(bf16[256,1024]{1,0:T(8,128)(2,1)} %x_ref.1, ...), custom_call_target="tpu_custom_call" | custom-call | tf_op jit(solution)/shard_map/pallas_call | solution.py:1073
  250.0 9.5 %shard_map.205 = (bf16[256,1024]{1,0:T(8,128)(2,1)}, f32[256,1024]{1,0:T(8,128)}, f32[1,128]{1,0:T(1,128)}, f32[128,1024]{1,0:T(8,128)}, f32[128,512]{1,0:T(8,12...) custom-call(bf16[3072,1024]{1,0:T(8,128)(2,1)} %bitcast.9, ...), custom_call_target="tpu_custom_call" | custom-call | tf_op jit(solution)/shard_map/pallas_call | solution.py:1168

commit v10 on v9

--- a/solution.py
+++ b/solution.py
@@ -337,7 +337,7 @@
                             across(zb, kind, d).start()
 
                 both_sides(k, arrive)
-            if k == 1:
+            if k == min(2, chips - 1):
                 both_sides(1, lambda zb, low: dout_copy(z, c, 1 if low else 0).start())
                 dout_copy(z, c, 2).start()
 

time: 261 us -> 259 us (level)
  Pallas kernels: 259 us -> 256 us
where the time goes in v10:
time: 259 us; the launch traced here: 257 us
  Pallas kernels  256 us (99%)
    pallas_call x1, Pallas kernels, call(): pl.pallas_call(kernel, out_shape=out_shape, in_specs=[pl.BlockSpec(memory...  247 us
    pallas_call x1, Pallas kernels, body(): pl.pallas_call(finish, grid=(steps,), in_specs=[moving(grad_experts), mov...  9.49 us

profile of v10, /device:TPU:10, one launch (start us, length us, event | category | flops | bytes accessed | tf_op | source)
XLA Modules:
  0.0 257.3 jit_solution(6922940800009589330)
XLA Ops:
  0.6 247.0 %shard_map.204 = (f32[256,1024]{1,0:T(8,128)}, bf16[256,1024]{1,0:T(8,128)(2,1)}, bf16[3,4,128,256]{3,2,1,0:T(8,128)(2,1)}, f32[128,128]{1,0:T(8,128)}, bf16[2,1...) custom-call(bf16[256,1024]{1,0:T(8,128)(2,1)} %x_ref.1, ...), custom_call_target="tpu_custom_call" | custom-call | tf_op jit(solution)/shard_map/pallas_call | solution.py:1073
  247.7 9.5 %shard_map.205 = (bf16[256,1024]{1,0:T(8,128)(2,1)}, f32[256,1024]{1,0:T(8,128)}, f32[1,128]{1,0:T(1,128)}, f32[128,1024]{1,0:T(8,128)}, f32[128,512]{1,0:T(8,12...) custom-call(bf16[3072,1024]{1,0:T(8,128)(2,1)} %bitcast.9, ...), custom_call_target="tpu_custom_call" | custom-call | tf_op jit(solution)/shard_map/pallas_call | solution.py:1168

commit v11 on v10

--- a/solution.py
+++ b/solution.py
@@ -79,18 +79,11 @@
         )
 
 
-def meet(devices, expected):
-    barrier = pltpu.get_barrier_semaphore()
-    for condition, device in devices:
-
-        def signal(device=device):
-            pl.semaphore_signal(barrier, inc=1, device_id=device, device_id_type=pl.DeviceIdType.MESH)
-
-        if condition is True:
-            signal()
-        else:
-            pl.when(condition)(signal)
-    pl.semaphore_wait(barrier, expected)
+def greet(devices):
+    for device in devices:
+        pl.semaphore_signal(
+            pltpu.get_barrier_semaphore(), inc=1, device_id=device, device_id_type=pl.DeviceIdType.MESH
+        )
 
 
 def attention_backward(
@@ -219,6 +212,11 @@
     mate, above, below = (r, z * 2 + 1 - c), (r, f + 2), (r, f - 2)
     make = Copies().make
 
+    peers = [mate]
+    for k in range(1, chips):
+        to = (z + k) % chips
+        peers += [(r, to * 2 + c), (r, to * 2 + 1 - c)]
+    greet(peers + [((r + d) % replicas, f) for d in range(1, replicas)])
     load_experts = pltpu.make_async_copy(we_hbm, ge_ref, we_sem.at[0])
     load_experts.start()
     own_dout = pltpu.make_async_copy(dout_ref, do_all.at[z, c], own_sem.at[0])
@@ -231,12 +229,7 @@
     own[:, H * HD + KVH * HD : QKV] = wv_ref[...]
     own[:, QKV:W_O] = packed.T.astype(BF)
     own[:, W_O:] = wo_ref[...]
-    peers = [(True, mate)]
-    for k in range(1, chips):
-        to = (z + k) % chips
-        peers += [(True, (r, to * 2 + c)), (True, (r, to * 2 + 1 - c))]
-    peers += [(True, ((r + d) % replicas, f)) for d in range(1, replicas)]
-    meet(peers, len(peers))
+    pl.semaphore_wait(pltpu.get_barrier_semaphore(), len(peers) + replicas - 1)
 
     def part(kind):
         if kind == 0:

time: 259 us -> 259 us (level)
  no operation moved by 1% of the time
where the time goes in v11:
time: 259 us; the launch traced here: 257 us
  Pallas kernels  256 us (99%)
    pallas_call x1, Pallas kernels, call(): pl.pallas_call(kernel, out_shape=out_shape, in_specs=[pl.BlockSpec(memory...  247 us
    pallas_call x1, Pallas kernels, body(): pl.pallas_call(finish, grid=(steps,), in_specs=[moving(grad_experts), mov...  9.49 us

profile of v11, /device:TPU:10, one launch (start us, length us, event | category | flops | bytes accessed | tf_op | source)
XLA Modules:
  0.0 257.3 jit_solution(17126756078137112151)
XLA Ops:
  0.6 246.9 %shard_map.204 = (f32[256,1024]{1,0:T(8,128)}, bf16[256,1024]{1,0:T(8,128)(2,1)}, bf16[3,4,128,256]{3,2,1,0:T(8,128)(2,1)}, f32[128,128]{1,0:T(8,128)}, bf16[2,1...) custom-call(bf16[256,1024]{1,0:T(8,128)(2,1)} %x_ref.1, ...), custom_call_target="tpu_custom_call" | custom-call | tf_op jit(solution)/shard_map/pallas_call | solution.py:1066
  247.6 9.5 %shard_map.205 = (bf16[256,1024]{1,0:T(8,128)(2,1)}, f32[256,1024]{1,0:T(8,128)}, f32[1,128]{1,0:T(1,128)}, f32[128,1024]{1,0:T(8,128)}, f32[128,512]{1,0:T(8,12...) custom-call(bf16[3072,1024]{1,0:T(8,128)(2,1)} %bitcast.9, ...), custom_call_target="tpu_custom_call" | custom-call | tf_op jit(solution)/shard_map/pallas_call | solution.py:1161
